TPU v7x, 256 devices: a whole 4x4x8 slice. The times are simulated.
256 devices in a mesh: tm: 16 (over z, core), lon: 8 (over y, x_lo), ens: 2 (over x_hi).
Axes of the slice: x: 4 (x_hi: 2, x_lo: 2; x = x_hi * 2 + x_lo), y: 4, z: 8, core: 2. Of those that a mesh axis runs over, the one named last changes fastest.
Arguments:
- anomalies: bfloat16 [8192, 1024], P('lon', 'ens'), may hold values from -6 to 6
- localization: bfloat16 [64, 3, 128, 128], P('lon'), may hold values from -0.3125 to 0.3125
- innovations: float32 [16, 4096], P('tm', 'lon'), may hold values from -6 to 6
- obs_cell: int32 [16, 4096], P('tm', 'lon'), may hold values from 0 to 1023
- tangent_blocks: float32 [16, 8, 128, 128], P('tm'), may hold values from -1 to 2
- tangent_order: int32 [16, 8], P('tm'), may hold values from 0 to 7, each once within a row
Outputs:
- forward_states: float32 [16, 1024, 1024], P('tm', ('ens', 'lon'))
- adjoint_states: float32 [16, 1024, 1024], P('tm', ('ens', 'lon'))
Inputs may be any that keep to these rules, and one draw needn't show every extreme that they name: Observation j of a step lies in sector j // 512, at that sector's cell obs_cell. `tangent_order`: each step's row names every block index once.
All inputs are finite; a program needn't handle non-finite values.
Results may differ from a plain program's by a relative error of at most 0.015.
Values may be sent and summed in bfloat16 or wider, within the bound.
No kernel may reach another device: no remote copies, remote signals or barrier semaphores. Data moves between devices by JAX's collectives and lax.ppermute only.
A program may use at most 64 MiB of HBM per device.

v0:
```python
import jax
import jax.numpy as jnp
from jax import lax
from jax.sharding import PartitionSpec as P

BLK = 128


precise_mode = lax.Precision.HIGHEST


def extended(cells, sides, width):
    for axis, dim in sides:
        count = lax.axis_size(axis)
        head = lax.slice_in_dim(cells, 0, width, axis=dim)
        tail = lax.slice_in_dim(cells, cells.shape[dim] - width, cells.shape[dim], axis=dim)
        cells = jnp.concatenate(
            [
                lax.ppermute(tail, axis, [(i, (i + 1) % count) for i in range(count)]),
                cells,
                lax.ppermute(head, axis, [((i + 1) % count, i) for i in range(count)]),
            ],
            axis=dim,
        )
    return cells


def entering(array, axis, join, neutral, backward):
    count = lax.axis_size(axis)
    place = lax.axis_index(axis)
    ahead = count - 1 - place if backward else place
    gathered = jax.tree.map(
        lambda a, kind: lax.all_gather(a.astype(kind), axis),
        array,
        jax.tree.map(lambda a: jnp.bfloat16 if a.dtype == jnp.float32 else a.dtype, array),
    )
    state = jax.tree.map(lambda a, e: jnp.zeros_like(a) + jnp.asarray(e, a.dtype), array, neutral)

    def one(turn, state):
        source = count - 1 - turn if backward else turn
        return join(
            state,
            jax.tree.map(
                lambda a, own: lax.dynamic_index_in_dim(a, source, 0, False).astype(own.dtype),
                gathered,
                array,
            ),
        )

    return lax.fori_loop(0, ahead, one, state)


def forward_apply(perm_matrix, blocks, state):
    row_count = state.shape[0]
    split_point = state.reshape(row_count, blocks.shape[0], blocks.shape[1])
    chosen = jnp.einsum("ik,mkc->mic", perm_matrix, split_point, precision=precise_mode)
    return jnp.einsum("mic,idc->mid", chosen, blocks, precision=precise_mode).reshape(row_count, -1)


def adjoint_apply(perm_matrix, blocks, state):
    row_count = state.shape[0]
    split_point = state.reshape(row_count, blocks.shape[0], blocks.shape[1])
    moved = jnp.einsum("mic,icd->mid", split_point, blocks, precision=precise_mode)
    placed = jnp.einsum("ij,mid->mjd", perm_matrix, moved, precision=precise_mode)
    return placed.reshape(row_count, -1)


def operator_product(left_perm, left_blocks, right_perm, right_blocks):
    perm_matrix = jnp.dot(left_perm, right_perm, precision=precise_mode)
    picked = jnp.einsum("ik,kce->ice", left_perm, right_blocks, precision=precise_mode)
    blocks = jnp.einsum("icd,ide->ice", left_blocks, picked, precision=precise_mode)
    return (perm_matrix, blocks)


def forward_combine(earlier, later):
    perm_matrix, blocks = operator_product(later[0], later[1], earlier[0], earlier[1])
    return (perm_matrix, blocks, forward_apply(later[0], later[1], earlier[2]) + later[2])


def adjoint_combine(earlier, later):
    perm_matrix, blocks = operator_product(earlier[0], earlier[1], later[0], later[1])
    return (perm_matrix, blocks, adjoint_apply(later[0], later[1], earlier[2]) + later[2])


def on_device(anomalies, localization, innovations, obs_cell, tangent_blocks, tangent_order):
    cells = anomalies.shape[0]
    half_cols = anomalies.shape[1]
    sector_count = lax.axis_size("lon")
    steps_here = tangent_blocks.shape[0]
    block_count = tangent_blocks.shape[1]
    block_size = tangent_blocks.shape[2]
    full_anomalies = lax.all_gather(anomalies, "ens", axis=1, tiled=True)
    positions = lax.broadcasted_iota(jnp.int32, (1, 1, cells), 2)
    obs_onehot = (obs_cell[:, :, None] == positions).astype(jnp.float32)
    cell_weight = jnp.einsum("to,toc->ct", innovations, obs_onehot, precision=precise_mode)
    weighted = (
        jnp.transpose(cell_weight)[:, :, None] * anomalies[None].astype(jnp.float32)
    ).astype(jnp.bfloat16)
    padded = extended(weighted, (("lon", 1),), BLK)
    cell_blocks = cells // BLK
    stacked = padded.reshape(steps_here, cell_blocks + 2, BLK, half_cols)
    localized = jnp.zeros((steps_here, cell_blocks, BLK, half_cols), jnp.float32)
    for offset in range(3):
        localized = localized + jnp.einsum(
            "bij,tbjm->tbim",
            localization[:, offset],
            stacked[:, offset : offset + cell_blocks],
            preferred_element_type=jnp.float32,
        )
    localized = localized.reshape(steps_here, cells, half_cols).astype(jnp.bfloat16)
    scale = float(cells * sector_count) ** (-0.5)
    forcing = lax.psum_scatter(
        (
            jnp.einsum("tcm,cr->mtr", localized, full_anomalies, preferred_element_type=jnp.float32)
            * scale
        ).astype(jnp.bfloat16),
        "lon",
        scatter_dimension=0,
        tiled=True,
    ).astype(jnp.float32)
    block_ids = lax.broadcasted_iota(jnp.int32, (1, 1, block_count), 2)
    perm_all = (tangent_order[:, :, None] == block_ids).astype(jnp.float32)
    forward_items = (perm_all[0], tangent_blocks[0], forcing[:, 0])
    adjoint_items = [
        (
            perm_all[0],
            tangent_blocks[0],
            adjoint_apply(perm_all[0], tangent_blocks[0], forcing[:, 0]),
        )
    ]
    adjoint_total = adjoint_items[steps_here - 1]
    empty = jnp.zeros((forcing.shape[0], forcing.shape[2]), jnp.float32)
    identity = (
        jnp.eye(block_count, dtype=jnp.float32),
        jnp.broadcast_to(
            jnp.eye(block_size, dtype=jnp.float32), (block_count, block_size, block_size)
        ),
        empty,
    )
    start_state = entering(forward_items, "tm", forward_combine, identity, False)[2]
    end_adjoint = entering(adjoint_total, "tm", adjoint_combine, identity, True)[2]
    state = start_state
    index = 0
    state = forward_apply(perm_all[index], tangent_blocks[index], state) + forcing[:, index]
    forward_list = [state]
    adjoint = end_adjoint
    adjoint_list = [empty] * steps_here
    index = 0
    adjoint = adjoint_apply(perm_all[index], tangent_blocks[index], adjoint + forcing[:, index])
    adjoint_list[index] = adjoint
    return (jnp.stack(forward_list, axis=0), jnp.stack(adjoint_list, axis=0))


def solution(mesh):
    placed = (
        P("lon", "ens"),
        P("lon", None, None, None),
        P("tm", "lon"),
        P("tm", "lon"),
        P("tm", None, None, None),
        P("tm", None),
    )
    return jax.shard_map(
        on_device,
        mesh=mesh,
        in_specs=placed,
        out_specs=(P("tm", ("ens", "lon"), None), P("tm", ("ens", "lon"), None)),
        check_vma=False,
    )
```

profile of v0, /device:TPU:225, one launch (start us, length us, event | category | flops | bytes accessed | tf_op | source)
XLA Modules:
  0.0 230.5 jit_solution(17604699884286328846)
XLA Ops:
  8.8 1.5 fusion.18
  10.6 1.3 collective-permute-start
  11.9 2.5 %collective-permute-start.1 = (bf16[1,128,512]{2,1,0:T(8,128)(2,1)S(1)}, bf16[1,128,512]{2,1,0:T(8,128)(2,1)S(1)}, u32[]{:S(2)}, u32[]{:S(2)}) collective-permute-start(bf16[1,128,512]{2,1,0:T(8,128)(2,1)S(1)} %get-tuple-element.186), channel_id=1, source_target_pairs={{2,0},{4,2},{6,4},{8,6},{10,8},{12,10},{14,12},{0,14},{3,1},{5,3},... | collective-permute-start | bytes 393224 | tf_op jit(solution)/shard_map/ppermute | solution.py:21
  14.5 2.9 %collective-permute-done = bf16[1,128,512]{2,1,0:T(8,128)(2,1)S(1)} collective-permute-done((bf16[1,128,512]{2,1,0:T(8,128)(2,1)S(1)}, bf16[1,128,512]{2,1,0:T(8,128)(2,1)S(1)}, u32[]{:S(2)}, u32[]{:S(2)}) %collective-permute-start) | collective-permute-done | bytes 131104 | tf_op jit(solution)/shard_map/ppermute | solution.py:19
  17.4 1.5 collective-permute-done.1
  20.3 30.3 %all-gather.7.cloned.1.call-done = bf16[1024,1024]{1,0:T(8,128)(2,1)} async-done(((bf16[1024,512]{1,0:T(8,128)(2,1)}), bf16[1024,1024]{1,0:T(8,128)(2,1)}) %all-gather.7.cloned.1.call-update) | async-done | bytes 2097168 | tf_op jit(solution)/shard_map/all_gather | solution.py:92
  50.6 3.9 %fusion.20 = bf16[512,1,1024]{2,0,1:T(8,128)(2,1)} fusion(bf16[1024,512]{1,0:T(8,128)(2,1)S(1)} %bitcast.191, bf16[1024,1024]{1,0:T(8,128)(2,1)} %all-gather.7.cloned.1.call-done), kind=kOutput, calls=%fused_computation.28 | convolution fusion | flops 1074790400 | bytes 4194304 | tf_op jit(solution)/shard_map/tcm,cr->mtr/dot_general | solution.py:114
  54.6 0.7 convert_element_type.123
  55.4 38.1 %reduce-scatter.2.cloned.1.call-done = bf16[64,1,1024]{2,0,1:T(8,128)(2,1)} async-done(((bf16[512,1,1024]{2,0,1:T(8,128)(2,1)}), bf16[64,1,1024]{2,0,1:T(8,128)(2,1)}) %reduce-scatter.2.cloned.1.call-update) | async-done | bytes 131088 | tf_op jit(solution)/shard_map/reduce_scatter | solution.py:112
  93.5 0.9 copy.44
  96.0 1.6 fusion.30
  97.7 20.6 %all_gather.11 = bf16[16,8,8]{2,1,0:T(8,128)(2,1)S(1)} all-gather(bf16[1,8,8]{2,1,0:T(8,128)(2,1)S(1)} %convert_convert_fusion), channel_id=1, replica_groups=mesh['tm'=16,'lon'=8,'ens'=2] {'tm'}, dimensions={0}, use_global_device_ids=true | all-gather | bytes 2176 | tf_op jit(solution)/shard_map/all_gather | solution.py:33
  118.3 19.8 %all-gather.11.cloned.1.call-done = bf16[16,64,1024]{2,1,0:T(8,128)(2,1)} async-done(((bf16[1,64,1024]{2,1,0:T(8,128)(2,1)}), bf16[16,64,1024]{2,1,0:T(8,128)(2,1)}) %all-gather.11.cloned.1.call-update) | async-done | bytes 2097168 | tf_op jit(solution)/shard_map/all_gather | solution.py:33
  138.2 0.9 copy-done.3
  140.1 0.7 stack_reshape.3
  140.8 36.9 %all-gather.9.cloned.1.call-done = bf16[16,64,1024]{2,1,0:T(8,128)(2,1)} async-done(((bf16[1,64,1024]{2,1,0:T(8,128)(2,1)}), bf16[16,64,1024]{2,1,0:T(8,128)(2,1)}) %all-gather.9.cloned.1.call-update) | async-done | bytes 2097168 | tf_op jit(solution)/shard_map/all_gather | solution.py:33
  177.7 42.8 %while.28 = (s32[]{:T(128)}, f32[64,1024]{1,0:T(8,128)S(1)}, s32[]{:T(128)}, bf16[16,8,128,128]{3,2,1,0:T(8,128)(2,1)}, bf16[16,8,8]{2,1,0:T(8,128)(2,1)S(1)}, /...) while((s32[]{:T(128)}, f32[64,1024]{1,0:T(8,128)S(1)}, s32[]{:T(128)}, ...), condition=%wide.region_2.3_spmd, body=%wide.region_1.2_spmd.sunk | while | flops 107085824 | bytes 2492555 | solution.py:50
  178.1 1.6 convolution_bitcast_fusion.12
  179.6 0.9 bitcast_add_fusion.4
  180.9 1.6 convolution_bitcast_fusion.12
  182.5 0.9 bitcast_add_fusion.4
  183.8 1.6 convolution_bitcast_fusion.12
  185.3 0.9 bitcast_add_fusion.4
  186.6 1.6 convolution_bitcast_fusion.12
  188.2 0.9 bitcast_add_fusion.4
  189.5 1.6 convolution_bitcast_fusion.12
  191.0 0.9 bitcast_add_fusion.4
  192.3 1.6 convolution_bitcast_fusion.12
  193.9 0.9 bitcast_add_fusion.4
  195.2 1.6 convolution_bitcast_fusion.12
  196.7 0.9 bitcast_add_fusion.4
  198.0 1.6 convolution_bitcast_fusion.12
  199.6 0.9 bitcast_add_fusion.4
  200.9 1.6 convolution_bitcast_fusion.12
  202.4 0.9 bitcast_add_fusion.4
  203.7 1.6 convolution_bitcast_fusion.12
  205.3 0.9 bitcast_add_fusion.4
  206.6 1.6 convolution_bitcast_fusion.12
  208.1 0.9 bitcast_add_fusion.4
  209.4 1.6 convolution_bitcast_fusion.12
  211.0 0.9 bitcast_add_fusion.4
  212.3 1.6 convolution_bitcast_fusion.12
  213.8 0.9 bitcast_add_fusion.4
  215.1 1.6 convolution_bitcast_fusion.12
  216.7 0.9 bitcast_add_fusion.4
  218.0 1.6 convolution_bitcast_fusion.12
  219.5 0.9 bitcast_add_fusion.4
  220.9 1.1 convolution_bitcast_fusion.5
  (72 shorter events, 11.0 us)
Async XLA Ops:
  8.0 0.8 copy-start
  8.0 2.3 copy-start.2
  8.0 42.6 %all-gather.7.cloned.1.call-start = ((), (), s32[]{:S(2)}) async-start(), calls=%async_computation.2 | async-start | bytes 3145728 | tf_op jit(solution)/shard_map/all_gather | solution.py:92
  8.8 84.8 %reduce-scatter.2.cloned.1.call-start = ((), (), s32[]{:S(2)}) async-start(), calls=%async_computation.3 | async-start | bytes 1179648 | tf_op jit(solution)/shard_map/reduce_scatter | solution.py:112
  10.6 8.4 %copy-start.4 = (bf16[8,3,128,128]{3,2,1,0:T(8,128)(2,1)S(1)}, bf16[8,3,128,128]{3,2,1,0:T(8,128)(2,1)}, u32[]{:S(2)}) copy-start(bf16[8,3,128,128]{3,2,1,0:T(8,128)(2,1)} %param.11) | copy-start | bytes 2359300
  10.6 6.7 %collective-permute-start = (bf16[1,128,512]{2,1,0:T(8,128)(2,1)S(1)}, bf16[1,128,512]{2,1,0:T(8,128)(2,1)S(1)}, u32[]{:S(2)}, u32[]{:S(2)}) collective-permute-start(bf16[1,128,512]{2,1,0:T(8,128)(2,1)S(1)} %get-tuple-element.185), channel_id=1, source_target_pairs={{0,2},{2,4},{4,6},{6,8},{8,10},{10,12},{12,14},{14,0},{1,3},{3,5},... | collective-permute-start | bytes 393224 | tf_op jit(solution)/shard_map/ppermute | solution.py:19
  11.9 7.0 %collective-permute-start.1 = (bf16[1,128,512]{2,1,0:T(8,128)(2,1)S(1)}, bf16[1,128,512]{2,1,0:T(8,128)(2,1)S(1)}, u32[]{:S(2)}, u32[]{:S(2)}) collective-permute-start(bf16[1,128,512]{2,1,0:T(8,128)(2,1)S(1)} %get-tuple-element.186), channel_id=1, source_target_pairs={{2,0},{4,2},{6,4},{8,6},{10,8},{12,10},{14,12},{0,14},{3,1},{5,3},... | collective-permute-start | bytes 393224 | tf_op jit(solution)/shard_map/ppermute | solution.py:21
  50.6 4.0 %copy-start.1 = (f32[1,8,128,128]{3,2,1,0:T(8,128)S(1)}, f32[1,8,128,128]{3,2,1,0:T(8,128)}, u32[]{:S(2)}) copy-start(f32[1,8,128,128]{3,2,1,0:T(8,128)} %param.14) | copy-start | bytes 1572868
  54.5 40.3 %copy-start.5 = (s32[1,8]{1,0:T(1,128)S(1)}, s32[1,8]{1,0:T(1,128)}, u32[]{:S(2)}) copy-start(s32[1,8]{1,0:T(1,128)} %param.15) | copy-start | bytes 100
  54.6 63.8 %all-gather.5.cloned.1.call-start = ((), (), s32[]{:S(2)}) async-start(), calls=%async_computation.1 | async-start | bytes 4456448 | tf_op jit(solution)/shard_map/all_gather | solution.py:33
  55.4 82.8 %all-gather.11.cloned.1.call-start = ((), (), s32[]{:S(2)}) async-start(), calls=%async_computation.5 | async-start | bytes 2228224 | tf_op jit(solution)/shard_map/all_gather | solution.py:33
  96.0 81.7 %all-gather.9.cloned.1.call-start = ((), (), s32[]{:S(2)}) async-start(), calls=%async_computation.4 | async-start | bytes 2228224 | tf_op jit(solution)/shard_map/all_gather | solution.py:33
  138.2 0.9 copy-start.3
Sparse Core Ops, SparseCore 0:
  10.6 39.9 all-gather.6
  54.7 38.7 reduce-scatter.1
Sparse Core Ops, SparseCore 1:
  57.4 40.7 all-gather.4
  100.5 37.6 all-gather.10
  139.9 37.8 all-gather.8
where the time goes:
time: 231 us
  waiting for transfers between devices  130 us (56%)
  matrix products  37.1 us (16%)
  blocking collectives  20.6 us (9%)
  other arithmetic  17.6 us (8%)
  between operations  15.9 us (7%)
  local copies, waits for them, and re-layouts  4.34 us (2%)
  starting transfers between devices  4.04 us (2%)
    all_gather x3, waiting for transfers between devices, entering(): lax.all_gather(a.astype(kind), axis)  56.7 us
    reduce_scatter x1, waiting for transfers between devices, on_device(): lax.psum_scatter((jnp.einsum('tcm,cr->mtr', localized, full_anomalies, pr...  38.1 us
    all_gather x1, waiting for transfers between devices, on_device(): full_anomalies = lax.all_gather(anomalies, 'ens', axis=1, tiled=True)  30.3 us
    dot_general x16, matrix products, forward_apply(): jnp.einsum('mic,idc->mid', chosen, blocks, precision=precise_mode)  24.6 us
    all_gather x1, blocking collectives, entering(): lax.all_gather(a.astype(kind), axis)  20.6 us
    add x15, other arithmetic, forward_combine(): forward_apply(later[0], later[1], earlier[2]) + later[2]  14.1 us
  transfers between devices with their start and end apart: 7, of which 6 were waited for; matrix products, arithmetic and copies ran while one was open for 4% of the time, Pallas kernels for 0%

commit v1 on v0

v1 whole, which is shorter than its diff:
```python
import functools

import jax
import jax.numpy as jnp
from jax import lax
from jax.experimental import pallas as pl
from jax.experimental.pallas import tpu as pltpu
from jax.sharding import Mesh
from jax.sharding import PartitionSpec as P

BLK = 128
NB = 8
COLS = NB * BLK
bf16 = jnp.bfloat16
f32 = jnp.float32
i32 = jnp.int32

VM = pl.BlockSpec(memory_space=pltpu.VMEM)
SM = pl.BlockSpec(memory_space=pltpu.SMEM)
HBM = pl.BlockSpec(memory_space=pltpu.HBM)
MIB = 1024 * 1024
NT = (((1,), (1,)), ((), ()))


def call(kernel, outs, ins, scratch=(), flops=0, data=0, grant=16, specs=None):
    made = pl.pallas_call(
        kernel,
        out_shape=outs,
        in_specs=ins,
        out_specs=specs or [VM] * len(outs),
        scratch_shapes=list(scratch),
        compiler_params=pltpu.CompilerParams(vmem_limit_bytes=grant * MIB),
        cost_estimate=pl.CostEstimate(flops=flops, bytes_accessed=data, transcendentals=0),
    )

    def run(*args):
        args = [pltpu.with_memory_space_constraint(a, pltpu.HBM) if i is HBM else a for a, i in zip(args, ins)]
        return made(*args)

    return run


def cols_at(i):
    return pl.ds(pl.multiple_of(i * BLK, BLK), BLK)


def rows_at(i, n):
    return pl.ds(pl.multiple_of(i * n, n), n)


def copies_of(pairs, sem):
    out = [pltpu.make_async_copy(a, b, sem.at[i]) for i, (a, b) in enumerate(pairs)]
    for c in out:
        c.start()
    return out


def entry_kernel(innov, cell, order, anom, loc, spread, up, down, piece, innov_v, cell_v, order_s, edge, ends, sem):
    co = lax.axis_index("co")
    cells = anom.shape[0]
    n = loc.shape[0]
    h = piece.shape[0]
    copies = copies_of(
        (
            (innov, innov_v),
            (cell, cell_v),
            (order, order_s),
            (anom.at[pl.ds(cells - BLK, BLK)], edge.at[0]),
            (anom.at[pl.ds(0, BLK)], edge.at[1]),
            (loc.at[n - 1, 2], ends.at[0]),
            (loc.at[0, 0], ends.at[1]),
            (anom.at[rows_at(co, h)], piece),
        ),
        sem,
    )
    for c in copies[:3]:
        c.wait()
    x = innov_v[...]
    hi = x.astype(bf16)
    mid = (x - hi.astype(f32)).astype(bf16)
    lo = (x - hi.astype(f32) - mid.astype(f32)).astype(bf16)
    rows = jnp.concatenate([hi, mid, lo, jnp.zeros((5, x.shape[1]), bf16)], axis=0)
    ids = lax.broadcasted_iota(i32, (cells, 1), 0)
    hit = jnp.where(ids == cell_v[...], 1.0, 0.0).astype(bf16)
    y = lax.dot_general(rows, hit, NT, preferred_element_type=f32)
    w = y[0:1] + y[1:2] + y[2:3]
    lane = lax.broadcasted_iota(i32, (8, BLK), 1)
    tag = jnp.zeros((8, BLK), f32)
    for i in range(NB):
        tag = jnp.where(lane == i, order_s[0, i].astype(f32), tag)
    one = jnp.concatenate([w[:, i * BLK : (i + 1) * BLK] for i in range(cells // BLK)] + [tag], axis=0)
    for k in range(spread.shape[0]):
        spread[k] = one
    for c in copies[3:]:
        c.wait()
    half = edge.shape[2]
    for j, out in enumerate((up, down)):
        out[:, :half] = edge[j]
        out[:, half:] = ends[j]


def plan_kernel(recv, tang, wt, blocks, traj, tang_v, ints, order_s, traj_s, sem):
    z = lax.axis_index("z")
    co = lax.axis_index("co")
    steps = recv.shape[0]
    (c,) = copies_of(((tang, tang_v),), sem)
    for k in range(steps):
        ints[k : k + 1] = recv[k, 8:9, :].astype(i32)
    d = pltpu.make_async_copy(ints, order_s, sem.at[1])
    d.start()
    pad = jnp.zeros((BLK - steps, BLK), f32)
    for i in range(8):
        part = jnp.concatenate([recv[:, i, :], pad], axis=0)
        wt[i * BLK : (i + 1) * BLK] = part.T
    d.wait()
    for q in range(NB):
        b = jnp.int32(q)
        for t in range(steps - 1, -1, -1):
            traj[t + 1, q] = b
            b = order_s[t, b]
        traj[0, q] = b
    mine = 2 * z + co + 1
    c.wait()
    for q in range(NB):
        blocks[q] = tang_v[traj[mine, q]].astype(bf16)


def ready_kernel(anom, loc, up0, up1, down0, down1, lt, gown, asel, anom_v, loc_v, pad, sem):
    co = lax.axis_index("co")
    copies = copies_of(((loc, loc_v), (anom, anom_v)), sem)
    n = loc.shape[0]
    half = anom.shape[1]
    before = jnp.where(co == 0, up0[:, :half], up1[:, :half])
    after = jnp.where(co == 0, down0[:, :half], down1[:, :half])
    copies[0].wait()
    for b in range(n):
        prev = up0[:, half:] if b == 0 else loc_v[b - 1, 2]
        nxt = down0[:, half:] if b == n - 1 else loc_v[b + 1, 0]
        lt[b] = jnp.concatenate([prev.T, loc_v[b, 1].T, nxt.T], axis=1)
    copies[1].wait()
    pad[:BLK] = before
    pad[BLK : BLK + n * BLK] = anom_v[...]
    pad[BLK + n * BLK :] = after
    for b in range(n):
        y = jnp.dot(lt[b], pad[b * BLK : (b + 3) * BLK], preferred_element_type=f32)
        gown[b * BLK : (b + 1) * BLK] = y.astype(bf16)
    at = anom_v[...].T
    for k in range(half // 64):
        asel[k * 32 : (k + 1) * 32] = jnp.where(co == 0, at[k * 64 : k * 64 + 32], at[k * 64 + 32 : (k + 1) * 64])


def product_kernel(scale, near, far, up0, up1, down0, down1, lt, gown, asel, wt, traj, out, pad, full, vals):
    co = lax.axis_index("co")
    e = lax.axis_index("ens")
    z = lax.axis_index("z")
    h, half = near.shape
    n = lt.shape[0]
    pad[:BLK] = jnp.where(co == 0, up1[:, :half], up0[:, :half])
    pad[pl.ds(pl.multiple_of(BLK + co * h, BLK), h)] = near[...]
    pad[pl.ds(pl.multiple_of(BLK + (1 - co) * h, BLK), h)] = far[...]
    pad[BLK + n * BLK :] = jnp.where(co == 0, down1[:, :half], down0[:, :half])
    there = pl.ds(pl.multiple_of((1 - e) * half, half), half)
    full[:, pl.ds(pl.multiple_of(e * half, half), half)] = gown[...]
    for b in range(n):
        y = jnp.dot(lt[b], pad[b * BLK : (b + 3) * BLK], preferred_element_type=f32)
        full[b * BLK : (b + 1) * BLK, there] = y.astype(bf16)
    steps = vals.shape[1] // BLK
    group = 4
    for g in range(0, steps, group):
        for t in range(g, g + group):
            y = wt[:, t : t + 1] * full[:, cols_at(traj[t + 1, z])].astype(f32)
            vals[:, t * BLK : (t + 1) * BLK] = y.astype(bf16)
        at = slice(g * BLK, (g + group) * BLK)
        y = jnp.dot(asel[...], vals[:, at], preferred_element_type=f32)
        out[:, at] = (y * scale).astype(bf16)


def split(x):
    hi = x.astype(bf16)
    lo = (x - hi.astype(f32)).astype(bf16)
    return jnp.concatenate([hi, lo], axis=0)


def times(x, block, transposed):
    dims = NT if transposed else (((1,), (0,)), ((), ()))
    y = lax.dot_general(split(x), block, dims, preferred_element_type=f32)
    rows = x.shape[0]
    return y[:rows] + y[rows:]


def scan_kernel(parts, mine, theirs, out):
    co = lax.axis_index("co")
    n = parts.shape[0]
    steps = parts.shape[2] // BLK
    even = jnp.where(co == 0, mine[...], theirs[...])
    odd = jnp.where(co == 0, theirs[...], mine[...])
    blocks = [(even if t % 2 == 0 else odd)[t // 2] for t in range(steps)]
    force = []
    for t in range(steps):
        at = slice(t * BLK, (t + 1) * BLK)
        y = parts[0, :, at].astype(f32)
        for s in range(1, n):
            y = y + parts[s, :, at].astype(f32)
        force.append(y)
    x = force[0]
    y = times(force[steps - 1], blocks[steps - 1], False)
    out[0, 0] = x.astype(bf16)
    out[steps - 1, 1] = y.astype(bf16)
    for k in range(1, steps):
        t = steps - 1 - k
        x = times(x, blocks[k], True) + force[k]
        y = times(y + force[t], blocks[t], False)
        out[k, 0] = x.astype(bf16)
        out[t, 1] = y.astype(bf16)


def place_kernel(recv, traj, x, y):
    t = 2 * lax.axis_index("z") + lax.axis_index("co")
    rows = recv.shape[2]
    for q in range(NB):
        for c in range(2):
            at = slice(c * rows, (c + 1) * rows)
            x[0, at, cols_at(traj[t + 1, q])] = recv[2 * q + c, 0].astype(f32)
            y[0, at, cols_at(traj[t, q])] = recv[2 * q + c, 1].astype(f32)


def on_device(anomalies, localization, innovations, obs_cell, tangent_blocks, tangent_order):
    cells, half = anomalies.shape
    n_lon = lax.axis_size("lon")
    nz = lax.axis_size("z")
    steps = 2 * nz
    shape = jax.ShapeDtypeStruct
    swap = [(0, 1), (1, 0)]
    scale = float(cells * n_lon) ** (-0.5)
    n = cells // BLK
    time = ("z", "co")

    spread, tail, head, piece = call(
        entry_kernel,
        [
            shape((steps, 16, BLK), f32),
            shape((BLK, half + BLK), bf16),
            shape((BLK, half + BLK), bf16),
            shape((cells // 2, half), bf16),
        ],
        [HBM] * 5,
        [
            pltpu.VMEM(innovations.shape, f32),
            pltpu.VMEM(obs_cell.shape, i32),
            pltpu.SMEM(tangent_order.shape, i32),
            pltpu.VMEM((2, BLK, half), bf16),
            pltpu.VMEM((2, BLK, BLK), bf16),
            pltpu.SemaphoreType.DMA((8,)),
        ],
        flops=10**7,
        data=10**6,
    )(innovations, obs_cell, tangent_order, anomalies, localization)

    upward, downward = [], []
    for c in range(2):
        for k in range(n_lon):
            for e in range(2):
                f = e if c == 0 else 1 - e
                k2 = (k + 1) % n_lon
                upward.append(((c * n_lon + k) * 2 + e, (c * n_lon + k2) * 2 + f))
                downward.append(((c * n_lon + k2) * 2 + e, (c * n_lon + k) * 2 + f))
    up0 = lax.ppermute(tail, ("co", "lon", "ens"), upward)
    down0 = lax.ppermute(head, ("co", "lon", "ens"), downward)
    near = lax.ppermute(piece, "ens", swap)
    recv = lax.all_to_all(spread, time, 0, 0, tiled=True)
    wt, blocks, traj = call(
        plan_kernel,
        [shape((cells, BLK), f32), shape((NB, BLK, BLK), bf16), shape((steps + 1, NB), i32)],
        [VM, HBM],
        [
            pltpu.VMEM((NB, BLK, BLK), f32),
            pltpu.VMEM((steps, BLK), i32),
            pltpu.SMEM((steps, BLK), i32),
            pltpu.SMEM((8, BLK), i32),
            pltpu.SemaphoreType.DMA((2,)),
        ],
        flops=10**6,
        data=10**6,
        specs=[VM, VM, SM],
    )(recv, tangent_blocks.reshape(NB, BLK, BLK))
    mine = lax.all_to_all(blocks, "z", 0, 0, tiled=True)

    up1 = lax.ppermute(up0, "co", swap)
    down1 = lax.ppermute(down0, "co", swap)
    lt, gown, asel = call(
        ready_kernel,
        [shape((n, BLK, 3 * BLK), bf16), shape((cells, half), bf16), shape((half // 2, cells), bf16)],
        [HBM, HBM, VM, VM, VM, VM],
        [
            pltpu.VMEM(anomalies.shape, bf16),
            pltpu.VMEM(localization.shape, bf16),
            pltpu.VMEM((cells + 2 * BLK, half), bf16),
            pltpu.SemaphoreType.DMA((2,)),
        ],
        flops=10**9,
        data=4 * 10**6,
    )(anomalies, localization, up0, up1, down0, down1)
    far = lax.ppermute(near, "co", swap)
    (prod,) = call(
        functools.partial(product_kernel, scale),
        [shape((half // 2, steps * BLK), bf16)],
        [VM] * 10 + [SM],
        [
            pltpu.VMEM((cells + 2 * BLK, half), bf16),
            pltpu.VMEM((cells, COLS), bf16),
            pltpu.VMEM((cells, steps * BLK), bf16),
        ],
        flops=10**9,
        data=4 * 10**6,
        grant=24,
    )(near, far, up0, up1, down0, down1, lt, gown, asel, wt, traj)
    rows = half // 2 // n_lon
    parts = lax.all_to_all(prod, "lon", 0, 0, tiled=True).reshape(n_lon, rows, steps * BLK)
    theirs = lax.ppermute(mine, "co", swap)
    (states,) = call(
        scan_kernel, [shape((steps, 2, rows, BLK), bf16)], [VM] * 3, flops=10**9, data=2 * 10**6
    )(parts, mine, theirs)
    back = lax.all_to_all(states, time, 0, 0, tiled=True)
    x, y = call(place_kernel, [shape((1, 2 * rows, COLS), f32)] * 2, [VM, SM], flops=10**6, data=10**6)(back, traj)
    return x, y


def solution(mesh):
    tm, lon, ens = (mesh.shape[a] for a in ("tm", "lon", "ens"))
    fine = Mesh(mesh.devices.reshape(tm // 2, 2, lon, ens), ("z", "co", "lon", "ens"))
    time = ("z", "co")
    placed = (
        P("lon", "ens"),
        P("lon", None, None, None),
        P(time, "lon"),
        P(time, "lon"),
        P(time, None, None, None),
        P(time, None),
    )
    outs = P(time, ("ens", "lon"), None)

    return jax.shard_map(on_device, mesh=fine, in_specs=placed, out_specs=(outs, outs), check_vma=False)
```

time: 231 us -> 86.5 us (0.37)
  the two profiles are of different devices: /device:TPU:225 before, /device:TPU:1 now
where the time goes in v1:
time: 86.5 us; the launch traced here: 86.1 us
  starting transfers between devices  33 us (38%)
  waiting for transfers between devices  20.2 us (23%)
  blocking collectives  16.7 us (19%)
  Pallas kernels  15.4 us (18%)
    all_to_all x1, blocking collectives, on_device(): back = lax.all_to_all(states, time, 0, 0, tiled=True)  16.7 us
    pallas_call x6, Pallas kernels, run(): return made(*args)  15.4 us
    all_to_all x1, waiting for transfers between devices, on_device(): lax.all_to_all(prod, 'lon', 0, 0, tiled=True)  13.7 us
    all_to_all x1, starting transfers between devices, on_device(): recv = lax.all_to_all(spread, time, 0, 0, tiled=True)  9.43 us
    all_to_all x1, starting transfers between devices, on_device(): mine = lax.all_to_all(blocks, 'z', 0, 0, tiled=True)  7.91 us
    ppermute x1, starting transfers between devices, on_device(): near = lax.ppermute(piece, 'ens', swap)  3.65 us
    all_to_all x1, starting transfers between devices, on_device(): lax.all_to_all(prod, 'lon', 0, 0, tiled=True)  3.56 us
    all_to_all x1, waiting for transfers between devices, on_device(): mine = lax.all_to_all(blocks, 'z', 0, 0, tiled=True)  2.72 us
  transfers between devices with their start and end apart: 10, of which 7 were waited for; matrix products, arithmetic and copies ran while one was open for 0% of the time, Pallas kernels for 11%

profile of v1, /device:TPU:1, one launch (start us, length us, event | category | flops | bytes accessed | tf_op | source)
XLA Modules:
  0.0 86.1 jit_solution(9280753021695085816)
XLA Ops:
  0.6 2.0 %shard_map.77 = (f32[16,16,128]{2,1,0:T(8,128)}, bf16[128,640]{1,0:T(8,128)(2,1)S(1)}, bf16[128,640]{1,0:T(8,128)(2,1)S(1)}, bf16[512,512]{1,0:T(8,128)(2,1)S(1)}) custom-call(f32[1,512]{1,0:T(1,128)} %innov.1, s32[1,512]{1,0:T(1,128)} %cell.1, s32[1,8]{1,0:T(1,128)} %order.1, bf16[1024,512]{1,0:T(8,128)(2,1)} %anom.3, bf16[8,3,128,128]{3,2,1,0:T(8,128)(2,1)} %loc.3), custom_call_target="tpu_custom_call" | custom-call | flops 10000000 | bytes 1000000 | tf_op jit(solution)/shard_map/pallas_call | solution.py:38
  2.6 3.6 %collective-permute-start = (bf16[512,512]{1,0:T(8,128)(2,1)S(1)}, bf16[512,512]{1,0:T(8,128)(2,1)S(1)}, u32[]{:S(2)}, u32[]{:S(2)}) collective-permute-start(bf16[512,512]{1,0:T(8,128)(2,1)S(1)} %get-tuple-element.12), channel_id=1, source_target_pairs={{0,1},{1,0},{2,3},{3,2},{4,5},{5,4},{6,7},{7,6},{8,9},{9,8},{10,11... | collective-permute-start | bytes 1572872 | tf_op jit(solution)/shard_map/ppermute | solution.py:269
  6.3 9.4 %all-to-all-start = ((f32[16,16,128]{2,1,0:T(8,128)}), f32[16,16,128]{2,1,0:T(8,128)S(1)}, u32[]{:S(2)}, u32[]{:S(2)}) async-start(f32[16,16,128]{2,1,0:T(8,128)} %get-tuple-element.18), calls=%async_computation | async-start | bytes 262144 | tf_op jit(solution)/shard_map/all_to_all | solution.py:270
  15.7 1.2 %collective-permute-done.near = bf16[512,512]{1,0:T(8,128)(2,1)S(1)} collective-permute-done((bf16[512,512]{1,0:T(8,128)(2,1)S(1)}, bf16[512,512]{1,0:T(8,128)(2,1)S(1)}, u32[]{:S(2)}, u32[]{:S(2)}) %collective-permute-start) | collective-permute-done | bytes 524320 | tf_op jit(solution)/shard_map/ppermute | solution.py:269
  16.9 2.3 %collective-permute-start.1 = (bf16[512,512]{1,0:T(8,128)(2,1)S(1)}, bf16[512,512]{1,0:T(8,128)(2,1)S(1)}, u32[]{:S(2)}, u32[]{:S(2)}) collective-permute-start(bf16[512,512]{1,0:T(8,128)(2,1)S(1)} %collective-permute-done.near), channel_id=1, source_target_pairs={{0,16},{16,0},{1,17},{17,1},{2,18},{18,2},{3,19},{19,3},{4,20},{20... | collective-permute-start | bytes 1572872 | tf_op jit(solution)/shard_map/ppermute | solution.py:303
  19.2 2.7 %collective-permute-start.2 = (bf16[128,640]{1,0:T(8,128)(2,1)S(1)}, bf16[128,640]{1,0:T(8,128)(2,1)S(1)}, u32[]{:S(2)}, u32[]{:S(2)}) collective-permute-start(bf16[128,640]{1,0:T(8,128)(2,1)S(1)} %get-tuple-element.13), channel_id=1, source_target_pairs={{0,2},{1,3},{2,4},{3,5},{4,6},{5,7},{6,8},{7,9},{8,10},{9,11},{10,... | collective-permute-start | bytes 491528 | tf_op jit(solution)/shard_map/ppermute | solution.py:267
  21.9 2.5 %collective-permute-start.4 = (bf16[128,640]{1,0:T(8,128)(2,1)S(1)}, bf16[128,640]{1,0:T(8,128)(2,1)S(1)}, u32[]{:S(2)}, u32[]{:S(2)}) collective-permute-start(bf16[128,640]{1,0:T(8,128)(2,1)S(1)} %get-tuple-element.14), channel_id=1, source_target_pairs={{2,0},{3,1},{4,2},{5,3},{6,4},{7,5},{8,6},{9,7},{10,8},{11,9},{12,... | collective-permute-start | bytes 491528 | tf_op jit(solution)/shard_map/ppermute | solution.py:268
  24.3 0.3 all-to-all-done.recv
  24.6 1.9 %shard_map.79 = (f32[1024,128]{1,0:T(8,128)S(1)}, bf16[8,128,128]{2,1,0:T(8,128)(2,1)}, s32[17,8]{1,0:T(8,128)S(1)}) custom-call(f32[16,16,128]{2,1,0:T(8,128)S(1)} %all-to-all-done.recv, f32[8,128,128]{2,1,0:T(8,128)} %bitcast.2), custom_call_target="tpu_custom_call" | custom-call | flops 1000000 | bytes 1000000 | tf_op jit(solution)/shard_map/pallas_call | solution.py:38
  26.5 7.9 %all-to-all-start.2 = ((bf16[8,128,128]{2,1,0:T(8,128)(2,1)}), bf16[8,128,128]{2,1,0:T(8,128)(2,1)S(1)}, u32[]{:S(2)}, u32[]{:S(2)}) async-start(bf16[8,128,128]{2,1,0:T(8,128)(2,1)} %get-tuple-element.21), calls=%async_computation.2 | async-start | bytes 524288 | tf_op jit(solution)/shard_map/all_to_all | solution.py:286
  34.4 0.0 collective-permute-done.2.up0
  34.4 0.1 collective-permute-start.3
  34.5 0.0 collective-permute-done.4.down0
  34.5 0.5 collective-permute-start.5
  35.0 0.9 %collective-permute-done.3.up1 = bf16[128,640]{1,0:T(8,128)(2,1)S(1)} collective-permute-done((bf16[128,640]{1,0:T(8,128)(2,1)S(1)}, bf16[128,640]{1,0:T(8,128)(2,1)S(1)}, u32[]{:S(2)}, u32[]{:S(2)}) %collective-permute-start.3) | collective-permute-done | bytes 163872 | tf_op jit(solution)/shard_map/ppermute | solution.py:288
  35.9 0.2 collective-permute-done.5.down1
  36.1 2.2 %shard_map.78 = (bf16[8,128,384]{2,1,0:T(8,128)(2,1)S(1)}, bf16[1024,512]{1,0:T(8,128)(2,1)S(1)}, bf16[256,1024]{1,0:T(8,128)(2,1)S(1)}) custom-call(bf16[1024,512]{1,0:T(8,128)(2,1)} %anom.3, bf16[8,3,128,128]{3,2,1,0:T(8,128)(2,1)} %loc.3, bf16[128,640]{1,0:T(8,128)(2,1)S(1)} %collective-permute-done.2.up0, ...), custom_call_target="tpu_custom_call" | custom-call | flops 1000000000 | bytes 4000000 | tf_op jit(solution)/shard_map/pallas_call | solution.py:38
  38.3 0.0 collective-permute-done.1.far
  38.4 5.7 %shard_map.80 = bf16[256,2048]{1,0:T(8,128)(2,1)} custom-call(bf16[512,512]{1,0:T(8,128)(2,1)S(1)} %collective-permute-done.near, bf16[512,512]{1,0:T(8,128)(2,1)S(1)} %collective-permute-done.1.far, bf16[128,640]{1,0:T(8,128)(2,1)S(1)} %collective-permute-done.2.up0, bf16[128,640]{1,0:T(8,128)(2,1)S(1)} %collective-permute-done.3.up1, ...), custom_call_target="tpu_custom_call" | custom-call | flops 1000000000 | bytes 4000000 | tf_op jit(solution)/shard_map/pallas_call | solution.py:38
  44.1 2.7 %all-to-all-done.2.mine = bf16[8,128,128]{2,1,0:T(8,128)(2,1)S(1)} async-done(((bf16[8,128,128]{2,1,0:T(8,128)(2,1)}), bf16[8,128,128]{2,1,0:T(8,128)(2,1)S(1)}, u32[]{:S(2)}, u32[]{:S(2)}) %all-to-all-start.2) | async-done | bytes 262176 | tf_op jit(solution)/shard_map/all_to_all | solution.py:286
  46.8 3.6 %all-to-all-start.1 = ((bf16[8,32,2048]{2,1,0:T(8,128)(2,1)}), bf16[8,32,2048]{2,1,0:T(8,128)(2,1)S(1)}, u32[]{:S(2)}, u32[]{:S(2)}) async-start(bf16[8,32,2048]{2,1,0:T(8,128)(2,1)} %bitcast.1), calls=%async_computation.1 | async-start | bytes 2097152 | tf_op jit(solution)/shard_map/all_to_all | solution.py:318
  50.4 0.5 collective-permute-start.6
  50.8 1.2 %collective-permute-done.6.theirs = bf16[8,128,128]{2,1,0:T(8,128)(2,1)S(1)} collective-permute-done((bf16[8,128,128]{2,1,0:T(8,128)(2,1)S(1)}, bf16[8,128,128]{2,1,0:T(8,128)(2,1)S(1)}, u32[]{:S(2)}, u32[]{:S(2)}) %collective-permute-start.6) | collective-permute-done | bytes 262176 | tf_op jit(solution)/shard_map/ppermute | solution.py:319
  52.0 13.7 %all-to-all-done.1.parts = bf16[8,32,2048]{2,1,0:T(8,128)(2,1)S(1)} async-done(((bf16[8,32,2048]{2,1,0:T(8,128)(2,1)}), bf16[8,32,2048]{2,1,0:T(8,128)(2,1)S(1)}, u32[]{:S(2)}, u32[]{:S(2)}) %all-to-all-start.1) | async-done | bytes 1048608 | tf_op jit(solution)/shard_map/all_to_all | solution.py:318
  65.7 2.0 %shard_map.81 = bf16[16,2,32,128]{3,2,1,0:T(8,128)(2,1)S(1)} custom-call(bf16[8,32,2048]{2,1,0:T(8,128)(2,1)S(1)} %all-to-all-done.1.parts, bf16[8,128,128]{2,1,0:T(8,128)(2,1)S(1)} %all-to-all-done.2.mine, bf16[8,128,128]{2,1,0:T(8,128)(2,1)S(1)} %collective-permute-done.6.theirs), custom_call_target="tpu_custom_call" | custom-call | flops 1000000000 | bytes 2000000 | tf_op jit(solution)/shard_map/pallas_call | solution.py:38
  67.7 16.7 %all_to_all.24.recv = bf16[16,2,32,128]{3,2,1,0:T(8,128)(2,1)S(1)} all-to-all(bf16[16,2,32,128]{3,2,1,0:T(8,128)(2,1)S(1)} %shard_map.81), channel_id=1, replica_groups=mesh['z'=8,'co'=2,'lon'=8,'ens'=2] {'z','co'}, dimensions={0} | all-to-all | bytes 524288 | tf_op jit(solution)/shard_map/all_to_all | solution.py:323
  84.5 1.6 %shard_map.82 = (f32[1,64,1024]{2,1,0:T(8,128)}, f32[1,64,1024]{2,1,0:T(8,128)}) custom-call(bf16[16,2,32,128]{3,2,1,0:T(8,128)(2,1)S(1)} %all_to_all.24.recv, s32[17,8]{1,0:T(8,128)S(1)} %get-tuple-element.20.traj), custom_call_target="tpu_custom_call" | custom-call | flops 1000000 | bytes 1000000 | tf_op jit(solution)/shard_map/pallas_call | solution.py:38
Async XLA Ops:
  2.6 14.3 %collective-permute-start = (bf16[512,512]{1,0:T(8,128)(2,1)S(1)}, bf16[512,512]{1,0:T(8,128)(2,1)S(1)}, u32[]{:S(2)}, u32[]{:S(2)}) collective-permute-start(bf16[512,512]{1,0:T(8,128)(2,1)S(1)} %get-tuple-element.12), channel_id=1, source_target_pairs={{0,1},{1,0},{2,3},{3,2},{4,5},{5,4},{6,7},{7,6},{8,9},{9,8},{10,11... | collective-permute-start | bytes 1572872 | tf_op jit(solution)/shard_map/ppermute | solution.py:269
  6.3 18.3 %all-to-all-start = ((f32[16,16,128]{2,1,0:T(8,128)}), f32[16,16,128]{2,1,0:T(8,128)S(1)}, u32[]{:S(2)}, u32[]{:S(2)}) async-start(f32[16,16,128]{2,1,0:T(8,128)} %get-tuple-element.18), calls=%async_computation | async-start | bytes 262144 | tf_op jit(solution)/shard_map/all_to_all | solution.py:270
  16.9 21.5 %collective-permute-start.1 = (bf16[512,512]{1,0:T(8,128)(2,1)S(1)}, bf16[512,512]{1,0:T(8,128)(2,1)S(1)}, u32[]{:S(2)}, u32[]{:S(2)}) collective-permute-start(bf16[512,512]{1,0:T(8,128)(2,1)S(1)} %collective-permute-done.near), channel_id=1, source_target_pairs={{0,16},{16,0},{1,17},{17,1},{2,18},{18,2},{3,19},{19,3},{4,20},{20... | collective-permute-start | bytes 1572872 | tf_op jit(solution)/shard_map/ppermute | solution.py:303
  19.2 15.3 %collective-permute-start.2 = (bf16[128,640]{1,0:T(8,128)(2,1)S(1)}, bf16[128,640]{1,0:T(8,128)(2,1)S(1)}, u32[]{:S(2)}, u32[]{:S(2)}) collective-permute-start(bf16[128,640]{1,0:T(8,128)(2,1)S(1)} %get-tuple-element.13), channel_id=1, source_target_pairs={{0,2},{1,3},{2,4},{3,5},{4,6},{5,7},{6,8},{7,9},{8,10},{9,11},{10,... | collective-permute-start | bytes 491528 | tf_op jit(solution)/shard_map/ppermute | solution.py:267
  21.9 12.7 %collective-permute-start.4 = (bf16[128,640]{1,0:T(8,128)(2,1)S(1)}, bf16[128,640]{1,0:T(8,128)(2,1)S(1)}, u32[]{:S(2)}, u32[]{:S(2)}) collective-permute-start(bf16[128,640]{1,0:T(8,128)(2,1)S(1)} %get-tuple-element.14), channel_id=1, source_target_pairs={{2,0},{3,1},{4,2},{5,3},{6,4},{7,5},{8,6},{9,7},{10,8},{11,9},{12,... | collective-permute-start | bytes 491528 | tf_op jit(solution)/shard_map/ppermute | solution.py:268
  26.5 20.3 %all-to-all-start.2 = ((bf16[8,128,128]{2,1,0:T(8,128)(2,1)}), bf16[8,128,128]{2,1,0:T(8,128)(2,1)S(1)}, u32[]{:S(2)}, u32[]{:S(2)}) async-start(bf16[8,128,128]{2,1,0:T(8,128)(2,1)} %get-tuple-element.21), calls=%async_computation.2 | async-start | bytes 524288 | tf_op jit(solution)/shard_map/all_to_all | solution.py:286
  34.4 1.5 %collective-permute-start.3 = (bf16[128,640]{1,0:T(8,128)(2,1)S(1)}, bf16[128,640]{1,0:T(8,128)(2,1)S(1)}, u32[]{:S(2)}, u32[]{:S(2)}) collective-permute-start(bf16[128,640]{1,0:T(8,128)(2,1)S(1)} %collective-permute-done.2.up0), channel_id=1, source_target_pairs={{0,16},{16,0},{1,17},{17,1},{2,18},{18,2},{3,19},{19,3},{4,20},{20... | collective-permute-start | bytes 491528 | tf_op jit(solution)/shard_map/ppermute | solution.py:288
  34.5 1.6 %collective-permute-start.5 = (bf16[128,640]{1,0:T(8,128)(2,1)S(1)}, bf16[128,640]{1,0:T(8,128)(2,1)S(1)}, u32[]{:S(2)}, u32[]{:S(2)}) collective-permute-start(bf16[128,640]{1,0:T(8,128)(2,1)S(1)} %collective-permute-done.4.down0), channel_id=1, source_target_pairs={{0,16},{16,0},{1,17},{17,1},{2,18},{18,2},{3,19},{19,3},{4,20},{20... | collective-permute-start | bytes 491528 | tf_op jit(solution)/shard_map/ppermute | solution.py:289
  46.8 18.9 %all-to-all-start.1 = ((bf16[8,32,2048]{2,1,0:T(8,128)(2,1)}), bf16[8,32,2048]{2,1,0:T(8,128)(2,1)S(1)}, u32[]{:S(2)}, u32[]{:S(2)}) async-start(bf16[8,32,2048]{2,1,0:T(8,128)(2,1)} %bitcast.1), calls=%async_computation.1 | async-start | bytes 2097152 | tf_op jit(solution)/shard_map/all_to_all | solution.py:318
  50.4 1.6 %collective-permute-start.6 = (bf16[8,128,128]{2,1,0:T(8,128)(2,1)S(1)}, bf16[8,128,128]{2,1,0:T(8,128)(2,1)S(1)}, u32[]{:S(2)}, u32[]{:S(2)}) collective-permute-start(bf16[8,128,128]{2,1,0:T(8,128)(2,1)S(1)} %all-to-all-done.2.mine), channel_id=1, source_target_pairs={{0,16},{16,0},{1,17},{17,1},{2,18},{18,2},{3,19},{19,3},{4,20},{20... | collective-permute-start | bytes 786440 | tf_op jit(solution)/shard_map/ppermute | solution.py:319

commit v2 on v1

--- a/solution.py
+++ b/solution.py
@@ -19,6 +19,7 @@
 SM = pl.BlockSpec(memory_space=pltpu.SMEM)
 HBM = pl.BlockSpec(memory_space=pltpu.HBM)
 MIB = 1024 * 1024
+WT = f32
 NT = (((1,), (1,)), ((), ()))
 
 
@@ -55,7 +56,9 @@
     return out
 
 
-def entry_kernel(innov, cell, order, anom, loc, spread, up, down, piece, innov_v, cell_v, order_s, edge, ends, sem):
+def entry_kernel(
+    innov, cell, order, anom, loc, tang, spread, up, down, piece, own, innov_v, cell_v, order_s, edge, ends, tang_v, sem
+):
     co = lax.axis_index("co")
     cells = anom.shape[0]
     n = loc.shape[0]
@@ -70,6 +73,7 @@
             (loc.at[n - 1, 2], ends.at[0]),
             (loc.at[0, 0], ends.at[1]),
             (anom.at[rows_at(co, h)], piece),
+            (tang, tang_v),
         ),
         sem,
     )
@@ -97,21 +101,19 @@
     for j, out in enumerate((up, down)):
         out[:, :half] = edge[j]
         out[:, half:] = ends[j]
-
-
-def plan_kernel(recv, tang, wt, blocks, traj, tang_v, ints, order_s, traj_s, sem):
+    own[...] = tang_v[...].astype(bf16)
+
+
+def choose_kernel(own, oth, recv, traj, *refs):
+    *outs, ints, order_s, picked, sem = refs
     z = lax.axis_index("z")
     co = lax.axis_index("co")
     steps = recv.shape[0]
-    (c,) = copies_of(((tang, tang_v),), sem)
+    nz = steps // 2
     for k in range(steps):
         ints[k : k + 1] = recv[k, 8:9, :].astype(i32)
-    d = pltpu.make_async_copy(ints, order_s, sem.at[1])
+    d = pltpu.make_async_copy(ints, order_s, sem.at[0])
     d.start()
-    pad = jnp.zeros((BLK - steps, BLK), f32)
-    for i in range(8):
-        part = jnp.concatenate([recv[:, i, :], pad], axis=0)
-        wt[i * BLK : (i + 1) * BLK] = part.T
     d.wait()
     for q in range(NB):
         b = jnp.int32(q)
@@ -119,19 +121,30 @@
             traj[t + 1, q] = b
             b = order_s[t, b]
         traj[0, q] = b
-    mine = 2 * z + co + 1
-    c.wait()
-    for q in range(NB):
-        blocks[q] = tang_v[traj[mine, q]].astype(bf16)
-
-
-def ready_kernel(anom, loc, up0, up1, down0, down1, lt, gown, asel, anom_v, loc_v, pad, sem):
+    copies = []
+    for d, out in enumerate(outs):
+        q = lax.rem(jnp.where(co == 0, z + d, z + nz - d), nz)
+        copies.append((own.at[traj[2 * z + co + 1, q]], picked.at[d]))
+        if d < nz // 2:
+            copies.append((oth.at[traj[2 * z + 2 - co, q]], out.at[1 - co]))
+    for c in copies_of(copies, sem.at[pl.ds(1, len(copies))]):
+        c.wait()
+    for d, out in enumerate(outs):
+        if d < nz // 2:
+            out[co] = picked[d].astype(bf16)
+        else:
+            out[...] = picked[d].astype(bf16)
+
+
+def ready_kernel(anom, loc, up0, up1, down0, down1, lt, gown, asel, ends, anom_v, loc_v, pad, sem):
     co = lax.axis_index("co")
     copies = copies_of(((loc, loc_v), (anom, anom_v)), sem)
     n = loc.shape[0]
     half = anom.shape[1]
     before = jnp.where(co == 0, up0[:, :half], up1[:, :half])
     after = jnp.where(co == 0, down0[:, :half], down1[:, :half])
+    ends[0] = jnp.where(co == 0, up1[:, :half], up0[:, :half])
+    ends[1] = jnp.where(co == 0, down1[:, :half], down0[:, :half])
     copies[0].wait()
     for b in range(n):
         prev = up0[:, half:] if b == 0 else loc_v[b - 1, 2]
@@ -149,30 +162,48 @@
         asel[k * 32 : (k + 1) * 32] = jnp.where(co == 0, at[k * 64 : k * 64 + 32], at[k * 64 + 32 : (k + 1) * 64])
 
 
-def product_kernel(scale, near, far, up0, up1, down0, down1, lt, gown, asel, wt, traj, out, pad, full, vals):
+def product_kernel(scale, near, far, ends, lt, gown, asel, recv, out, pad, full, vals, wt, ints, order_s, sem):
     co = lax.axis_index("co")
     e = lax.axis_index("ens")
     z = lax.axis_index("z")
+    steps = recv.shape[0]
+    for k in range(steps):
+        ints[k : k + 1] = recv[k, 8:9, :].astype(i32)
     h, half = near.shape
     n = lt.shape[0]
-    pad[:BLK] = jnp.where(co == 0, up1[:, :half], up0[:, :half])
+    d, up, down = copies_of(
+        (
+            (ints, order_s),
+            (ends.at[0], pad.at[pl.ds(0, BLK)]),
+            (ends.at[1], pad.at[pl.ds(BLK + n * BLK, BLK)]),
+        ),
+        sem,
+    )
     pad[pl.ds(pl.multiple_of(BLK + co * h, BLK), h)] = near[...]
     pad[pl.ds(pl.multiple_of(BLK + (1 - co) * h, BLK), h)] = far[...]
-    pad[BLK + n * BLK :] = jnp.where(co == 0, down1[:, :half], down0[:, :half])
     there = pl.ds(pl.multiple_of((1 - e) * half, half), half)
     full[:, pl.ds(pl.multiple_of(e * half, half), half)] = gown[...]
+    blank = jnp.zeros((BLK - steps, BLK), f32)
+    up.wait()
+    down.wait()
     for b in range(n):
         y = jnp.dot(lt[b], pad[b * BLK : (b + 3) * BLK], preferred_element_type=f32)
         full[b * BLK : (b + 1) * BLK, there] = y.astype(bf16)
-    steps = vals.shape[1] // BLK
+        wt[b * BLK : (b + 1) * BLK] = jnp.concatenate([recv[:, b, :], blank], axis=0).T.astype(wt.dtype)
+    d.wait()
+    at = [None] * steps
+    b = z
+    for t in range(steps - 1, -1, -1):
+        at[t] = cols_at(b)
+        b = order_s[t, b]
     group = 4
     for g in range(0, steps, group):
         for t in range(g, g + group):
-            y = wt[:, t : t + 1] * full[:, cols_at(traj[t + 1, z])].astype(f32)
+            y = wt[:, t : t + 1] * full[:, at[t]].astype(wt.dtype)
             vals[:, t * BLK : (t + 1) * BLK] = y.astype(bf16)
-        at = slice(g * BLK, (g + group) * BLK)
-        y = jnp.dot(asel[...], vals[:, at], preferred_element_type=f32)
-        out[:, at] = (y * scale).astype(bf16)
+        cols = slice(g * BLK, (g + group) * BLK)
+        y = jnp.dot(asel[...], vals[:, cols], preferred_element_type=f32)
+        out[:, cols] = (y * scale).astype(bf16)
 
 
 def split(x):
@@ -188,13 +219,22 @@
     return y[:rows] + y[rows:]
 
 
-def scan_kernel(parts, mine, theirs, out):
+def scan_kernel(parts, *refs):
+    *held, out, blocks = refs
     co = lax.axis_index("co")
+    z = lax.axis_index("z")
     n = parts.shape[0]
     steps = parts.shape[2] // BLK
-    even = jnp.where(co == 0, mine[...], theirs[...])
-    odd = jnp.where(co == 0, theirs[...], mine[...])
-    blocks = [(even if t % 2 == 0 else odd)[t // 2] for t in range(steps)]
+    nz = steps // 2
+    h = nz // 2
+    for d in range(h):
+        for j, src in enumerate((held[d], held[h + d]) if d else (held[0],)):
+            back = (co == 0) if j == 0 else (co == 1)
+            k = lax.rem(jnp.where(back, z + nz - d, z + d), nz)
+            blocks[pl.ds(2 * k, 2)] = src[...]
+    k = lax.rem(z + h, nz)
+    blocks[2 * k + co] = held[2 * h][...]
+    blocks[2 * k + 1 - co] = held[2 * h + 1][...]
     force = []
     for t in range(steps):
         at = slice(t * BLK, (t + 1) * BLK)
@@ -235,26 +275,28 @@
     n = cells // BLK
     time = ("z", "co")
 
-    spread, tail, head, piece = call(
+    spread, tail, head, piece, own_blocks = call(
         entry_kernel,
         [
             shape((steps, 16, BLK), f32),
             shape((BLK, half + BLK), bf16),
             shape((BLK, half + BLK), bf16),
             shape((cells // 2, half), bf16),
-        ],
-        [HBM] * 5,
+            shape((NB, BLK, BLK), bf16),
+        ],
+        [HBM] * 6,
         [
             pltpu.VMEM(innovations.shape, f32),
             pltpu.VMEM(obs_cell.shape, i32),
             pltpu.SMEM(tangent_order.shape, i32),
             pltpu.VMEM((2, BLK, half), bf16),
             pltpu.VMEM((2, BLK, BLK), bf16),
-            pltpu.SemaphoreType.DMA((8,)),
+            pltpu.VMEM((NB, BLK, BLK), f32),
+            pltpu.SemaphoreType.DMA((9,)),
         ],
         flops=10**7,
         data=10**6,
-    )(innovations, obs_cell, tangent_order, anomalies, localization)
+    )(innovations, obs_cell, tangent_order, anomalies, localization, tangent_blocks.reshape(NB, BLK, BLK))
 
     upward, downward = [], []
     for c in range(2):
@@ -268,28 +310,45 @@
     down0 = lax.ppermute(head, ("co", "lon", "ens"), downward)
     near = lax.ppermute(piece, "ens", swap)
     recv = lax.all_to_all(spread, time, 0, 0, tiled=True)
-    wt, blocks, traj = call(
-        plan_kernel,
-        [shape((cells, BLK), f32), shape((NB, BLK, BLK), bf16), shape((steps + 1, NB), i32)],
-        [VM, HBM],
-        [
-            pltpu.VMEM((NB, BLK, BLK), f32),
+    oth_blocks = lax.ppermute(own_blocks, "co", swap)
+    count = nz + 1
+    traj, *sends = call(
+        choose_kernel,
+        [shape((steps + 1, NB), i32)] + [shape((2, BLK, BLK), bf16)] * (nz // 2) + [shape((BLK, BLK), bf16)],
+        [HBM, HBM, VM],
+        [
             pltpu.VMEM((steps, BLK), i32),
             pltpu.SMEM((steps, BLK), i32),
-            pltpu.SMEM((8, BLK), i32),
-            pltpu.SemaphoreType.DMA((2,)),
+            pltpu.VMEM((nz // 2 + 1, BLK, BLK), f32),
+            pltpu.SemaphoreType.DMA((count + 1,)),
         ],
         flops=10**6,
         data=10**6,
-        specs=[VM, VM, SM],
-    )(recv, tangent_blocks.reshape(NB, BLK, BLK))
-    mine = lax.all_to_all(blocks, "z", 0, 0, tiled=True)
+        specs=[SM] + [VM] * (nz // 2 + 1),
+    )(tangent_blocks.reshape(NB, BLK, BLK), oth_blocks, recv)
+    got = []
+    for d in range(1, nz // 2):
+        pairs = []
+        for k in range(nz):
+            pairs.append((2 * k, (k + d) % nz * 2))
+            pairs.append((2 * k + 1, (k - d) % nz * 2 + 1))
+        got.append(lax.ppermute(sends[d], time, pairs))
+    last = lax.ppermute(sends[nz // 2], "z", [(k, (k + nz // 2) % nz) for k in range(nz)])
+    crossed = []
+    for g in got + [last]:
+        crossed.append(lax.ppermute(g, "co", swap))
+    held = [sends[0], *got, sends[0], *crossed[:-1], last, crossed[-1]]
 
     up1 = lax.ppermute(up0, "co", swap)
     down1 = lax.ppermute(down0, "co", swap)
-    lt, gown, asel = call(
+    lt, gown, asel, ends = call(
         ready_kernel,
-        [shape((n, BLK, 3 * BLK), bf16), shape((cells, half), bf16), shape((half // 2, cells), bf16)],
+        [
+            shape((n, BLK, 3 * BLK), bf16),
+            shape((cells, half), bf16),
+            shape((half // 2, cells), bf16),
+            shape((2, BLK, half), bf16),
+        ],
         [HBM, HBM, VM, VM, VM, VM],
         [
             pltpu.VMEM(anomalies.shape, bf16),
@@ -304,22 +363,30 @@
     (prod,) = call(
         functools.partial(product_kernel, scale),
         [shape((half // 2, steps * BLK), bf16)],
-        [VM] * 10 + [SM],
+        [VM, VM, HBM, VM, VM, VM, VM],
         [
             pltpu.VMEM((cells + 2 * BLK, half), bf16),
             pltpu.VMEM((cells, COLS), bf16),
             pltpu.VMEM((cells, steps * BLK), bf16),
+            pltpu.VMEM((cells, BLK), WT),
+            pltpu.VMEM((steps, BLK), i32),
+            pltpu.SMEM((steps, BLK), i32),
+            pltpu.SemaphoreType.DMA((3,)),
         ],
         flops=10**9,
         data=4 * 10**6,
         grant=24,
-    )(near, far, up0, up1, down0, down1, lt, gown, asel, wt, traj)
+    )(near, far, ends, lt, gown, asel, recv)
     rows = half // 2 // n_lon
     parts = lax.all_to_all(prod, "lon", 0, 0, tiled=True).reshape(n_lon, rows, steps * BLK)
-    theirs = lax.ppermute(mine, "co", swap)
     (states,) = call(
-        scan_kernel, [shape((steps, 2, rows, BLK), bf16)], [VM] * 3, flops=10**9, data=2 * 10**6
-    )(parts, mine, theirs)
+        scan_kernel,
+        [shape((steps, 2, rows, BLK), bf16)],
+        [VM] * (1 + len(held)),
+        [pltpu.VMEM((steps, BLK, BLK), bf16)],
+        flops=10**9,
+        data=2 * 10**6,
+    )(parts, *held)
     back = lax.all_to_all(states, time, 0, 0, tiled=True)
     x, y = call(place_kernel, [shape((1, 2 * rows, COLS), f32)] * 2, [VM, SM], flops=10**6, data=10**6)(back, traj)
     return x, y

time: 86.5 us -> 100 us (1.16)
  starting transfers between devices: 33 us -> 41 us
  local copies, waits for them, and re-layouts: 0 us -> 7.74 us
  waiting for transfers between devices: 20.2 us -> 17.7 us
  Pallas kernels: 15.4 us -> 16.6 us
    ppermute x1 -> x9, starting transfers between devices: 0.48 us -> 15 us  [the longest x4 6.18 us: on_device(): crossed.append(lax.ppermute(g, 'co', swap))]
    all_to_all x1, waiting for transfers between devices: 13.7 us -> 0.01 us  [on_device(): lax.all_to_all(prod, 'lon', 0, 0, tiled=True)]
    ppermute x1, waiting for transfers between devices: 1.17 us -> 10.6 us  [on_device(): near = lax.ppermute(piece, 'ens', swap)]
    all_to_all x1 -> x0, starting transfers between devices: 7.91 us -> none  [on_device(): mine = lax.all_to_all(blocks, 'z', 0, 0, tiled=True)]
    unnamed x0 -> x24, local copies, waits for them, and re-layouts: none -> 7.74 us
    ppermute x1, waiting for transfers between devices: 0.01 us -> 3.37 us  [on_device(): up0 = lax.ppermute(tail, ('co', 'lon', 'ens'), upward)]
    all_to_all x1 -> x0, waiting for transfers between devices: 2.72 us -> none  [on_device(): mine = lax.all_to_all(blocks, 'z', 0, 0, tiled=True)]
    all_to_all x1, starting transfers between devices: 3.56 us -> 5.69 us  [on_device(): lax.all_to_all(prod, 'lon', 0, 0, tiled=True)]
  transfers between devices with their start and end apart: 10 -> 17, of which waited for: 7 -> 7; matrix products, arithmetic and copies ran while one was open for 0% -> 0% of each run, Pallas kernels for 11% -> 5%
where the time goes in v2:
time: 100 us; the launch traced here: 99.5 us
  starting transfers between devices  41 us (41%)
  waiting for transfers between devices  17.7 us (18%)
  Pallas kernels  16.6 us (17%)
  blocking collectives  15.9 us (16%)
  local copies, waits for them, and re-layouts  7.74 us (8%)
    pallas_call x6, Pallas kernels, run(): return made(*args)  16.6 us
    all_to_all x1, blocking collectives, on_device(): back = lax.all_to_all(states, time, 0, 0, tiled=True)  15.9 us
    ppermute x1, waiting for transfers between devices, on_device(): near = lax.ppermute(piece, 'ens', swap)  10.6 us
    all_to_all x1, starting transfers between devices, on_device(): recv = lax.all_to_all(spread, time, 0, 0, tiled=True)  8.78 us
    unnamed x24, local copies, waits for them, and re-layouts  7.74 us
    ppermute x4, starting transfers between devices, on_device(): crossed.append(lax.ppermute(g, 'co', swap))  6.18 us
    all_to_all x1, starting transfers between devices, on_device(): lax.all_to_all(prod, 'lon', 0, 0, tiled=True)  5.69 us
    ppermute x3, starting transfers between devices, on_device(): got.append(lax.ppermute(sends[d], time, pairs))  5.22 us
  transfers between devices with their start and end apart: 17, of which 7 were waited for; matrix products, arithmetic and copies ran while one was open for 0% of the time, Pallas kernels for 5%

profile of v2, /device:TPU:1, one launch (start us, length us, event | category | flops | bytes accessed | tf_op | source)
XLA Modules:
  0.0 99.5 jit_solution(10774485229437917040)
XLA Ops:
  0.6 2.1 %shard_map.77 = (f32[16,16,128]{2,1,0:T(8,128)}, bf16[128,640]{1,0:T(8,128)(2,1)S(1)}, bf16[128,640]{1,0:T(8,128)(2,1)S(1)}, bf16[512,512]{1,0:T(8,128)(2,1)S(1)}, bf16[8,128,128]{2,1,0:T(8,128)(2,1)S(1)}) custom-call(f32[1,512]{1,0:T(1,128)} %innov.1, s32[1,512]{1,0:T(1,128)} %cell.1, s32[1,8]{1,0:T(1,128)} %order.1, bf16[1024,512]{1,0:T(8,128)(2,1)} %anom.3, ...), custom_call_target="tpu_custom_call" | custom-call | flops 10000000 | bytes 1000000 | tf_op jit(solution)/shard_map/pallas_call | solution.py:39
  2.8 0.0 copy-start.1
  2.8 0.7 copy-done.1
  3.5 3.6 %collective-permute-start = (bf16[512,512]{1,0:T(8,128)(2,1)S(1)}, bf16[512,512]{1,0:T(8,128)(2,1)S(1)}, u32[]{:S(2)}, u32[]{:S(2)}) collective-permute-start(bf16[512,512]{1,0:T(8,128)(2,1)S(1)} %get-tuple-element.17), channel_id=1, source_target_pairs={{0,1},{1,0},{2,3},{3,2},{4,5},{5,4},{6,7},{7,6},{8,9},{9,8},{10,11... | collective-permute-start | bytes 1572872 | tf_op jit(solution)/shard_map/ppermute | solution.py:311
  7.0 10.6 %collective-permute-done.near = bf16[512,512]{1,0:T(8,128)(2,1)S(1)} collective-permute-done((bf16[512,512]{1,0:T(8,128)(2,1)S(1)}, bf16[512,512]{1,0:T(8,128)(2,1)S(1)}, u32[]{:S(2)}, u32[]{:S(2)}) %collective-permute-start) | collective-permute-done | bytes 524320 | tf_op jit(solution)/shard_map/ppermute | solution.py:311
  17.6 2.3 %collective-permute-start.1 = (bf16[512,512]{1,0:T(8,128)(2,1)S(1)}, bf16[512,512]{1,0:T(8,128)(2,1)S(1)}, u32[]{:S(2)}, u32[]{:S(2)}) collective-permute-start(bf16[512,512]{1,0:T(8,128)(2,1)S(1)} %collective-permute-done.near), channel_id=1, source_target_pairs={{0,16},{16,0},{1,17},{17,1},{2,18},{18,2},{3,19},{19,3},{4,20},{20... | collective-permute-start | bytes 1572872 | tf_op jit(solution)/shard_map/ppermute | solution.py:362
  19.9 2.7 %collective-permute-start.2 = (bf16[128,640]{1,0:T(8,128)(2,1)S(1)}, bf16[128,640]{1,0:T(8,128)(2,1)S(1)}, u32[]{:S(2)}, u32[]{:S(2)}) collective-permute-start(bf16[128,640]{1,0:T(8,128)(2,1)S(1)} %get-tuple-element.18), channel_id=1, source_target_pairs={{0,2},{1,3},{2,4},{3,5},{4,6},{5,7},{6,8},{7,9},{8,10},{9,11},{10,... | collective-permute-start | bytes 491528 | tf_op jit(solution)/shard_map/ppermute | solution.py:309
  22.6 2.5 %collective-permute-start.4 = (bf16[128,640]{1,0:T(8,128)(2,1)S(1)}, bf16[128,640]{1,0:T(8,128)(2,1)S(1)}, u32[]{:S(2)}, u32[]{:S(2)}) collective-permute-start(bf16[128,640]{1,0:T(8,128)(2,1)S(1)} %get-tuple-element.19), channel_id=1, source_target_pairs={{2,0},{3,1},{4,2},{5,3},{6,4},{7,5},{8,6},{9,7},{10,8},{11,9},{12,... | collective-permute-start | bytes 491528 | tf_op jit(solution)/shard_map/ppermute | solution.py:310
  25.1 3.4 %collective-permute-done.2.up0 = bf16[128,640]{1,0:T(8,128)(2,1)S(1)} collective-permute-done((bf16[128,640]{1,0:T(8,128)(2,1)S(1)}, bf16[128,640]{1,0:T(8,128)(2,1)S(1)}, u32[]{:S(2)}, u32[]{:S(2)}) %collective-permute-start.2) | collective-permute-done | bytes 163872 | tf_op jit(solution)/shard_map/ppermute | solution.py:309
  28.4 0.0 collective-permute-start.3
  28.4 0.0 collective-permute-done.4.down0
  28.4 0.5 collective-permute-start.5
  29.0 0.7 copy-done.5
  29.6 8.8 %all-to-all-start = ((f32[16,16,128]{2,1,0:T(8,128)}), f32[16,16,128]{2,1,0:T(8,128)S(1)}, u32[]{:S(2)}, u32[]{:S(2)}) async-start(f32[16,16,128]{2,1,0:T(8,128)} %get-tuple-element.24), calls=%async_computation | async-start | bytes 262144 | tf_op jit(solution)/shard_map/all_to_all | solution.py:312
  38.4 0.6 copy-done.7
  39.1 0.7 copy-done.9
  39.7 0.9 copy-done.4
  40.7 0.9 copy-done.6
  41.6 0.9 copy-done.8
  42.5 0.9 copy-done.10
  43.4 2.2 %shard_map.78 = (bf16[8,128,384]{2,1,0:T(8,128)(2,1)S(1)}, bf16[1024,512]{1,0:T(8,128)(2,1)S(1)}, bf16[256,1024]{1,0:T(8,128)(2,1)S(1)}, bf16[2,128,512]{2,1,0:T(8,128)(2,1)S(1)}) custom-call(bf16[1024,512]{1,0:T(8,128)(2,1)} %anom.3, bf16[8,3,128,128]{3,2,1,0:T(8,128)(2,1)} %loc.3, bf16[128,640]{1,0:T(8,128)(2,1)S(1)} %copy-done.4, ...), custom_call_target="tpu_custom_call" | custom-call | flops 1000000000 | bytes 4000000 | tf_op jit(solution)/shard_map/pallas_call | solution.py:39
  45.6 0.0 copy-start
  45.6 0.7 copy-done
  46.3 1.0 all-to-all-done.recv
  47.3 5.7 %shard_map.79 = bf16[256,2048]{1,0:T(8,128)(2,1)} custom-call(bf16[512,512]{1,0:T(8,128)(2,1)S(1)} %collective-permute-done.near, bf16[512,512]{1,0:T(8,128)(2,1)S(1)} %collective-permute-done.1.far, bf16[2,128,512]{2,1,0:T(8,128)(2,1)} %copy-done, bf16[8,128,384]{2,1,0:T(8,128)(2,1)S(1)} %get-tuple-element.21.lt, ...), custom_call_target="tpu_custom_call" | custom-call | flops 1000000000 | bytes 4000000 | tf_op jit(solution)/shard_map/pallas_call | solution.py:39
  53.0 0.0 copy-start.2
  53.0 5.7 %all-to-all-start.1 = ((bf16[8,32,2048]{2,1,0:T(8,128)(2,1)}), bf16[8,32,2048]{2,1,0:T(8,128)(2,1)S(1)}, u32[]{:S(2)}, u32[]{:S(2)}) async-start(bf16[8,32,2048]{2,1,0:T(8,128)(2,1)} %bitcast.1), calls=%async_computation.1 | async-start | bytes 2097152 | tf_op jit(solution)/shard_map/all_to_all | solution.py:381
  58.7 0.2 collective-permute-start.6
  59.0 1.4 %collective-permute-done.6.oth = bf16[8,128,128]{2,1,0:T(8,128)(2,1)S(1)} collective-permute-done((bf16[8,128,128]{2,1,0:T(8,128)(2,1)S(1)}, bf16[8,128,128]{2,1,0:T(8,128)(2,1)S(1)}, u32[]{:S(2)}, u32[]{:S(2)}) %collective-permute-start.6) | collective-permute-done | bytes 262176 | tf_op jit(solution)/shard_map/ppermute | solution.py:313
  60.3 0.7 copy-done.11
  61.0 2.9 %shard_map.80 = (s32[17,8]{1,0:T(8,128)S(1)}, bf16[2,128,128]{2,1,0:T(8,128)(2,1)S(1)}, bf16[2,128,128]{2,1,0:T(8,128)(2,1)S(1)}, bf16[2,128,128]{2,1,0:T(8,128)...) custom-call(f32[8,128,128]{2,1,0:T(8,128)} %bitcast.3, bf16[8,128,128]{2,1,0:T(8,128)(2,1)} %copy-done.11, ...), custom_call_target="tpu_custom_call" | custom-call | flops 1000000 | bytes 1000000 | tf_op jit(solution)/shard_map/pallas_call | solution.py:39
  63.9 2.0 %collective-permute-start.7 = (bf16[2,128,128]{2,1,0:T(8,128)(2,1)S(1)}, bf16[2,128,128]{2,1,0:T(8,128)(2,1)S(1)}, u32[]{:S(2)}, u32[]{:S(2)}) collective-permute-start(bf16[2,128,128]{2,1,0:T(8,128)(2,1)S(1)} %get-tuple-element.27), channel_id=1, source_target_pairs={{0,32},{16,240},{32,64},{48,16},{64,96},{80,48},{96,128},{112,80},... | collective-permute-start | bytes 196616 | tf_op jit(solution)/shard_map/ppermute | solution.py:335
  65.9 2.0 %collective-permute-start.8 = (bf16[2,128,128]{2,1,0:T(8,128)(2,1)S(1)}, bf16[2,128,128]{2,1,0:T(8,128)(2,1)S(1)}, u32[]{:S(2)}, u32[]{:S(2)}) collective-permute-start(bf16[2,128,128]{2,1,0:T(8,128)(2,1)S(1)} %get-tuple-element.28), channel_id=1, source_target_pairs={{0,64},{16,208},{32,96},{48,240},{64,128},{80,16},{96,160},{112,48... | collective-permute-start | bytes 196616 | tf_op jit(solution)/shard_map/ppermute | solution.py:335
  68.0 1.2 %collective-permute-start.9 = (bf16[2,128,128]{2,1,0:T(8,128)(2,1)S(1)}, bf16[2,128,128]{2,1,0:T(8,128)(2,1)S(1)}, u32[]{:S(2)}, u32[]{:S(2)}) collective-permute-start(bf16[2,128,128]{2,1,0:T(8,128)(2,1)S(1)} %get-tuple-element.29), channel_id=1, source_target_pairs={{0,96},{16,176},{32,128},{48,208},{64,160},{80,240},{96,192},{112,... | collective-permute-start | bytes 196616 | tf_op jit(solution)/shard_map/ppermute | solution.py:335
  69.1 3.4 %collective-permute-start.13 = (bf16[128,128]{1,0:T(8,128)(2,1)S(1)}, bf16[128,128]{1,0:T(8,128)(2,1)S(1)}, u32[]{:S(2)}, u32[]{:S(2)}) collective-permute-start(bf16[128,128]{1,0:T(8,128)(2,1)S(1)} %get-tuple-element.30), channel_id=1, source_target_pairs={{0,128},{32,160},{64,192},{96,224},{128,0},{160,32},{192,64},{224,... | collective-permute-start | bytes 98312 | tf_op jit(solution)/shard_map/ppermute | solution.py:336
  72.5 0.0 collective-permute-done.7.refs_1_
  72.5 0.2 collective-permute-start.10
  72.7 0.3 collective-permute-start.11
  73.0 0.2 collective-permute-done.9.refs_3_
  73.2 2.7 %collective-permute-start.12 = (bf16[2,128,128]{2,1,0:T(8,128)(2,1)S(1)}, bf16[2,128,128]{2,1,0:T(8,128)(2,1)S(1)}, u32[]{:S(2)}, u32[]{:S(2)}) collective-permute-start(bf16[2,128,128]{2,1,0:T(8,128)(2,1)S(1)} %collective-permute-done.9.refs_3_), channel_id=1, source_target_pairs={{0,16},{16,0},{1,17},{17,1},{2,18},{18,2},{3,19},{19,3},{4,20},{20... | collective-permute-start | bytes 196616 | tf_op jit(solution)/shard_map/ppermute | solution.py:339
  75.8 0.3 collective-permute-done.13.refs_8_
  76.1 3.0 %collective-permute-start.14 = (bf16[128,128]{1,0:T(8,128)(2,1)S(1)}, bf16[128,128]{1,0:T(8,128)(2,1)S(1)}, u32[]{:S(2)}, u32[]{:S(2)}) collective-permute-start(bf16[128,128]{1,0:T(8,128)(2,1)S(1)} %collective-permute-done.13.refs_8_), channel_id=1, source_target_pairs={{0,16},{16,0},{1,17},{17,1},{2,18},{18,2},{3,19},{19,3},{4,20},{20... | collective-permute-start | bytes 98312 | tf_op jit(solution)/shard_map/ppermute | solution.py:339
  79.1 0.9 collective-permute-done.14.refs_9_
  80.0 0.0 collective-permute-done.11.refs_6_
  80.0 0.0 collective-permute-done.12.refs_7_
  80.0 2.0 %shard_map.81 = bf16[16,2,32,128]{3,2,1,0:T(8,128)(2,1)S(1)} custom-call(bf16[8,32,2048]{2,1,0:T(8,128)(2,1)S(1)} %all-to-all-done.1.parts, bf16[2,128,128]{2,1,0:T(8,128)(2,1)S(1)} %get-tuple-element.26.refs_0_.refs_4_, bf16[2,128,128]{2,1,0:T(8,128)(2,1)S(1)} %collective-permute-done.7.refs_1_, bf16[2,128,128]{2,1,0:T(8,128)(2,1)S(1)} %collective-permute-done.8.refs_2_, ...), custom_call_target="tpu_custom_call" | custom-call | flops 1000000000 | bytes 2000000 | tf_op jit(solution)/shard_map/pallas_call | solution.py:39
  82.0 15.9 %all_to_all.19.recv = bf16[16,2,32,128]{3,2,1,0:T(8,128)(2,1)S(1)} all-to-all(bf16[16,2,32,128]{3,2,1,0:T(8,128)(2,1)S(1)} %shard_map.81), channel_id=1, replica_groups=mesh['z'=8,'co'=2,'lon'=8,'ens'=2] {'z','co'}, dimensions={0} | all-to-all | bytes 524288 | tf_op jit(solution)/shard_map/all_to_all | solution.py:390
  97.9 1.6 %shard_map.82 = (f32[1,64,1024]{2,1,0:T(8,128)}, f32[1,64,1024]{2,1,0:T(8,128)}) custom-call(bf16[16,2,32,128]{3,2,1,0:T(8,128)(2,1)S(1)} %all_to_all.19.recv, s32[17,8]{1,0:T(8,128)S(1)} %get-tuple-element.31.traj), custom_call_target="tpu_custom_call" | custom-call | flops 1000000 | bytes 1000000 | tf_op jit(solution)/shard_map/pallas_call | solution.py:39
  (17 shorter events, 0.0 us)
Async XLA Ops:
  2.8 0.7 copy-start.1
  3.5 14.2 %collective-permute-start = (bf16[512,512]{1,0:T(8,128)(2,1)S(1)}, bf16[512,512]{1,0:T(8,128)(2,1)S(1)}, u32[]{:S(2)}, u32[]{:S(2)}) collective-permute-start(bf16[512,512]{1,0:T(8,128)(2,1)S(1)} %get-tuple-element.17), channel_id=1, source_target_pairs={{0,1},{1,0},{2,3},{3,2},{4,5},{5,4},{6,7},{7,6},{8,9},{9,8},{10,11... | collective-permute-start | bytes 1572872 | tf_op jit(solution)/shard_map/ppermute | solution.py:311
  17.6 29.6 %collective-permute-start.1 = (bf16[512,512]{1,0:T(8,128)(2,1)S(1)}, bf16[512,512]{1,0:T(8,128)(2,1)S(1)}, u32[]{:S(2)}, u32[]{:S(2)}) collective-permute-start(bf16[512,512]{1,0:T(8,128)(2,1)S(1)} %collective-permute-done.near), channel_id=1, source_target_pairs={{0,16},{16,0},{1,17},{17,1},{2,18},{18,2},{3,19},{19,3},{4,20},{20... | collective-permute-start | bytes 1572872 | tf_op jit(solution)/shard_map/ppermute | solution.py:362
  19.9 8.5 %collective-permute-start.2 = (bf16[128,640]{1,0:T(8,128)(2,1)S(1)}, bf16[128,640]{1,0:T(8,128)(2,1)S(1)}, u32[]{:S(2)}, u32[]{:S(2)}) collective-permute-start(bf16[128,640]{1,0:T(8,128)(2,1)S(1)} %get-tuple-element.18), channel_id=1, source_target_pairs={{0,2},{1,3},{2,4},{3,5},{4,6},{5,7},{6,8},{7,9},{8,10},{9,11},{10,... | collective-permute-start | bytes 491528 | tf_op jit(solution)/shard_map/ppermute | solution.py:309
  22.6 5.8 %collective-permute-start.4 = (bf16[128,640]{1,0:T(8,128)(2,1)S(1)}, bf16[128,640]{1,0:T(8,128)(2,1)S(1)}, u32[]{:S(2)}, u32[]{:S(2)}) collective-permute-start(bf16[128,640]{1,0:T(8,128)(2,1)S(1)} %get-tuple-element.19), channel_id=1, source_target_pairs={{2,0},{3,1},{4,2},{5,3},{6,4},{7,5},{8,6},{9,7},{10,8},{11,9},{12,... | collective-permute-start | bytes 491528 | tf_op jit(solution)/shard_map/ppermute | solution.py:310
  28.4 10.0 %copy-start.3 = (bf16[128,640]{1,0:T(8,128)(2,1)}, bf16[128,640]{1,0:T(8,128)(2,1)S(1)}, u32[]{:S(2)}) copy-start(bf16[128,640]{1,0:T(8,128)(2,1)S(1)} %collective-permute-done.2.up0) | copy-start | bytes 491524
  28.4 10.0 %collective-permute-start.3 = (bf16[128,640]{1,0:T(8,128)(2,1)S(1)}, bf16[128,640]{1,0:T(8,128)(2,1)S(1)}, u32[]{:S(2)}, u32[]{:S(2)}) collective-permute-start(bf16[128,640]{1,0:T(8,128)(2,1)S(1)} %collective-permute-done.2.up0), channel_id=1, source_target_pairs={{0,16},{16,0},{1,17},{17,1},{2,18},{18,2},{3,19},{19,3},{4,20},{20... | collective-permute-start | bytes 491528 | tf_op jit(solution)/shard_map/ppermute | solution.py:342
  28.4 10.6 %collective-permute-start.5 = (bf16[128,640]{1,0:T(8,128)(2,1)S(1)}, bf16[128,640]{1,0:T(8,128)(2,1)S(1)}, u32[]{:S(2)}, u32[]{:S(2)}) collective-permute-start(bf16[128,640]{1,0:T(8,128)(2,1)S(1)} %collective-permute-done.4.down0), channel_id=1, source_target_pairs={{0,16},{16,0},{1,17},{17,1},{2,18},{18,2},{3,19},{19,3},{4,20},{20... | collective-permute-start | bytes 491528 | tf_op jit(solution)/shard_map/ppermute | solution.py:343
  29.0 0.7 copy-start.5
  29.6 17.7 %all-to-all-start = ((f32[16,16,128]{2,1,0:T(8,128)}), f32[16,16,128]{2,1,0:T(8,128)S(1)}, u32[]{:S(2)}, u32[]{:S(2)}) async-start(f32[16,16,128]{2,1,0:T(8,128)} %get-tuple-element.24), calls=%async_computation | async-start | bytes 262144 | tf_op jit(solution)/shard_map/all_to_all | solution.py:312
  38.4 0.7 copy-start.7
  39.1 0.7 copy-start.9
  39.7 0.9 copy-start.4
  40.7 0.9 copy-start.6
  41.6 0.9 copy-start.8
  42.5 0.9 copy-start.10
  45.6 0.7 copy-start
  53.0 5.7 %copy-start.2 = (bf16[8,128,128]{2,1,0:T(8,128)(2,1)S(1)}, bf16[8,128,128]{2,1,0:T(8,128)(2,1)}, u32[]{:S(2)}) copy-start(bf16[8,128,128]{2,1,0:T(8,128)(2,1)} %copy-done.1) | copy-start | bytes 786436
  53.0 27.0 %all-to-all-start.1 = ((bf16[8,32,2048]{2,1,0:T(8,128)(2,1)}), bf16[8,32,2048]{2,1,0:T(8,128)(2,1)S(1)}, u32[]{:S(2)}, u32[]{:S(2)}) async-start(bf16[8,32,2048]{2,1,0:T(8,128)(2,1)} %bitcast.1), calls=%async_computation.1 | async-start | bytes 2097152 | tf_op jit(solution)/shard_map/all_to_all | solution.py:381
  58.7 1.6 %collective-permute-start.6 = (bf16[8,128,128]{2,1,0:T(8,128)(2,1)S(1)}, bf16[8,128,128]{2,1,0:T(8,128)(2,1)S(1)}, u32[]{:S(2)}, u32[]{:S(2)}) collective-permute-start(bf16[8,128,128]{2,1,0:T(8,128)(2,1)S(1)} %copy-done.2), channel_id=1, source_target_pairs={{0,16},{16,0},{1,17},{17,1},{2,18},{18,2},{3,19},{19,3},{4,20},{20... | collective-permute-start | bytes 786440 | tf_op jit(solution)/shard_map/ppermute | solution.py:313
  60.3 0.7 copy-start.11
  63.9 8.6 %collective-permute-start.7 = (bf16[2,128,128]{2,1,0:T(8,128)(2,1)S(1)}, bf16[2,128,128]{2,1,0:T(8,128)(2,1)S(1)}, u32[]{:S(2)}, u32[]{:S(2)}) collective-permute-start(bf16[2,128,128]{2,1,0:T(8,128)(2,1)S(1)} %get-tuple-element.27), channel_id=1, source_target_pairs={{0,32},{16,240},{32,64},{48,16},{64,96},{80,48},{96,128},{112,80},... | collective-permute-start | bytes 196616 | tf_op jit(solution)/shard_map/ppermute | solution.py:335
  65.9 6.8 %collective-permute-start.8 = (bf16[2,128,128]{2,1,0:T(8,128)(2,1)S(1)}, bf16[2,128,128]{2,1,0:T(8,128)(2,1)S(1)}, u32[]{:S(2)}, u32[]{:S(2)}) collective-permute-start(bf16[2,128,128]{2,1,0:T(8,128)(2,1)S(1)} %get-tuple-element.28), channel_id=1, source_target_pairs={{0,64},{16,208},{32,96},{48,240},{64,128},{80,16},{96,160},{112,48... | collective-permute-start | bytes 196616 | tf_op jit(solution)/shard_map/ppermute | solution.py:335
  68.0 5.2 %collective-permute-start.9 = (bf16[2,128,128]{2,1,0:T(8,128)(2,1)S(1)}, bf16[2,128,128]{2,1,0:T(8,128)(2,1)S(1)}, u32[]{:S(2)}, u32[]{:S(2)}) collective-permute-start(bf16[2,128,128]{2,1,0:T(8,128)(2,1)S(1)} %get-tuple-element.29), channel_id=1, source_target_pairs={{0,96},{16,176},{32,128},{48,208},{64,160},{80,240},{96,192},{112,... | collective-permute-start | bytes 196616 | tf_op jit(solution)/shard_map/ppermute | solution.py:335
  69.1 7.0 %collective-permute-start.13 = (bf16[128,128]{1,0:T(8,128)(2,1)S(1)}, bf16[128,128]{1,0:T(8,128)(2,1)S(1)}, u32[]{:S(2)}, u32[]{:S(2)}) collective-permute-start(bf16[128,128]{1,0:T(8,128)(2,1)S(1)} %get-tuple-element.30), channel_id=1, source_target_pairs={{0,128},{32,160},{64,192},{96,224},{128,0},{160,32},{192,64},{224,... | collective-permute-start | bytes 98312 | tf_op jit(solution)/shard_map/ppermute | solution.py:336
  72.5 7.5 %collective-permute-start.10 = (bf16[2,128,128]{2,1,0:T(8,128)(2,1)S(1)}, bf16[2,128,128]{2,1,0:T(8,128)(2,1)S(1)}, u32[]{:S(2)}, u32[]{:S(2)}) collective-permute-start(bf16[2,128,128]{2,1,0:T(8,128)(2,1)S(1)} %collective-permute-done.7.refs_1_), channel_id=1, source_target_pairs={{0,16},{16,0},{1,17},{17,1},{2,18},{18,2},{3,19},{19,3},{4,20},{20... | collective-permute-start | bytes 196616 | tf_op jit(solution)/shard_map/ppermute | solution.py:339
  72.7 7.3 %collective-permute-start.11 = (bf16[2,128,128]{2,1,0:T(8,128)(2,1)S(1)}, bf16[2,128,128]{2,1,0:T(8,128)(2,1)S(1)}, u32[]{:S(2)}, u32[]{:S(2)}) collective-permute-start(bf16[2,128,128]{2,1,0:T(8,128)(2,1)S(1)} %collective-permute-done.8.refs_2_), channel_id=1, source_target_pairs={{0,16},{16,0},{1,17},{17,1},{2,18},{18,2},{3,19},{19,3},{4,20},{20... | collective-permute-start | bytes 196616 | tf_op jit(solution)/shard_map/ppermute | solution.py:339
  73.2 6.8 %collective-permute-start.12 = (bf16[2,128,128]{2,1,0:T(8,128)(2,1)S(1)}, bf16[2,128,128]{2,1,0:T(8,128)(2,1)S(1)}, u32[]{:S(2)}, u32[]{:S(2)}) collective-permute-start(bf16[2,128,128]{2,1,0:T(8,128)(2,1)S(1)} %collective-permute-done.9.refs_3_), channel_id=1, source_target_pairs={{0,16},{16,0},{1,17},{17,1},{2,18},{18,2},{3,19},{19,3},{4,20},{20... | collective-permute-start | bytes 196616 | tf_op jit(solution)/shard_map/ppermute | solution.py:339
  76.1 3.9 %collective-permute-start.14 = (bf16[128,128]{1,0:T(8,128)(2,1)S(1)}, bf16[128,128]{1,0:T(8,128)(2,1)S(1)}, u32[]{:S(2)}, u32[]{:S(2)}) collective-permute-start(bf16[128,128]{1,0:T(8,128)(2,1)S(1)} %collective-permute-done.13.refs_8_), channel_id=1, source_target_pairs={{0,16},{16,0},{1,17},{17,1},{2,18},{18,2},{3,19},{19,3},{4,20},{20... | collective-permute-start | bytes 98312 | tf_op jit(solution)/shard_map/ppermute | solution.py:339

commit v3 on v2

--- a/solution.py
+++ b/solution.py
@@ -19,7 +19,6 @@
 SM = pl.BlockSpec(memory_space=pltpu.SMEM)
 HBM = pl.BlockSpec(memory_space=pltpu.HBM)
 MIB = 1024 * 1024
-WT = f32
 NT = (((1,), (1,)), ((), ()))
 
 
@@ -115,12 +114,13 @@
     d = pltpu.make_async_copy(ints, order_s, sem.at[0])
     d.start()
     d.wait()
+    at = [jnp.int32(q) for q in range(NB)]
+    for t in range(steps - 1, -1, -1):
+        for q in range(NB):
+            traj[t + 1, q] = at[q]
+        at = [order_s[t, b] for b in at]
     for q in range(NB):
-        b = jnp.int32(q)
-        for t in range(steps - 1, -1, -1):
-            traj[t + 1, q] = b
-            b = order_s[t, b]
-        traj[0, q] = b
+        traj[0, q] = at[q]
     copies = []
     for d, out in enumerate(outs):
         q = lax.rem(jnp.where(co == 0, z + d, z + nz - d), nz)
@@ -136,11 +136,16 @@
             out[...] = picked[d].astype(bf16)
 
 
-def ready_kernel(anom, loc, up0, up1, down0, down1, lt, gown, asel, ends, anom_v, loc_v, pad, sem):
+def ready_kernel(anom, loc, *refs):
+    *edges, lt, gown, asel, ends, anom_v, loc_v, edge_v, pad, sem = refs
     co = lax.axis_index("co")
-    copies = copies_of(((loc, loc_v), (anom, anom_v)), sem)
+    pairs = [(a, edge_v.at[i]) for i, a in enumerate(edges)]
+    copies = copies_of(((loc, loc_v), (anom, anom_v), *pairs), sem)
     n = loc.shape[0]
     half = anom.shape[1]
+    for c in copies[2:]:
+        c.wait()
+    up0, up1, down0, down1 = (edge_v.at[i] for i in range(4))
     before = jnp.where(co == 0, up0[:, :half], up1[:, :half])
     after = jnp.where(co == 0, down0[:, :half], down1[:, :half])
     ends[0] = jnp.where(co == 0, up1[:, :half], up0[:, :half])
@@ -162,7 +167,9 @@
         asel[k * 32 : (k + 1) * 32] = jnp.where(co == 0, at[k * 64 : k * 64 + 32], at[k * 64 + 32 : (k + 1) * 64])
 
 
-def product_kernel(scale, near, far, ends, lt, gown, asel, recv, out, pad, full, vals, wt, ints, order_s, sem):
+def product_kernel(
+    scale, near, far, ends, lt, gown, asel, recv, out, pad, full, vals, wt, res, ints, order_s, sem, out_sem
+):
     co = lax.axis_index("co")
     e = lax.axis_index("ens")
     z = lax.axis_index("z")
@@ -171,39 +178,47 @@
         ints[k : k + 1] = recv[k, 8:9, :].astype(i32)
     h, half = near.shape
     n = lt.shape[0]
-    d, up, down = copies_of(
+    there = pl.ds(pl.multiple_of((1 - e) * half, half), half)
+    copies = copies_of(
         (
+            (near, pad.at[pl.ds(pl.multiple_of(BLK + co * h, BLK), h)]),
+            (far, pad.at[pl.ds(pl.multiple_of(BLK + (1 - co) * h, BLK), h)]),
             (ints, order_s),
-            (ends.at[0], pad.at[pl.ds(0, BLK)]),
-            (ends.at[1], pad.at[pl.ds(BLK + n * BLK, BLK)]),
+            (gown, full.at[:, pl.ds(pl.multiple_of(e * half, half), half)]),
         ),
         sem,
     )
-    pad[pl.ds(pl.multiple_of(BLK + co * h, BLK), h)] = near[...]
-    pad[pl.ds(pl.multiple_of(BLK + (1 - co) * h, BLK), h)] = far[...]
-    there = pl.ds(pl.multiple_of((1 - e) * half, half), half)
-    full[:, pl.ds(pl.multiple_of(e * half, half), half)] = gown[...]
     blank = jnp.zeros((BLK - steps, BLK), f32)
-    up.wait()
-    down.wait()
+    for b in range(n):
+        wt[b * BLK : (b + 1) * BLK] = jnp.concatenate([recv[:, b, :], blank], axis=0).T
+    pad[:BLK] = ends[0]
+    pad[BLK + n * BLK :] = ends[1]
+    copies[0].wait()
+    copies[1].wait()
     for b in range(n):
         y = jnp.dot(lt[b], pad[b * BLK : (b + 3) * BLK], preferred_element_type=f32)
         full[b * BLK : (b + 1) * BLK, there] = y.astype(bf16)
-        wt[b * BLK : (b + 1) * BLK] = jnp.concatenate([recv[:, b, :], blank], axis=0).T.astype(wt.dtype)
-    d.wait()
+    copies[2].wait()
+    copies[3].wait()
     at = [None] * steps
     b = z
     for t in range(steps - 1, -1, -1):
         at[t] = cols_at(b)
         b = order_s[t, b]
     group = 4
+    sent = []
     for g in range(0, steps, group):
         for t in range(g, g + group):
-            y = wt[:, t : t + 1] * full[:, at[t]].astype(wt.dtype)
+            y = wt[:, t : t + 1] * full[:, at[t]].astype(f32)
             vals[:, t * BLK : (t + 1) * BLK] = y.astype(bf16)
         cols = slice(g * BLK, (g + group) * BLK)
         y = jnp.dot(asel[...], vals[:, cols], preferred_element_type=f32)
-        out[:, cols] = (y * scale).astype(bf16)
+        res[:, cols] = (y * scale).astype(bf16)
+        c = pltpu.make_async_copy(res.at[:, cols], out.at[:, cols], out_sem.at[g // group])
+        c.start()
+        sent.append(c)
+    for c in sent:
+        c.wait()
 
 
 def split(x):
@@ -349,12 +364,13 @@
             shape((half // 2, cells), bf16),
             shape((2, BLK, half), bf16),
         ],
-        [HBM, HBM, VM, VM, VM, VM],
+        [HBM] * 6,
         [
             pltpu.VMEM(anomalies.shape, bf16),
             pltpu.VMEM(localization.shape, bf16),
+            pltpu.VMEM((4, BLK, half + BLK), bf16),
             pltpu.VMEM((cells + 2 * BLK, half), bf16),
-            pltpu.SemaphoreType.DMA((2,)),
+            pltpu.SemaphoreType.DMA((6,)),
         ],
         flops=10**9,
         data=4 * 10**6,
@@ -363,19 +379,22 @@
     (prod,) = call(
         functools.partial(product_kernel, scale),
         [shape((half // 2, steps * BLK), bf16)],
-        [VM, VM, HBM, VM, VM, VM, VM],
+        [HBM, HBM, VM, VM, VM, VM, VM],
         [
             pltpu.VMEM((cells + 2 * BLK, half), bf16),
             pltpu.VMEM((cells, COLS), bf16),
             pltpu.VMEM((cells, steps * BLK), bf16),
-            pltpu.VMEM((cells, BLK), WT),
+            pltpu.VMEM((cells, BLK), f32),
+            pltpu.VMEM((half // 2, steps * BLK), bf16),
             pltpu.VMEM((steps, BLK), i32),
             pltpu.SMEM((steps, BLK), i32),
-            pltpu.SemaphoreType.DMA((3,)),
+            pltpu.SemaphoreType.DMA((4,)),
+            pltpu.SemaphoreType.DMA((4,)),
         ],
         flops=10**9,
         data=4 * 10**6,
         grant=24,
+        specs=[HBM],
     )(near, far, ends, lt, gown, asel, recv)
     rows = half // 2 // n_lon
     parts = lax.all_to_all(prod, "lon", 0, 0, tiled=True).reshape(n_lon, rows, steps * BLK)

time: 100 us -> 96.4 us (0.964)
  waiting for transfers between devices: 17.7 us -> 24.6 us
  local copies, waits for them, and re-layouts: 7.74 us -> 1.37 us
  starting transfers between devices: 41 us -> 36.9 us
    unnamed x24 -> x10, local copies, waits for them, and re-layouts: 7.74 us -> 1.37 us
    all_to_all x1, waiting for transfers between devices: 0.96 us -> 5.5 us  [on_device(): recv = lax.all_to_all(spread, time, 0, 0, tiled=True)]
    ppermute x1, waiting for transfers between devices: 0.28 us -> 2.8 us  [on_device(): lax.ppermute(sends[nz // 2], 'z', [(k, (k + nz // 2) % nz) for k in range...]
    ppermute x4, starting transfers between devices: 6.18 us -> 4.31 us  [on_device(): crossed.append(lax.ppermute(g, 'co', swap))]
    ppermute x3, starting transfers between devices: 5.22 us -> 4.07 us  [on_device(): got.append(lax.ppermute(sends[d], time, pairs))]
  transfers between devices with their start and end apart: 17 -> 17, of which waited for: 7 -> 6; matrix products, arithmetic and copies ran while one was open for 0% -> 0% of each run, Pallas kernels for 5% -> 6%
where the time goes in v3:
time: 96.4 us; the launch traced here: 96 us
  starting transfers between devices  36.9 us (38%)
  waiting for transfers between devices  24.6 us (26%)
  Pallas kernels  17 us (18%)
  blocking collectives  15.5 us (16%)
  local copies, waits for them, and re-layouts  1.37 us (1%)
    pallas_call x6, Pallas kernels, run(): return made(*args)  17 us
    all_to_all x1, blocking collectives, on_device(): back = lax.all_to_all(states, time, 0, 0, tiled=True)  15.5 us
    ppermute x1, waiting for transfers between devices, on_device(): near = lax.ppermute(piece, 'ens', swap)  10.6 us
    all_to_all x1, starting transfers between devices, on_device(): recv = lax.all_to_all(spread, time, 0, 0, tiled=True)  8.78 us
    all_to_all x1, starting transfers between devices, on_device(): lax.all_to_all(prod, 'lon', 0, 0, tiled=True)  5.56 us
    all_to_all x1, waiting for transfers between devices, on_device(): recv = lax.all_to_all(spread, time, 0, 0, tiled=True)  5.5 us
    ppermute x4, starting transfers between devices, on_device(): crossed.append(lax.ppermute(g, 'co', swap))  4.31 us
    ppermute x3, starting transfers between devices, on_device(): got.append(lax.ppermute(sends[d], time, pairs))  4.07 us
  transfers between devices with their start and end apart: 17, of which 6 were waited for; matrix products, arithmetic and copies ran while one was open for 0% of the time, Pallas kernels for 6%

profile of v3, /device:TPU:1, one launch (start us, length us, event | category | flops | bytes accessed | tf_op | source)
XLA Modules:
  0.0 96.0 jit_solution(12089495322404343274)
XLA Ops:
  0.6 2.1 %shard_map.77 = (f32[16,16,128]{2,1,0:T(8,128)}, bf16[128,640]{1,0:T(8,128)(2,1)S(1)}, bf16[128,640]{1,0:T(8,128)(2,1)S(1)}, bf16[512,512]{1,0:T(8,128)(2,1)S(1)}, bf16[8,128,128]{2,1,0:T(8,128)(2,1)S(1)}) custom-call(f32[1,512]{1,0:T(1,128)} %innov.1, s32[1,512]{1,0:T(1,128)} %cell.1, s32[1,8]{1,0:T(1,128)} %order.1, bf16[1024,512]{1,0:T(8,128)(2,1)} %anom.3, ...), custom_call_target="tpu_custom_call" | custom-call | flops 10000000 | bytes 1000000 | tf_op jit(solution)/shard_map/pallas_call | solution.py:38
  2.8 3.6 %collective-permute-start = (bf16[512,512]{1,0:T(8,128)(2,1)S(1)}, bf16[512,512]{1,0:T(8,128)(2,1)S(1)}, u32[]{:S(2)}, u32[]{:S(2)}) collective-permute-start(bf16[512,512]{1,0:T(8,128)(2,1)S(1)} %get-tuple-element.17), channel_id=1, source_target_pairs={{0,1},{1,0},{2,3},{3,2},{4,5},{5,4},{6,7},{7,6},{8,9},{9,8},{10,11... | collective-permute-start | bytes 1572872 | tf_op jit(solution)/shard_map/ppermute | solution.py:326
  6.4 10.6 %collective-permute-done.near = bf16[512,512]{1,0:T(8,128)(2,1)S(1)} collective-permute-done((bf16[512,512]{1,0:T(8,128)(2,1)S(1)}, bf16[512,512]{1,0:T(8,128)(2,1)S(1)}, u32[]{:S(2)}, u32[]{:S(2)}) %collective-permute-start) | collective-permute-done | bytes 524320 | tf_op jit(solution)/shard_map/ppermute | solution.py:326
  17.0 2.3 %collective-permute-start.1 = (bf16[512,512]{1,0:T(8,128)(2,1)S(1)}, bf16[512,512]{1,0:T(8,128)(2,1)}, u32[]{:S(2)}, u32[]{:S(2)}) collective-permute-start(bf16[512,512]{1,0:T(8,128)(2,1)S(1)} %collective-permute-done.near), channel_id=1, source_target_pairs={{0,16},{16,0},{1,17},{17,1},{2,18},{18,2},{3,19},{19,3},{4,20},{20... | collective-permute-start | bytes 1572872 | tf_op jit(solution)/shard_map/ppermute | solution.py:378
  19.3 2.7 %collective-permute-start.2 = (bf16[128,640]{1,0:T(8,128)(2,1)S(1)}, bf16[128,640]{1,0:T(8,128)(2,1)S(1)}, u32[]{:S(2)}, u32[]{:S(2)}) collective-permute-start(bf16[128,640]{1,0:T(8,128)(2,1)S(1)} %get-tuple-element.18), channel_id=1, source_target_pairs={{0,2},{1,3},{2,4},{3,5},{4,6},{5,7},{6,8},{7,9},{8,10},{9,11},{10,... | collective-permute-start | bytes 491528 | tf_op jit(solution)/shard_map/ppermute | solution.py:324
  22.0 2.5 %collective-permute-start.4 = (bf16[128,640]{1,0:T(8,128)(2,1)S(1)}, bf16[128,640]{1,0:T(8,128)(2,1)S(1)}, u32[]{:S(2)}, u32[]{:S(2)}) collective-permute-start(bf16[128,640]{1,0:T(8,128)(2,1)S(1)} %get-tuple-element.19), channel_id=1, source_target_pairs={{2,0},{3,1},{4,2},{5,3},{6,4},{7,5},{8,6},{9,7},{10,8},{11,9},{12,... | collective-permute-start | bytes 491528 | tf_op jit(solution)/shard_map/ppermute | solution.py:325
  24.4 3.4 %collective-permute-done.2.refs_0_ = bf16[128,640]{1,0:T(8,128)(2,1)S(1)} collective-permute-done((bf16[128,640]{1,0:T(8,128)(2,1)S(1)}, bf16[128,640]{1,0:T(8,128)(2,1)S(1)}, u32[]{:S(2)}, u32[]{:S(2)}) %collective-permute-start.2) | collective-permute-done | bytes 163872 | tf_op jit(solution)/shard_map/ppermute | solution.py:324
  27.8 0.0 collective-permute-start.3
  27.8 0.0 collective-permute-done.4.refs_2_
  27.8 0.0 copy-start.3
  27.8 0.5 collective-permute-start.5
  28.3 8.8 %all-to-all-start = ((f32[16,16,128]{2,1,0:T(8,128)}), f32[16,16,128]{2,1,0:T(8,128)S(1)}, u32[]{:S(2)}, u32[]{:S(2)}) async-start(f32[16,16,128]{2,1,0:T(8,128)} %get-tuple-element.24), calls=%async_computation | async-start | bytes 262144 | tf_op jit(solution)/shard_map/all_to_all | solution.py:327
  37.1 0.0 collective-permute-done.3.refs_1_
  37.1 0.0 copy-done.2
  37.1 0.0 copy-done.3
  37.2 0.0 copy-start.4
  37.2 0.7 copy-done.4
  37.8 0.0 collective-permute-done.5.refs_3_
  37.8 2.7 %shard_map.78 = (bf16[8,128,384]{2,1,0:T(8,128)(2,1)S(1)}, bf16[1024,512]{1,0:T(8,128)(2,1)S(1)}, bf16[256,1024]{1,0:T(8,128)(2,1)S(1)}, bf16[2,128,512]{2,1,0:T(8,128)(2,1)S(1)}) custom-call(bf16[1024,512]{1,0:T(8,128)(2,1)} %anom.3, bf16[8,3,128,128]{3,2,1,0:T(8,128)(2,1)} %loc.3, bf16[128,640]{1,0:T(8,128)(2,1)} %copy-done.2, bf16[128,640]{1,0:T(8,128)(2,1)} %copy-done.4, ...), custom_call_target="tpu_custom_call" | custom-call | flops 1000000000 | bytes 4000000 | tf_op jit(solution)/shard_map/pallas_call | solution.py:38
  40.5 0.0 copy-done
  40.5 5.5 %all-to-all-done.recv = f32[16,16,128]{2,1,0:T(8,128)S(1)} async-done(((f32[16,16,128]{2,1,0:T(8,128)}), f32[16,16,128]{2,1,0:T(8,128)S(1)}, u32[]{:S(2)}, u32[]{:S(2)}) %all-to-all-start) | async-done | bytes 131104 | tf_op jit(solution)/shard_map/all_to_all | solution.py:327
  46.0 0.0 collective-permute-done.1.far
  46.0 5.7 %shard_map.79 = bf16[256,2048]{1,0:T(8,128)(2,1)} custom-call(bf16[512,512]{1,0:T(8,128)(2,1)} %copy-done, bf16[512,512]{1,0:T(8,128)(2,1)} %collective-permute-done.1.far, bf16[2,128,512]{2,1,0:T(8,128)(2,1)S(1)} %get-tuple-element.20.ends, bf16[8,128,384]{2,1,0:T(8,128)(2,1)S(1)} %get-tuple-element.21.lt, bf16[1024,512]{1,0:T(8,128)(2,1)S(1)} %get-tuple-element.22.gown, ...), custom_call_target="tpu_custom_call" | custom-call | flops 1000000000 | bytes 4000000 | tf_op jit(solution)/shard_map/pallas_call | solution.py:38
  51.7 5.6 %all-to-all-start.1 = ((bf16[8,32,2048]{2,1,0:T(8,128)(2,1)}), bf16[8,32,2048]{2,1,0:T(8,128)(2,1)S(1)}, u32[]{:S(2)}, u32[]{:S(2)}) async-start(bf16[8,32,2048]{2,1,0:T(8,128)(2,1)} %bitcast.1), calls=%async_computation.1 | async-start | bytes 2097152 | tf_op jit(solution)/shard_map/all_to_all | solution.py:400
  57.3 0.1 collective-permute-start.6
  57.4 1.4 %collective-permute-done.6.oth = bf16[8,128,128]{2,1,0:T(8,128)(2,1)S(1)} collective-permute-done((bf16[8,128,128]{2,1,0:T(8,128)(2,1)S(1)}, bf16[8,128,128]{2,1,0:T(8,128)(2,1)S(1)}, u32[]{:S(2)}, u32[]{:S(2)}) %collective-permute-start.6) | collective-permute-done | bytes 262176 | tf_op jit(solution)/shard_map/ppermute | solution.py:328
  58.8 0.7 copy-done.1
  59.5 2.8 %shard_map.80 = (s32[17,8]{1,0:T(8,128)S(1)}, bf16[2,128,128]{2,1,0:T(8,128)(2,1)S(1)}, bf16[2,128,128]{2,1,0:T(8,128)(2,1)S(1)}, bf16[2,128,128]{2,1,0:T(8,128)...) custom-call(f32[8,128,128]{2,1,0:T(8,128)} %bitcast.3, bf16[8,128,128]{2,1,0:T(8,128)(2,1)} %copy-done.1, ...), custom_call_target="tpu_custom_call" | custom-call | flops 1000000 | bytes 1000000 | tf_op jit(solution)/shard_map/pallas_call | solution.py:38
  62.4 0.1 collective-permute-start.7
  62.5 1.4 %collective-permute-start.8 = (bf16[2,128,128]{2,1,0:T(8,128)(2,1)S(1)}, bf16[2,128,128]{2,1,0:T(8,128)(2,1)S(1)}, u32[]{:S(2)}, u32[]{:S(2)}) collective-permute-start(bf16[2,128,128]{2,1,0:T(8,128)(2,1)S(1)} %get-tuple-element.28), channel_id=1, source_target_pairs={{0,64},{16,208},{32,96},{48,240},{64,128},{80,16},{96,160},{112,48... | collective-permute-start | bytes 196616 | tf_op jit(solution)/shard_map/ppermute | solution.py:350
  63.9 2.5 %collective-permute-start.9 = (bf16[2,128,128]{2,1,0:T(8,128)(2,1)S(1)}, bf16[2,128,128]{2,1,0:T(8,128)(2,1)S(1)}, u32[]{:S(2)}, u32[]{:S(2)}) collective-permute-start(bf16[2,128,128]{2,1,0:T(8,128)(2,1)S(1)} %get-tuple-element.29), channel_id=1, source_target_pairs={{0,96},{16,176},{32,128},{48,208},{64,160},{80,240},{96,192},{112,... | collective-permute-start | bytes 196616 | tf_op jit(solution)/shard_map/ppermute | solution.py:350
  66.4 2.4 %collective-permute-start.13 = (bf16[128,128]{1,0:T(8,128)(2,1)S(1)}, bf16[128,128]{1,0:T(8,128)(2,1)S(1)}, u32[]{:S(2)}, u32[]{:S(2)}) collective-permute-start(bf16[128,128]{1,0:T(8,128)(2,1)S(1)} %get-tuple-element.30), channel_id=1, source_target_pairs={{0,128},{32,160},{64,192},{96,224},{128,0},{160,32},{192,64},{224,... | collective-permute-start | bytes 98312 | tf_op jit(solution)/shard_map/ppermute | solution.py:351
  68.9 0.0 collective-permute-done.7.refs_1_
  68.9 1.0 %collective-permute-start.10 = (bf16[2,128,128]{2,1,0:T(8,128)(2,1)S(1)}, bf16[2,128,128]{2,1,0:T(8,128)(2,1)S(1)}, u32[]{:S(2)}, u32[]{:S(2)}) collective-permute-start(bf16[2,128,128]{2,1,0:T(8,128)(2,1)S(1)} %collective-permute-done.7.refs_1_), channel_id=1, source_target_pairs={{0,16},{16,0},{1,17},{17,1},{2,18},{18,2},{3,19},{19,3},{4,20},{20... | collective-permute-start | bytes 196616 | tf_op jit(solution)/shard_map/ppermute | solution.py:354
  69.9 0.0 collective-permute-done.8.refs_2_
  69.9 0.1 collective-permute-start.11
  70.0 0.0 collective-permute-done.9.refs_3_
  70.0 2.5 %collective-permute-start.12 = (bf16[2,128,128]{2,1,0:T(8,128)(2,1)S(1)}, bf16[2,128,128]{2,1,0:T(8,128)(2,1)S(1)}, u32[]{:S(2)}, u32[]{:S(2)}) collective-permute-start(bf16[2,128,128]{2,1,0:T(8,128)(2,1)S(1)} %collective-permute-done.9.refs_3_), channel_id=1, source_target_pairs={{0,16},{16,0},{1,17},{17,1},{2,18},{18,2},{3,19},{19,3},{4,20},{20... | collective-permute-start | bytes 196616 | tf_op jit(solution)/shard_map/ppermute | solution.py:354
  72.6 2.8 %collective-permute-done.13.refs_8_ = bf16[128,128]{1,0:T(8,128)(2,1)S(1)} collective-permute-done((bf16[128,128]{1,0:T(8,128)(2,1)S(1)}, bf16[128,128]{1,0:T(8,128)(2,1)S(1)}, u32[]{:S(2)}, u32[]{:S(2)}) %collective-permute-start.13) | collective-permute-done | bytes 32800 | tf_op jit(solution)/shard_map/ppermute | solution.py:351
  75.4 0.6 collective-permute-start.14
  76.0 0.9 collective-permute-done.14.refs_9_
  76.9 0.0 collective-permute-done.10.refs_5_
  76.9 0.0 collective-permute-done.11.refs_6_
  76.9 0.0 collective-permute-done.12.refs_7_
  76.9 0.0 all-to-all-done.1.parts
  76.9 2.0 %shard_map.81 = bf16[16,2,32,128]{3,2,1,0:T(8,128)(2,1)S(1)} custom-call(bf16[8,32,2048]{2,1,0:T(8,128)(2,1)S(1)} %all-to-all-done.1.parts, bf16[2,128,128]{2,1,0:T(8,128)(2,1)S(1)} %get-tuple-element.26.refs_0_.refs_4_, bf16[2,128,128]{2,1,0:T(8,128)(2,1)S(1)} %collective-permute-done.7.refs_1_, bf16[2,128,128]{2,1,0:T(8,128)(2,1)S(1)} %collective-permute-done.8.refs_2_, ...), custom_call_target="tpu_custom_call" | custom-call | flops 1000000000 | bytes 2000000 | tf_op jit(solution)/shard_map/pallas_call | solution.py:38
  78.9 15.5 %all_to_all.19.recv = bf16[16,2,32,128]{3,2,1,0:T(8,128)(2,1)S(1)} all-to-all(bf16[16,2,32,128]{3,2,1,0:T(8,128)(2,1)S(1)} %shard_map.81), channel_id=1, replica_groups=mesh['z'=8,'co'=2,'lon'=8,'ens'=2] {'z','co'}, dimensions={0} | all-to-all | bytes 524288 | tf_op jit(solution)/shard_map/all_to_all | solution.py:409
  94.4 1.6 %shard_map.82 = (f32[1,64,1024]{2,1,0:T(8,128)}, f32[1,64,1024]{2,1,0:T(8,128)}) custom-call(bf16[16,2,32,128]{3,2,1,0:T(8,128)(2,1)S(1)} %all_to_all.19.recv, s32[17,8]{1,0:T(8,128)S(1)} %get-tuple-element.31.traj), custom_call_target="tpu_custom_call" | custom-call | flops 1000000 | bytes 1000000 | tf_op jit(solution)/shard_map/pallas_call | solution.py:38
  (3 shorter events, 0.0 us)
Async XLA Ops:
  2.8 14.3 %collective-permute-start = (bf16[512,512]{1,0:T(8,128)(2,1)S(1)}, bf16[512,512]{1,0:T(8,128)(2,1)S(1)}, u32[]{:S(2)}, u32[]{:S(2)}) collective-permute-start(bf16[512,512]{1,0:T(8,128)(2,1)S(1)} %get-tuple-element.17), channel_id=1, source_target_pairs={{0,1},{1,0},{2,3},{3,2},{4,5},{5,4},{6,7},{7,6},{8,9},{9,8},{10,11... | collective-permute-start | bytes 1572872 | tf_op jit(solution)/shard_map/ppermute | solution.py:326
  17.0 23.5 %copy-start = (bf16[512,512]{1,0:T(8,128)(2,1)}, bf16[512,512]{1,0:T(8,128)(2,1)S(1)}, u32[]{:S(2)}) copy-start(bf16[512,512]{1,0:T(8,128)(2,1)S(1)} %collective-permute-done.near) | copy-start | bytes 1572868
  17.0 29.0 %collective-permute-start.1 = (bf16[512,512]{1,0:T(8,128)(2,1)S(1)}, bf16[512,512]{1,0:T(8,128)(2,1)}, u32[]{:S(2)}, u32[]{:S(2)}) collective-permute-start(bf16[512,512]{1,0:T(8,128)(2,1)S(1)} %collective-permute-done.near), channel_id=1, source_target_pairs={{0,16},{16,0},{1,17},{17,1},{2,18},{18,2},{3,19},{19,3},{4,20},{20... | collective-permute-start | bytes 1572872 | tf_op jit(solution)/shard_map/ppermute | solution.py:378
  19.3 8.5 %collective-permute-start.2 = (bf16[128,640]{1,0:T(8,128)(2,1)S(1)}, bf16[128,640]{1,0:T(8,128)(2,1)S(1)}, u32[]{:S(2)}, u32[]{:S(2)}) collective-permute-start(bf16[128,640]{1,0:T(8,128)(2,1)S(1)} %get-tuple-element.18), channel_id=1, source_target_pairs={{0,2},{1,3},{2,4},{3,5},{4,6},{5,7},{6,8},{7,9},{8,10},{9,11},{10,... | collective-permute-start | bytes 491528 | tf_op jit(solution)/shard_map/ppermute | solution.py:324
  22.0 5.8 %collective-permute-start.4 = (bf16[128,640]{1,0:T(8,128)(2,1)S(1)}, bf16[128,640]{1,0:T(8,128)(2,1)S(1)}, u32[]{:S(2)}, u32[]{:S(2)}) collective-permute-start(bf16[128,640]{1,0:T(8,128)(2,1)S(1)} %get-tuple-element.19), channel_id=1, source_target_pairs={{2,0},{3,1},{4,2},{5,3},{6,4},{7,5},{8,6},{9,7},{10,8},{11,9},{12,... | collective-permute-start | bytes 491528 | tf_op jit(solution)/shard_map/ppermute | solution.py:325
  27.8 9.3 %copy-start.2 = (bf16[128,640]{1,0:T(8,128)(2,1)}, bf16[128,640]{1,0:T(8,128)(2,1)S(1)}, u32[]{:S(2)}) copy-start(bf16[128,640]{1,0:T(8,128)(2,1)S(1)} %collective-permute-done.2.refs_0_) | copy-start | bytes 491524
  27.8 9.3 %collective-permute-start.3 = (bf16[128,640]{1,0:T(8,128)(2,1)S(1)}, bf16[128,640]{1,0:T(8,128)(2,1)S(1)}, u32[]{:S(2)}, u32[]{:S(2)}) collective-permute-start(bf16[128,640]{1,0:T(8,128)(2,1)S(1)} %collective-permute-done.2.refs_0_), channel_id=1, source_target_pairs={{0,16},{16,0},{1,17},{17,1},{2,18},{18,2},{3,19},{19,3},{4,20},{20... | collective-permute-start | bytes 491528 | tf_op jit(solution)/shard_map/ppermute | solution.py:357
  27.8 9.3 %copy-start.3 = (bf16[128,640]{1,0:T(8,128)(2,1)}, bf16[128,640]{1,0:T(8,128)(2,1)S(1)}, u32[]{:S(2)}) copy-start(bf16[128,640]{1,0:T(8,128)(2,1)S(1)} %collective-permute-done.4.refs_2_) | copy-start | bytes 491524
  27.8 10.0 %collective-permute-start.5 = (bf16[128,640]{1,0:T(8,128)(2,1)S(1)}, bf16[128,640]{1,0:T(8,128)(2,1)}, u32[]{:S(2)}, u32[]{:S(2)}) collective-permute-start(bf16[128,640]{1,0:T(8,128)(2,1)S(1)} %collective-permute-done.4.refs_2_), channel_id=1, source_target_pairs={{0,16},{16,0},{1,17},{17,1},{2,18},{18,2},{3,19},{19,3},{4,20},{20... | collective-permute-start | bytes 491528 | tf_op jit(solution)/shard_map/ppermute | solution.py:358
  28.3 17.7 %all-to-all-start = ((f32[16,16,128]{2,1,0:T(8,128)}), f32[16,16,128]{2,1,0:T(8,128)S(1)}, u32[]{:S(2)}, u32[]{:S(2)}) async-start(f32[16,16,128]{2,1,0:T(8,128)} %get-tuple-element.24), calls=%async_computation | async-start | bytes 262144 | tf_op jit(solution)/shard_map/all_to_all | solution.py:327
  37.2 0.7 copy-start.4
  51.7 25.2 %all-to-all-start.1 = ((bf16[8,32,2048]{2,1,0:T(8,128)(2,1)}), bf16[8,32,2048]{2,1,0:T(8,128)(2,1)S(1)}, u32[]{:S(2)}, u32[]{:S(2)}) async-start(bf16[8,32,2048]{2,1,0:T(8,128)(2,1)} %bitcast.1), calls=%async_computation.1 | async-start | bytes 2097152 | tf_op jit(solution)/shard_map/all_to_all | solution.py:400
  57.3 1.5 %collective-permute-start.6 = (bf16[8,128,128]{2,1,0:T(8,128)(2,1)S(1)}, bf16[8,128,128]{2,1,0:T(8,128)(2,1)S(1)}, u32[]{:S(2)}, u32[]{:S(2)}) collective-permute-start(bf16[8,128,128]{2,1,0:T(8,128)(2,1)S(1)} %get-tuple-element.25), channel_id=1, source_target_pairs={{0,16},{16,0},{1,17},{17,1},{2,18},{18,2},{3,19},{19,3},{4,20},{20... | collective-permute-start | bytes 786440 | tf_op jit(solution)/shard_map/ppermute | solution.py:328
  58.8 0.7 copy-start.1
  62.4 6.5 %collective-permute-start.7 = (bf16[2,128,128]{2,1,0:T(8,128)(2,1)S(1)}, bf16[2,128,128]{2,1,0:T(8,128)(2,1)S(1)}, u32[]{:S(2)}, u32[]{:S(2)}) collective-permute-start(bf16[2,128,128]{2,1,0:T(8,128)(2,1)S(1)} %get-tuple-element.27), channel_id=1, source_target_pairs={{0,32},{16,240},{32,64},{48,16},{64,96},{80,48},{96,128},{112,80},... | collective-permute-start | bytes 196616 | tf_op jit(solution)/shard_map/ppermute | solution.py:350
  62.5 7.4 %collective-permute-start.8 = (bf16[2,128,128]{2,1,0:T(8,128)(2,1)S(1)}, bf16[2,128,128]{2,1,0:T(8,128)(2,1)S(1)}, u32[]{:S(2)}, u32[]{:S(2)}) collective-permute-start(bf16[2,128,128]{2,1,0:T(8,128)(2,1)S(1)} %get-tuple-element.28), channel_id=1, source_target_pairs={{0,64},{16,208},{32,96},{48,240},{64,128},{80,16},{96,160},{112,48... | collective-permute-start | bytes 196616 | tf_op jit(solution)/shard_map/ppermute | solution.py:350
  63.9 6.1 %collective-permute-start.9 = (bf16[2,128,128]{2,1,0:T(8,128)(2,1)S(1)}, bf16[2,128,128]{2,1,0:T(8,128)(2,1)S(1)}, u32[]{:S(2)}, u32[]{:S(2)}) collective-permute-start(bf16[2,128,128]{2,1,0:T(8,128)(2,1)S(1)} %get-tuple-element.29), channel_id=1, source_target_pairs={{0,96},{16,176},{32,128},{48,208},{64,160},{80,240},{96,192},{112,... | collective-permute-start | bytes 196616 | tf_op jit(solution)/shard_map/ppermute | solution.py:350
  66.4 8.9 %collective-permute-start.13 = (bf16[128,128]{1,0:T(8,128)(2,1)S(1)}, bf16[128,128]{1,0:T(8,128)(2,1)S(1)}, u32[]{:S(2)}, u32[]{:S(2)}) collective-permute-start(bf16[128,128]{1,0:T(8,128)(2,1)S(1)} %get-tuple-element.30), channel_id=1, source_target_pairs={{0,128},{32,160},{64,192},{96,224},{128,0},{160,32},{192,64},{224,... | collective-permute-start | bytes 98312 | tf_op jit(solution)/shard_map/ppermute | solution.py:351
  68.9 8.0 %collective-permute-start.10 = (bf16[2,128,128]{2,1,0:T(8,128)(2,1)S(1)}, bf16[2,128,128]{2,1,0:T(8,128)(2,1)S(1)}, u32[]{:S(2)}, u32[]{:S(2)}) collective-permute-start(bf16[2,128,128]{2,1,0:T(8,128)(2,1)S(1)} %collective-permute-done.7.refs_1_), channel_id=1, source_target_pairs={{0,16},{16,0},{1,17},{17,1},{2,18},{18,2},{3,19},{19,3},{4,20},{20... | collective-permute-start | bytes 196616 | tf_op jit(solution)/shard_map/ppermute | solution.py:354
  69.9 6.9 %collective-permute-start.11 = (bf16[2,128,128]{2,1,0:T(8,128)(2,1)S(1)}, bf16[2,128,128]{2,1,0:T(8,128)(2,1)S(1)}, u32[]{:S(2)}, u32[]{:S(2)}) collective-permute-start(bf16[2,128,128]{2,1,0:T(8,128)(2,1)S(1)} %collective-permute-done.8.refs_2_), channel_id=1, source_target_pairs={{0,16},{16,0},{1,17},{17,1},{2,18},{18,2},{3,19},{19,3},{4,20},{20... | collective-permute-start | bytes 196616 | tf_op jit(solution)/shard_map/ppermute | solution.py:354
  70.0 6.8 %collective-permute-start.12 = (bf16[2,128,128]{2,1,0:T(8,128)(2,1)S(1)}, bf16[2,128,128]{2,1,0:T(8,128)(2,1)S(1)}, u32[]{:S(2)}, u32[]{:S(2)}) collective-permute-start(bf16[2,128,128]{2,1,0:T(8,128)(2,1)S(1)} %collective-permute-done.9.refs_3_), channel_id=1, source_target_pairs={{0,16},{16,0},{1,17},{17,1},{2,18},{18,2},{3,19},{19,3},{4,20},{20... | collective-permute-start | bytes 196616 | tf_op jit(solution)/shard_map/ppermute | solution.py:354
  75.4 1.5 %collective-permute-start.14 = (bf16[128,128]{1,0:T(8,128)(2,1)S(1)}, bf16[128,128]{1,0:T(8,128)(2,1)S(1)}, u32[]{:S(2)}, u32[]{:S(2)}) collective-permute-start(bf16[128,128]{1,0:T(8,128)(2,1)S(1)} %collective-permute-done.13.refs_8_), channel_id=1, source_target_pairs={{0,16},{16,0},{1,17},{17,1},{2,18},{18,2},{3,19},{19,3},{4,20},{20... | collective-permute-start | bytes 98312 | tf_op jit(solution)/shard_map/ppermute | solution.py:354

commit v4 on v3

--- a/solution.py
+++ b/solution.py
@@ -205,16 +205,16 @@
     for t in range(steps - 1, -1, -1):
         at[t] = cols_at(b)
         b = order_s[t, b]
-    group = 4
+    for t in range(steps):
+        w = jnp.broadcast_to(wt[:, t : t + 1], (n * BLK, BLK)).astype(bf16)
+        vals[:, t * BLK : (t + 1) * BLK] = w * full[:, at[t]]
     sent = []
-    for g in range(0, steps, group):
-        for t in range(g, g + group):
-            y = wt[:, t : t + 1] * full[:, at[t]].astype(f32)
-            vals[:, t * BLK : (t + 1) * BLK] = y.astype(bf16)
-        cols = slice(g * BLK, (g + group) * BLK)
+    width = steps * BLK // out_sem.shape[0]
+    for g in range(out_sem.shape[0]):
+        cols = slice(g * width, (g + 1) * width)
         y = jnp.dot(asel[...], vals[:, cols], preferred_element_type=f32)
         res[:, cols] = (y * scale).astype(bf16)
-        c = pltpu.make_async_copy(res.at[:, cols], out.at[:, cols], out_sem.at[g // group])
+        c = pltpu.make_async_copy(res.at[:, cols], out.at[:, cols], out_sem.at[g])
         c.start()
         sent.append(c)
     for c in sent:
@@ -234,22 +234,28 @@
     return y[:rows] + y[rows:]
 
 
-def scan_kernel(parts, *refs):
-    *held, out, blocks = refs
+def pack_kernel(*refs):
+    *got, out = refs
+    for j, src in enumerate(got[:-1]):
+        out[2 * j : 2 * j + 2] = src[...]
+    out[2 * len(got) - 2] = got[-1][...]
+
+
+def scan_kernel(parts, own, mine, theirs, out, blocks):
     co = lax.axis_index("co")
     z = lax.axis_index("z")
     n = parts.shape[0]
     steps = parts.shape[2] // BLK
     nz = steps // 2
     h = nz // 2
-    for d in range(h):
-        for j, src in enumerate((held[d], held[h + d]) if d else (held[0],)):
-            back = (co == 0) if j == 0 else (co == 1)
+    blocks[pl.ds(2 * z, 2)] = own[...]
+    for d in range(1, h):
+        for src, back in ((mine, co == 0), (theirs, co == 1)):
             k = lax.rem(jnp.where(back, z + nz - d, z + d), nz)
-            blocks[pl.ds(2 * k, 2)] = src[...]
+            blocks[pl.ds(2 * k, 2)] = src[2 * d - 2 : 2 * d]
     k = lax.rem(z + h, nz)
-    blocks[2 * k + co] = held[2 * h][...]
-    blocks[2 * k + 1 - co] = held[2 * h + 1][...]
+    blocks[2 * k + co] = mine[2 * h - 2]
+    blocks[2 * k + 1 - co] = theirs[2 * h - 2]
     force = []
     for t in range(steps):
         at = slice(t * BLK, (t + 1) * BLK)
@@ -269,14 +275,20 @@
         out[t, 1] = y.astype(bf16)
 
 
-def place_kernel(recv, traj, x, y):
+def place_kernel(recv, traj, x, y, xs, ys, sem):
     t = 2 * lax.axis_index("z") + lax.axis_index("co")
     rows = recv.shape[2]
-    for q in range(NB):
-        for c in range(2):
-            at = slice(c * rows, (c + 1) * rows)
-            x[0, at, cols_at(traj[t + 1, q])] = recv[2 * q + c, 0].astype(f32)
-            y[0, at, cols_at(traj[t, q])] = recv[2 * q + c, 1].astype(f32)
+    sent = []
+    for j, (to, held) in enumerate(((x, xs), (y, ys))):
+        for q in range(NB):
+            at = cols_at(traj[t + 1 - j, q])
+            for c in range(2):
+                held[0, c * rows : (c + 1) * rows, at] = recv[2 * q + c, j].astype(f32)
+        c = pltpu.make_async_copy(held, to, sem.at[j])
+        c.start()
+        sent.append(c)
+    for c in sent:
+        c.wait()
 
 
 def on_device(anomalies, localization, innovations, obs_cell, tangent_blocks, tangent_order):
@@ -349,10 +361,8 @@
             pairs.append((2 * k + 1, (k - d) % nz * 2 + 1))
         got.append(lax.ppermute(sends[d], time, pairs))
     last = lax.ppermute(sends[nz // 2], "z", [(k, (k + nz // 2) % nz) for k in range(nz)])
-    crossed = []
-    for g in got + [last]:
-        crossed.append(lax.ppermute(g, "co", swap))
-    held = [sends[0], *got, sends[0], *crossed[:-1], last, crossed[-1]]
+    (mine,) = call(pack_kernel, [shape((nz - 1, BLK, BLK), bf16)], [VM] * (nz // 2), data=10**6)(*got, last)
+    theirs = lax.ppermute(mine, "co", swap)
 
     up1 = lax.ppermute(up0, "co", swap)
     down1 = lax.ppermute(down0, "co", swap)
@@ -379,7 +389,7 @@
     (prod,) = call(
         functools.partial(product_kernel, scale),
         [shape((half // 2, steps * BLK), bf16)],
-        [HBM, HBM, VM, VM, VM, VM, VM],
+        [HBM, VM, VM, VM, VM, VM, VM],
         [
             pltpu.VMEM((cells + 2 * BLK, half), bf16),
             pltpu.VMEM((cells, COLS), bf16),
@@ -389,11 +399,11 @@
             pltpu.VMEM((steps, BLK), i32),
             pltpu.SMEM((steps, BLK), i32),
             pltpu.SemaphoreType.DMA((4,)),
-            pltpu.SemaphoreType.DMA((4,)),
+            pltpu.SemaphoreType.DMA((2,)),
         ],
         flops=10**9,
         data=4 * 10**6,
-        grant=24,
+        grant=14,
         specs=[HBM],
     )(near, far, ends, lt, gown, asel, recv)
     rows = half // 2 // n_lon
@@ -401,13 +411,21 @@
     (states,) = call(
         scan_kernel,
         [shape((steps, 2, rows, BLK), bf16)],
-        [VM] * (1 + len(held)),
+        [VM] * 4,
         [pltpu.VMEM((steps, BLK, BLK), bf16)],
         flops=10**9,
         data=2 * 10**6,
-    )(parts, *held)
+    )(parts, sends[0], mine, theirs)
     back = lax.all_to_all(states, time, 0, 0, tiled=True)
-    x, y = call(place_kernel, [shape((1, 2 * rows, COLS), f32)] * 2, [VM, SM], flops=10**6, data=10**6)(back, traj)
+    x, y = call(
+        place_kernel,
+        [shape((1, 2 * rows, COLS), f32)] * 2,
+        [VM, SM],
+        [pltpu.VMEM((1, 2 * rows, COLS), f32), pltpu.VMEM((1, 2 * rows, COLS), f32), pltpu.SemaphoreType.DMA((2,))],
+        flops=10**6,
+        data=10**6,
+        specs=[HBM, HBM],
+    )(back, traj)
     return x, y
 
 

time: 96.4 us -> 96 us (level)
  waiting for transfers between devices: 24.6 us -> 28.4 us
  starting transfers between devices: 36.9 us -> 33.4 us
    ppermute x4 -> x1, starting transfers between devices: 4.31 us -> 0.67 us  [on_device(): theirs = lax.ppermute(mine, 'co', swap)]
    ppermute x1, waiting for transfers between devices: 2.8 us -> 6.37 us  [on_device(): lax.ppermute(sends[nz // 2], 'z', [(k, (k + nz // 2) % nz) for k in range...]
    pallas_call x6 -> x7, Pallas kernels: 17 us -> 16.1 us  [run(): return made(*args)]
  transfers between devices with their start and end apart: 17 -> 14, of which waited for: 6 -> 6; matrix products, arithmetic and copies ran while one was open for 0% -> 0% of each run, Pallas kernels for 6% -> 6%
where the time goes in v4:
time: 96 us; the launch traced here: 95.6 us
  starting transfers between devices  33.4 us (35%)
  waiting for transfers between devices  28.4 us (30%)
  Pallas kernels  16.1 us (17%)
  blocking collectives  15.6 us (16%)
  local copies, waits for them, and re-layouts  1.37 us (1%)
    pallas_call x7, Pallas kernels, run(): return made(*args)  16.1 us
    all_to_all x1, blocking collectives, on_device(): back = lax.all_to_all(states, time, 0, 0, tiled=True)  15.6 us
    ppermute x1, waiting for transfers between devices, on_device(): near = lax.ppermute(piece, 'ens', swap)  10.6 us
    all_to_all x1, starting transfers between devices, on_device(): recv = lax.all_to_all(spread, time, 0, 0, tiled=True)  8.78 us
    ppermute x1, waiting for transfers between devices, on_device(): lax.ppermute(sends[nz // 2], 'z', [(k, (k + nz // 2) % nz) for k in range...  6.37 us
    all_to_all x1, starting transfers between devices, on_device(): lax.all_to_all(prod, 'lon', 0, 0, tiled=True)  5.56 us
    all_to_all x1, waiting for transfers between devices, on_device(): recv = lax.all_to_all(spread, time, 0, 0, tiled=True)  5.51 us
    ppermute x3, starting transfers between devices, on_device(): got.append(lax.ppermute(sends[d], time, pairs))  4.07 us
  transfers between devices with their start and end apart: 14, of which 6 were waited for; matrix products, arithmetic and copies ran while one was open for 0% of the time, Pallas kernels for 6%

profile of v4, /device:TPU:1, one launch (start us, length us, event | category | flops | bytes accessed | tf_op | source)
XLA Modules:
  0.0 95.6 jit_solution(12836550057906224542)
XLA Ops:
  0.6 2.1 %shard_map.77 = (f32[16,16,128]{2,1,0:T(8,128)}, bf16[128,640]{1,0:T(8,128)(2,1)S(1)}, bf16[128,640]{1,0:T(8,128)(2,1)S(1)}, bf16[512,512]{1,0:T(8,128)(2,1)S(1)}, bf16[8,128,128]{2,1,0:T(8,128)(2,1)S(1)}) custom-call(f32[1,512]{1,0:T(1,128)} %innov.1, s32[1,512]{1,0:T(1,128)} %cell.1, s32[1,8]{1,0:T(1,128)} %order.1, bf16[1024,512]{1,0:T(8,128)(2,1)} %anom.3, ...), custom_call_target="tpu_custom_call" | custom-call | flops 10000000 | bytes 1000000 | tf_op jit(solution)/shard_map/pallas_call | solution.py:38
  2.8 3.6 %collective-permute-start = (bf16[512,512]{1,0:T(8,128)(2,1)S(1)}, bf16[512,512]{1,0:T(8,128)(2,1)}, u32[]{:S(2)}, u32[]{:S(2)}) collective-permute-start(bf16[512,512]{1,0:T(8,128)(2,1)S(1)} %get-tuple-element.17), channel_id=1, source_target_pairs={{0,1},{1,0},{2,3},{3,2},{4,5},{5,4},{6,7},{7,6},{8,9},{9,8},{10,11... | collective-permute-start | bytes 1572872 | tf_op jit(solution)/shard_map/ppermute | solution.py:338
  6.4 10.6 %collective-permute-done.near = bf16[512,512]{1,0:T(8,128)(2,1)} collective-permute-done((bf16[512,512]{1,0:T(8,128)(2,1)S(1)}, bf16[512,512]{1,0:T(8,128)(2,1)}, u32[]{:S(2)}, u32[]{:S(2)}) %collective-permute-start) | collective-permute-done | bytes 524320 | tf_op jit(solution)/shard_map/ppermute | solution.py:338
  17.0 2.4 %collective-permute-start.1 = (bf16[512,512]{1,0:T(8,128)(2,1)}, bf16[512,512]{1,0:T(8,128)(2,1)S(1)}, u32[]{:S(2)}, u32[]{:S(2)}) collective-permute-start(bf16[512,512]{1,0:T(8,128)(2,1)} %collective-permute-done.near), channel_id=1, source_target_pairs={{0,16},{16,0},{1,17},{17,1},{2,18},{18,2},{3,19},{19,3},{4,20},{20... | collective-permute-start | bytes 1572872 | tf_op jit(solution)/shard_map/ppermute | solution.py:388
  19.4 2.7 %collective-permute-start.2 = (bf16[128,640]{1,0:T(8,128)(2,1)S(1)}, bf16[128,640]{1,0:T(8,128)(2,1)S(1)}, u32[]{:S(2)}, u32[]{:S(2)}) collective-permute-start(bf16[128,640]{1,0:T(8,128)(2,1)S(1)} %get-tuple-element.18), channel_id=1, source_target_pairs={{0,2},{1,3},{2,4},{3,5},{4,6},{5,7},{6,8},{7,9},{8,10},{9,11},{10,... | collective-permute-start | bytes 491528 | tf_op jit(solution)/shard_map/ppermute | solution.py:336
  22.1 2.5 %collective-permute-start.4 = (bf16[128,640]{1,0:T(8,128)(2,1)S(1)}, bf16[128,640]{1,0:T(8,128)(2,1)S(1)}, u32[]{:S(2)}, u32[]{:S(2)}) collective-permute-start(bf16[128,640]{1,0:T(8,128)(2,1)S(1)} %get-tuple-element.19), channel_id=1, source_target_pairs={{2,0},{3,1},{4,2},{5,3},{6,4},{7,5},{8,6},{9,7},{10,8},{11,9},{12,... | collective-permute-start | bytes 491528 | tf_op jit(solution)/shard_map/ppermute | solution.py:337
  24.5 3.4 %collective-permute-done.2.refs_0_ = bf16[128,640]{1,0:T(8,128)(2,1)S(1)} collective-permute-done((bf16[128,640]{1,0:T(8,128)(2,1)S(1)}, bf16[128,640]{1,0:T(8,128)(2,1)S(1)}, u32[]{:S(2)}, u32[]{:S(2)}) %collective-permute-start.2) | collective-permute-done | bytes 163872 | tf_op jit(solution)/shard_map/ppermute | solution.py:336
  27.9 0.0 copy-start.1
  27.9 0.0 collective-permute-start.3
  27.9 0.0 collective-permute-done.4.refs_2_
  27.9 0.0 copy-start.2
  27.9 0.5 collective-permute-start.5
  28.4 8.8 %all-to-all-start = ((f32[16,16,128]{2,1,0:T(8,128)}), f32[16,16,128]{2,1,0:T(8,128)S(1)}, u32[]{:S(2)}, u32[]{:S(2)}) async-start(f32[16,16,128]{2,1,0:T(8,128)} %get-tuple-element.24), calls=%async_computation | async-start | bytes 262144 | tf_op jit(solution)/shard_map/all_to_all | solution.py:339
  37.2 0.0 collective-permute-done.3.refs_1_
  37.2 0.0 copy-done.1
  37.2 0.0 copy-done.2
  37.2 0.0 copy-start.3
  37.3 0.7 copy-done.3
  37.9 0.0 collective-permute-done.5.refs_3_
  37.9 2.7 %shard_map.78 = (bf16[8,128,384]{2,1,0:T(8,128)(2,1)S(1)}, bf16[1024,512]{1,0:T(8,128)(2,1)S(1)}, bf16[256,1024]{1,0:T(8,128)(2,1)S(1)}, bf16[2,128,512]{2,1,0:T(8,128)(2,1)S(1)}) custom-call(bf16[1024,512]{1,0:T(8,128)(2,1)} %anom.3, bf16[8,3,128,128]{3,2,1,0:T(8,128)(2,1)} %loc.3, bf16[128,640]{1,0:T(8,128)(2,1)} %copy-done.1, bf16[128,640]{1,0:T(8,128)(2,1)} %copy-done.3, ...), custom_call_target="tpu_custom_call" | custom-call | flops 1000000000 | bytes 4000000 | tf_op jit(solution)/shard_map/pallas_call | solution.py:38
  40.6 5.5 %all-to-all-done.recv = f32[16,16,128]{2,1,0:T(8,128)S(1)} async-done(((f32[16,16,128]{2,1,0:T(8,128)}), f32[16,16,128]{2,1,0:T(8,128)S(1)}, u32[]{:S(2)}, u32[]{:S(2)}) %all-to-all-start) | async-done | bytes 131104 | tf_op jit(solution)/shard_map/all_to_all | solution.py:339
  46.1 0.0 collective-permute-done.1.far
  46.1 4.8 %shard_map.79 = bf16[256,2048]{1,0:T(8,128)(2,1)} custom-call(bf16[512,512]{1,0:T(8,128)(2,1)} %collective-permute-done.near, bf16[512,512]{1,0:T(8,128)(2,1)S(1)} %collective-permute-done.1.far, bf16[2,128,512]{2,1,0:T(8,128)(2,1)S(1)} %get-tuple-element.20.ends, bf16[8,128,384]{2,1,0:T(8,128)(2,1)S(1)} %get-tuple-element.21.lt, ...), custom_call_target="tpu_custom_call" | custom-call | flops 1000000000 | bytes 4000000 | tf_op jit(solution)/shard_map/pallas_call | solution.py:38
  50.9 5.6 %all-to-all-start.1 = ((bf16[8,32,2048]{2,1,0:T(8,128)(2,1)}), bf16[8,32,2048]{2,1,0:T(8,128)(2,1)S(1)}, u32[]{:S(2)}, u32[]{:S(2)}) async-start(bf16[8,32,2048]{2,1,0:T(8,128)(2,1)} %bitcast.1), calls=%async_computation.1 | async-start | bytes 2097152 | tf_op jit(solution)/shard_map/all_to_all | solution.py:410
  56.5 0.1 collective-permute-start.6
  56.6 1.4 %collective-permute-done.6.oth = bf16[8,128,128]{2,1,0:T(8,128)(2,1)S(1)} collective-permute-done((bf16[8,128,128]{2,1,0:T(8,128)(2,1)S(1)}, bf16[8,128,128]{2,1,0:T(8,128)(2,1)S(1)}, u32[]{:S(2)}, u32[]{:S(2)}) %collective-permute-start.6) | collective-permute-done | bytes 262176 | tf_op jit(solution)/shard_map/ppermute | solution.py:340
  58.0 0.0 copy-start
  58.0 0.7 copy-done
  58.7 2.8 %shard_map.80 = (s32[17,8]{1,0:T(8,128)S(1)}, bf16[2,128,128]{2,1,0:T(8,128)(2,1)S(1)}, bf16[2,128,128]{2,1,0:T(8,128)(2,1)S(1)}, bf16[2,128,128]{2,1,0:T(8,128)...) custom-call(f32[8,128,128]{2,1,0:T(8,128)} %bitcast.3, bf16[8,128,128]{2,1,0:T(8,128)(2,1)} %copy-done, ...), custom_call_target="tpu_custom_call" | custom-call | flops 1000000 | bytes 1000000 | tf_op jit(solution)/shard_map/pallas_call | solution.py:38
  61.6 0.2 collective-permute-start.7
  61.7 1.4 %collective-permute-start.8 = (bf16[2,128,128]{2,1,0:T(8,128)(2,1)S(1)}, bf16[2,128,128]{2,1,0:T(8,128)(2,1)S(1)}, u32[]{:S(2)}, u32[]{:S(2)}) collective-permute-start(bf16[2,128,128]{2,1,0:T(8,128)(2,1)S(1)} %get-tuple-element.28), channel_id=1, source_target_pairs={{0,64},{16,208},{32,96},{48,240},{64,128},{80,16},{96,160},{112,48... | collective-permute-start | bytes 196616 | tf_op jit(solution)/shard_map/ppermute | solution.py:362
  63.2 2.5 %collective-permute-start.9 = (bf16[2,128,128]{2,1,0:T(8,128)(2,1)S(1)}, bf16[2,128,128]{2,1,0:T(8,128)(2,1)S(1)}, u32[]{:S(2)}, u32[]{:S(2)}) collective-permute-start(bf16[2,128,128]{2,1,0:T(8,128)(2,1)S(1)} %get-tuple-element.29), channel_id=1, source_target_pairs={{0,96},{16,176},{32,128},{48,208},{64,160},{80,240},{96,192},{112,... | collective-permute-start | bytes 196616 | tf_op jit(solution)/shard_map/ppermute | solution.py:362
  65.6 2.5 %collective-permute-start.10 = (bf16[128,128]{1,0:T(8,128)(2,1)S(1)}, bf16[128,128]{1,0:T(8,128)(2,1)S(1)}, u32[]{:S(2)}, u32[]{:S(2)}) collective-permute-start(bf16[128,128]{1,0:T(8,128)(2,1)S(1)} %get-tuple-element.30), channel_id=1, source_target_pairs={{0,128},{32,160},{64,192},{96,224},{128,0},{160,32},{192,64},{224,... | collective-permute-start | bytes 98312 | tf_op jit(solution)/shard_map/ppermute | solution.py:363
  68.1 6.4 %collective-permute-done.10.refs_3_ = bf16[128,128]{1,0:T(8,128)(2,1)S(1)} collective-permute-done((bf16[128,128]{1,0:T(8,128)(2,1)S(1)}, bf16[128,128]{1,0:T(8,128)(2,1)S(1)}, u32[]{:S(2)}, u32[]{:S(2)}) %collective-permute-start.10) | collective-permute-done | bytes 32800 | tf_op jit(solution)/shard_map/ppermute | solution.py:363
  74.5 0.0 collective-permute-done.7.refs_0_
  74.5 0.0 collective-permute-done.8.refs_1_
  74.5 0.0 collective-permute-done.9.refs_2_
  74.5 0.7 collective-permute-start.11
  75.2 1.1 %collective-permute-done.11.theirs = bf16[7,128,128]{2,1,0:T(8,128)(2,1)S(1)} collective-permute-done((bf16[7,128,128]{2,1,0:T(8,128)(2,1)S(1)}, bf16[7,128,128]{2,1,0:T(8,128)(2,1)S(1)}, u32[]{:S(2)}, u32[]{:S(2)}) %collective-permute-start.11) | collective-permute-done | bytes 229408 | tf_op jit(solution)/shard_map/ppermute | solution.py:365
  76.3 0.0 all-to-all-done.1.parts
  76.3 2.0 %shard_map.82 = bf16[16,2,32,128]{3,2,1,0:T(8,128)(2,1)S(1)} custom-call(bf16[8,32,2048]{2,1,0:T(8,128)(2,1)S(1)} %all-to-all-done.1.parts, bf16[2,128,128]{2,1,0:T(8,128)(2,1)S(1)} %get-tuple-element.26.own, bf16[7,128,128]{2,1,0:T(8,128)(2,1)S(1)} %shard_map.81.mine, bf16[7,128,128]{2,1,0:T(8,128)(2,1)S(1)} %collective-permute-done.11.theirs), custom_call_target="tpu_custom_call" | custom-call | flops 1000000000 | bytes 2000000 | tf_op jit(solution)/shard_map/pallas_call | solution.py:38
  78.4 15.6 %all_to_all.19.recv = bf16[16,2,32,128]{3,2,1,0:T(8,128)(2,1)S(1)} all-to-all(bf16[16,2,32,128]{3,2,1,0:T(8,128)(2,1)S(1)} %shard_map.82), channel_id=1, replica_groups=mesh['z'=8,'co'=2,'lon'=8,'ens'=2] {'z','co'}, dimensions={0} | all-to-all | bytes 524288 | tf_op jit(solution)/shard_map/all_to_all | solution.py:419
  94.0 1.6 %shard_map.83 = (f32[1,64,1024]{2,1,0:T(8,128)}, f32[1,64,1024]{2,1,0:T(8,128)}) custom-call(bf16[16,2,32,128]{3,2,1,0:T(8,128)(2,1)S(1)} %all_to_all.19.recv, s32[17,8]{1,0:T(8,128)S(1)} %get-tuple-element.31.traj), custom_call_target="tpu_custom_call" | custom-call | flops 1000000 | bytes 1000000 | tf_op jit(solution)/shard_map/pallas_call | solution.py:38
  (1 shorter events, 0.0 us)
Async XLA Ops:
  2.8 14.3 %collective-permute-start = (bf16[512,512]{1,0:T(8,128)(2,1)S(1)}, bf16[512,512]{1,0:T(8,128)(2,1)}, u32[]{:S(2)}, u32[]{:S(2)}) collective-permute-start(bf16[512,512]{1,0:T(8,128)(2,1)S(1)} %get-tuple-element.17), channel_id=1, source_target_pairs={{0,1},{1,0},{2,3},{3,2},{4,5},{5,4},{6,7},{7,6},{8,9},{9,8},{10,11... | collective-permute-start | bytes 1572872 | tf_op jit(solution)/shard_map/ppermute | solution.py:338
  17.0 29.1 %collective-permute-start.1 = (bf16[512,512]{1,0:T(8,128)(2,1)}, bf16[512,512]{1,0:T(8,128)(2,1)S(1)}, u32[]{:S(2)}, u32[]{:S(2)}) collective-permute-start(bf16[512,512]{1,0:T(8,128)(2,1)} %collective-permute-done.near), channel_id=1, source_target_pairs={{0,16},{16,0},{1,17},{17,1},{2,18},{18,2},{3,19},{19,3},{4,20},{20... | collective-permute-start | bytes 1572872 | tf_op jit(solution)/shard_map/ppermute | solution.py:388
  19.4 8.5 %collective-permute-start.2 = (bf16[128,640]{1,0:T(8,128)(2,1)S(1)}, bf16[128,640]{1,0:T(8,128)(2,1)S(1)}, u32[]{:S(2)}, u32[]{:S(2)}) collective-permute-start(bf16[128,640]{1,0:T(8,128)(2,1)S(1)} %get-tuple-element.18), channel_id=1, source_target_pairs={{0,2},{1,3},{2,4},{3,5},{4,6},{5,7},{6,8},{7,9},{8,10},{9,11},{10,... | collective-permute-start | bytes 491528 | tf_op jit(solution)/shard_map/ppermute | solution.py:336
  22.1 5.8 %collective-permute-start.4 = (bf16[128,640]{1,0:T(8,128)(2,1)S(1)}, bf16[128,640]{1,0:T(8,128)(2,1)S(1)}, u32[]{:S(2)}, u32[]{:S(2)}) collective-permute-start(bf16[128,640]{1,0:T(8,128)(2,1)S(1)} %get-tuple-element.19), channel_id=1, source_target_pairs={{2,0},{3,1},{4,2},{5,3},{6,4},{7,5},{8,6},{9,7},{10,8},{11,9},{12,... | collective-permute-start | bytes 491528 | tf_op jit(solution)/shard_map/ppermute | solution.py:337
  27.9 9.3 %copy-start.1 = (bf16[128,640]{1,0:T(8,128)(2,1)}, bf16[128,640]{1,0:T(8,128)(2,1)S(1)}, u32[]{:S(2)}) copy-start(bf16[128,640]{1,0:T(8,128)(2,1)S(1)} %collective-permute-done.2.refs_0_) | copy-start | bytes 491524
  27.9 9.3 %collective-permute-start.3 = (bf16[128,640]{1,0:T(8,128)(2,1)S(1)}, bf16[128,640]{1,0:T(8,128)(2,1)S(1)}, u32[]{:S(2)}, u32[]{:S(2)}) collective-permute-start(bf16[128,640]{1,0:T(8,128)(2,1)S(1)} %collective-permute-done.2.refs_0_), channel_id=1, source_target_pairs={{0,16},{16,0},{1,17},{17,1},{2,18},{18,2},{3,19},{19,3},{4,20},{20... | collective-permute-start | bytes 491528 | tf_op jit(solution)/shard_map/ppermute | solution.py:367
  27.9 9.3 %copy-start.2 = (bf16[128,640]{1,0:T(8,128)(2,1)}, bf16[128,640]{1,0:T(8,128)(2,1)S(1)}, u32[]{:S(2)}) copy-start(bf16[128,640]{1,0:T(8,128)(2,1)S(1)} %collective-permute-done.4.refs_2_) | copy-start | bytes 491524
  27.9 10.0 %collective-permute-start.5 = (bf16[128,640]{1,0:T(8,128)(2,1)S(1)}, bf16[128,640]{1,0:T(8,128)(2,1)}, u32[]{:S(2)}, u32[]{:S(2)}) collective-permute-start(bf16[128,640]{1,0:T(8,128)(2,1)S(1)} %collective-permute-done.4.refs_2_), channel_id=1, source_target_pairs={{0,16},{16,0},{1,17},{17,1},{2,18},{18,2},{3,19},{19,3},{4,20},{20... | collective-permute-start | bytes 491528 | tf_op jit(solution)/shard_map/ppermute | solution.py:368
  28.4 17.7 %all-to-all-start = ((f32[16,16,128]{2,1,0:T(8,128)}), f32[16,16,128]{2,1,0:T(8,128)S(1)}, u32[]{:S(2)}, u32[]{:S(2)}) async-start(f32[16,16,128]{2,1,0:T(8,128)} %get-tuple-element.24), calls=%async_computation | async-start | bytes 262144 | tf_op jit(solution)/shard_map/all_to_all | solution.py:339
  37.2 0.7 copy-start.3
  50.9 25.4 %all-to-all-start.1 = ((bf16[8,32,2048]{2,1,0:T(8,128)(2,1)}), bf16[8,32,2048]{2,1,0:T(8,128)(2,1)S(1)}, u32[]{:S(2)}, u32[]{:S(2)}) async-start(bf16[8,32,2048]{2,1,0:T(8,128)(2,1)} %bitcast.1), calls=%async_computation.1 | async-start | bytes 2097152 | tf_op jit(solution)/shard_map/all_to_all | solution.py:410
  56.5 1.5 %collective-permute-start.6 = (bf16[8,128,128]{2,1,0:T(8,128)(2,1)S(1)}, bf16[8,128,128]{2,1,0:T(8,128)(2,1)S(1)}, u32[]{:S(2)}, u32[]{:S(2)}) collective-permute-start(bf16[8,128,128]{2,1,0:T(8,128)(2,1)S(1)} %get-tuple-element.25), channel_id=1, source_target_pairs={{0,16},{16,0},{1,17},{17,1},{2,18},{18,2},{3,19},{19,3},{4,20},{20... | collective-permute-start | bytes 786440 | tf_op jit(solution)/shard_map/ppermute | solution.py:340
  58.0 0.7 copy-start
  61.6 13.0 %collective-permute-start.7 = (bf16[2,128,128]{2,1,0:T(8,128)(2,1)S(1)}, bf16[2,128,128]{2,1,0:T(8,128)(2,1)S(1)}, u32[]{:S(2)}, u32[]{:S(2)}) collective-permute-start(bf16[2,128,128]{2,1,0:T(8,128)(2,1)S(1)} %get-tuple-element.27), channel_id=1, source_target_pairs={{0,32},{16,240},{32,64},{48,16},{64,96},{80,48},{96,128},{112,80},... | collective-permute-start | bytes 196616 | tf_op jit(solution)/shard_map/ppermute | solution.py:362
  61.7 12.8 %collective-permute-start.8 = (bf16[2,128,128]{2,1,0:T(8,128)(2,1)S(1)}, bf16[2,128,128]{2,1,0:T(8,128)(2,1)S(1)}, u32[]{:S(2)}, u32[]{:S(2)}) collective-permute-start(bf16[2,128,128]{2,1,0:T(8,128)(2,1)S(1)} %get-tuple-element.28), channel_id=1, source_target_pairs={{0,64},{16,208},{32,96},{48,240},{64,128},{80,16},{96,160},{112,48... | collective-permute-start | bytes 196616 | tf_op jit(solution)/shard_map/ppermute | solution.py:362
  63.2 11.4 %collective-permute-start.9 = (bf16[2,128,128]{2,1,0:T(8,128)(2,1)S(1)}, bf16[2,128,128]{2,1,0:T(8,128)(2,1)S(1)}, u32[]{:S(2)}, u32[]{:S(2)}) collective-permute-start(bf16[2,128,128]{2,1,0:T(8,128)(2,1)S(1)} %get-tuple-element.29), channel_id=1, source_target_pairs={{0,96},{16,176},{32,128},{48,208},{64,160},{80,240},{96,192},{112,... | collective-permute-start | bytes 196616 | tf_op jit(solution)/shard_map/ppermute | solution.py:362
  65.6 8.9 %collective-permute-start.10 = (bf16[128,128]{1,0:T(8,128)(2,1)S(1)}, bf16[128,128]{1,0:T(8,128)(2,1)S(1)}, u32[]{:S(2)}, u32[]{:S(2)}) collective-permute-start(bf16[128,128]{1,0:T(8,128)(2,1)S(1)} %get-tuple-element.30), channel_id=1, source_target_pairs={{0,128},{32,160},{64,192},{96,224},{128,0},{160,32},{192,64},{224,... | collective-permute-start | bytes 98312 | tf_op jit(solution)/shard_map/ppermute | solution.py:363
  74.5 1.8 %collective-permute-start.11 = (bf16[7,128,128]{2,1,0:T(8,128)(2,1)S(1)}, bf16[7,128,128]{2,1,0:T(8,128)(2,1)S(1)}, u32[]{:S(2)}, u32[]{:S(2)}) collective-permute-start(bf16[7,128,128]{2,1,0:T(8,128)(2,1)S(1)} %shard_map.81.mine), channel_id=1, source_target_pairs={{0,16},{16,0},{1,17},{17,1},{2,18},{18,2},{3,19},{19,3},{4,20},{20... | collective-permute-start | bytes 688136 | tf_op jit(solution)/shard_map/ppermute | solution.py:365

commit v5 on v4

--- a/solution.py
+++ b/solution.py
@@ -104,14 +104,14 @@
 
 
 def choose_kernel(own, oth, recv, traj, *refs):
-    *outs, ints, order_s, picked, sem = refs
+    *outs, ints, order_s, sem = refs
     z = lax.axis_index("z")
     co = lax.axis_index("co")
     steps = recv.shape[0]
     nz = steps // 2
     for k in range(steps):
         ints[k : k + 1] = recv[k, 8:9, :].astype(i32)
-    d = pltpu.make_async_copy(ints, order_s, sem.at[0])
+    d = pltpu.make_async_copy(ints, order_s, sem)
     d.start()
     d.wait()
     at = [jnp.int32(q) for q in range(NB)]
@@ -121,33 +121,23 @@
         at = [order_s[t, b] for b in at]
     for q in range(NB):
         traj[0, q] = at[q]
-    copies = []
     for d, out in enumerate(outs):
         q = lax.rem(jnp.where(co == 0, z + d, z + nz - d), nz)
-        copies.append((own.at[traj[2 * z + co + 1, q]], picked.at[d]))
+        mine = own[traj[2 * z + co + 1, q]]
         if d < nz // 2:
-            copies.append((oth.at[traj[2 * z + 2 - co, q]], out.at[1 - co]))
-    for c in copies_of(copies, sem.at[pl.ds(1, len(copies))]):
-        c.wait()
-    for d, out in enumerate(outs):
-        if d < nz // 2:
-            out[co] = picked[d].astype(bf16)
+            out[co] = mine
+            out[1 - co] = oth[traj[2 * z + 2 - co, q]]
         else:
-            out[...] = picked[d].astype(bf16)
-
-
-def ready_kernel(anom, loc, *refs):
-    *edges, lt, gown, asel, ends, anom_v, loc_v, edge_v, pad, sem = refs
+            out[...] = mine
+
+
+def ready_kernel(anom, loc, up0, up1, down0, down1, lt, gown, asel, ends, anom_v, loc_v, pad, held, sem, out_sem):
     co = lax.axis_index("co")
-    pairs = [(a, edge_v.at[i]) for i, a in enumerate(edges)]
-    copies = copies_of(((loc, loc_v), (anom, anom_v), *pairs), sem)
+    copies = copies_of(((loc, loc_v), (anom, anom_v)), sem)
     n = loc.shape[0]
     half = anom.shape[1]
-    for c in copies[2:]:
-        c.wait()
-    up0, up1, down0, down1 = (edge_v.at[i] for i in range(4))
-    before = jnp.where(co == 0, up0[:, :half], up1[:, :half])
-    after = jnp.where(co == 0, down0[:, :half], down1[:, :half])
+    pad[:BLK] = jnp.where(co == 0, up0[:, :half], up1[:, :half])
+    pad[BLK + n * BLK :] = jnp.where(co == 0, down0[:, :half], down1[:, :half])
     ends[0] = jnp.where(co == 0, up1[:, :half], up0[:, :half])
     ends[1] = jnp.where(co == 0, down1[:, :half], down0[:, :half])
     copies[0].wait()
@@ -156,15 +146,16 @@
         nxt = down0[:, half:] if b == n - 1 else loc_v[b + 1, 0]
         lt[b] = jnp.concatenate([prev.T, loc_v[b, 1].T, nxt.T], axis=1)
     copies[1].wait()
-    pad[:BLK] = before
     pad[BLK : BLK + n * BLK] = anom_v[...]
-    pad[BLK + n * BLK :] = after
     for b in range(n):
         y = jnp.dot(lt[b], pad[b * BLK : (b + 3) * BLK], preferred_element_type=f32)
-        gown[b * BLK : (b + 1) * BLK] = y.astype(bf16)
+        held[b * BLK : (b + 1) * BLK] = y.astype(bf16)
+    sent = pltpu.make_async_copy(held, gown, out_sem)
+    sent.start()
     at = anom_v[...].T
     for k in range(half // 64):
         asel[k * 32 : (k + 1) * 32] = jnp.where(co == 0, at[k * 64 : k * 64 + 32], at[k * 64 + 32 : (k + 1) * 64])
+    sent.wait()
 
 
 def product_kernel(
@@ -338,21 +329,16 @@
     near = lax.ppermute(piece, "ens", swap)
     recv = lax.all_to_all(spread, time, 0, 0, tiled=True)
     oth_blocks = lax.ppermute(own_blocks, "co", swap)
-    count = nz + 1
     traj, *sends = call(
         choose_kernel,
         [shape((steps + 1, NB), i32)] + [shape((2, BLK, BLK), bf16)] * (nz // 2) + [shape((BLK, BLK), bf16)],
-        [HBM, HBM, VM],
-        [
-            pltpu.VMEM((steps, BLK), i32),
-            pltpu.SMEM((steps, BLK), i32),
-            pltpu.VMEM((nz // 2 + 1, BLK, BLK), f32),
-            pltpu.SemaphoreType.DMA((count + 1,)),
-        ],
+        [VM] * 3,
+        [pltpu.VMEM((steps, BLK), i32), pltpu.SMEM((steps, BLK), i32), pltpu.SemaphoreType.DMA],
         flops=10**6,
         data=10**6,
         specs=[SM] + [VM] * (nz // 2 + 1),
-    )(tangent_blocks.reshape(NB, BLK, BLK), oth_blocks, recv)
+        grant=4,
+    )(own_blocks, oth_blocks, recv)
     got = []
     for d in range(1, nz // 2):
         pairs = []
@@ -370,26 +356,29 @@
         ready_kernel,
         [
             shape((n, BLK, 3 * BLK), bf16),
-            shape((cells, half), bf16),
+            pltpu.HBM((cells, half), bf16),
             shape((half // 2, cells), bf16),
             shape((2, BLK, half), bf16),
         ],
-        [HBM] * 6,
+        [HBM, HBM, VM, VM, VM, VM],
         [
             pltpu.VMEM(anomalies.shape, bf16),
             pltpu.VMEM(localization.shape, bf16),
-            pltpu.VMEM((4, BLK, half + BLK), bf16),
             pltpu.VMEM((cells + 2 * BLK, half), bf16),
-            pltpu.SemaphoreType.DMA((6,)),
+            pltpu.VMEM((cells, half), bf16),
+            pltpu.SemaphoreType.DMA((2,)),
+            pltpu.SemaphoreType.DMA,
         ],
         flops=10**9,
         data=4 * 10**6,
+        specs=[VM, HBM, VM, VM],
+        grant=10,
     )(anomalies, localization, up0, up1, down0, down1)
     far = lax.ppermute(near, "co", swap)
     (prod,) = call(
         functools.partial(product_kernel, scale),
         [shape((half // 2, steps * BLK), bf16)],
-        [HBM, VM, VM, VM, VM, VM, VM],
+        [HBM, VM, VM, VM, HBM, VM, VM],
         [
             pltpu.VMEM((cells + 2 * BLK, half), bf16),
             pltpu.VMEM((cells, COLS), bf16),

time: 96 us -> 94.1 us (0.980)
  local copies, waits for them, and re-layouts: 1.37 us -> 0 us
    unnamed x8 -> x0, local copies, waits for them, and re-layouts: 1.37 us -> none
  transfers between devices with their start and end apart: 14 -> 14, of which waited for: 6 -> 6; matrix products, arithmetic and copies ran while one was open for 0% -> 0% of each run, Pallas kernels for 6% -> 5%
where the time goes in v5:
time: 94.1 us; the launch traced here: 93.8 us
  starting transfers between devices  33.4 us (35%)
  waiting for transfers between devices  28.6 us (30%)
  blocking collectives  15.6 us (17%)
  Pallas kernels  15.5 us (16%)
    all_to_all x1, blocking collectives, on_device(): back = lax.all_to_all(states, time, 0, 0, tiled=True)  15.6 us
    pallas_call x7, Pallas kernels, run(): return made(*args)  15.5 us
    ppermute x1, waiting for transfers between devices, on_device(): near = lax.ppermute(piece, 'ens', swap)  10.6 us
    all_to_all x1, starting transfers between devices, on_device(): recv = lax.all_to_all(spread, time, 0, 0, tiled=True)  8.78 us
    ppermute x1, waiting for transfers between devices, on_device(): lax.ppermute(sends[nz // 2], 'z', [(k, (k + nz // 2) % nz) for k in range...  6.38 us
    all_to_all x1, waiting for transfers between devices, on_device(): recv = lax.all_to_all(spread, time, 0, 0, tiled=True)  5.67 us
    all_to_all x1, starting transfers between devices, on_device(): lax.all_to_all(prod, 'lon', 0, 0, tiled=True)  5.56 us
    ppermute x3, starting transfers between devices, on_device(): got.append(lax.ppermute(sends[d], time, pairs))  4.06 us
  transfers between devices with their start and end apart: 14, of which 6 were waited for; matrix products, arithmetic and copies ran while one was open for 0% of the time, Pallas kernels for 5%

profile of v5, /device:TPU:1, one launch (start us, length us, event | category | flops | bytes accessed | tf_op | source)
XLA Modules:
  0.0 93.8 jit_solution(8794765534433732263)
XLA Ops:
  0.6 2.1 %shard_map.77 = (f32[16,16,128]{2,1,0:T(8,128)}, bf16[128,640]{1,0:T(8,128)(2,1)S(1)}, bf16[128,640]{1,0:T(8,128)(2,1)S(1)}, bf16[512,512]{1,0:T(8,128)(2,1)S(1)}, bf16[8,128,128]{2,1,0:T(8,128)(2,1)S(1)}) custom-call(f32[1,512]{1,0:T(1,128)} %innov.1, s32[1,512]{1,0:T(1,128)} %cell.1, s32[1,8]{1,0:T(1,128)} %order.1, bf16[1024,512]{1,0:T(8,128)(2,1)} %anom.3, ...), custom_call_target="tpu_custom_call" | custom-call | flops 10000000 | bytes 1000000 | tf_op jit(solution)/shard_map/pallas_call | solution.py:38
  2.8 3.6 %collective-permute-start = (bf16[512,512]{1,0:T(8,128)(2,1)S(1)}, bf16[512,512]{1,0:T(8,128)(2,1)}, u32[]{:S(2)}, u32[]{:S(2)}) collective-permute-start(bf16[512,512]{1,0:T(8,128)(2,1)S(1)} %get-tuple-element.17), channel_id=1, source_target_pairs={{0,1},{1,0},{2,3},{3,2},{4,5},{5,4},{6,7},{7,6},{8,9},{9,8},{10,11... | collective-permute-start | bytes 1572872 | tf_op jit(solution)/shard_map/ppermute | solution.py:329
  6.4 10.6 %collective-permute-done.near = bf16[512,512]{1,0:T(8,128)(2,1)} collective-permute-done((bf16[512,512]{1,0:T(8,128)(2,1)S(1)}, bf16[512,512]{1,0:T(8,128)(2,1)}, u32[]{:S(2)}, u32[]{:S(2)}) %collective-permute-start) | collective-permute-done | bytes 524320 | tf_op jit(solution)/shard_map/ppermute | solution.py:329
  17.0 2.4 %collective-permute-start.1 = (bf16[512,512]{1,0:T(8,128)(2,1)}, bf16[512,512]{1,0:T(8,128)(2,1)S(1)}, u32[]{:S(2)}, u32[]{:S(2)}) collective-permute-start(bf16[512,512]{1,0:T(8,128)(2,1)} %collective-permute-done.near), channel_id=1, source_target_pairs={{0,16},{16,0},{1,17},{17,1},{2,18},{18,2},{3,19},{19,3},{4,20},{20... | collective-permute-start | bytes 1572872 | tf_op jit(solution)/shard_map/ppermute | solution.py:377
  19.4 2.7 %collective-permute-start.2 = (bf16[128,640]{1,0:T(8,128)(2,1)S(1)}, bf16[128,640]{1,0:T(8,128)(2,1)S(1)}, u32[]{:S(2)}, u32[]{:S(2)}) collective-permute-start(bf16[128,640]{1,0:T(8,128)(2,1)S(1)} %get-tuple-element.18), channel_id=1, source_target_pairs={{0,2},{1,3},{2,4},{3,5},{4,6},{5,7},{6,8},{7,9},{8,10},{9,11},{10,... | collective-permute-start | bytes 491528 | tf_op jit(solution)/shard_map/ppermute | solution.py:327
  22.1 2.5 %collective-permute-start.4 = (bf16[128,640]{1,0:T(8,128)(2,1)S(1)}, bf16[128,640]{1,0:T(8,128)(2,1)S(1)}, u32[]{:S(2)}, u32[]{:S(2)}) collective-permute-start(bf16[128,640]{1,0:T(8,128)(2,1)S(1)} %get-tuple-element.19), channel_id=1, source_target_pairs={{2,0},{3,1},{4,2},{5,3},{6,4},{7,5},{8,6},{9,7},{10,8},{11,9},{12,... | collective-permute-start | bytes 491528 | tf_op jit(solution)/shard_map/ppermute | solution.py:328
  24.6 3.4 %collective-permute-done.2.up0 = bf16[128,640]{1,0:T(8,128)(2,1)S(1)} collective-permute-done((bf16[128,640]{1,0:T(8,128)(2,1)S(1)}, bf16[128,640]{1,0:T(8,128)(2,1)S(1)}, u32[]{:S(2)}, u32[]{:S(2)}) %collective-permute-start.2) | collective-permute-done | bytes 163872 | tf_op jit(solution)/shard_map/ppermute | solution.py:327
  27.9 0.0 collective-permute-start.3
  27.9 0.0 collective-permute-done.4.down0
  27.9 0.5 collective-permute-start.5
  28.4 8.8 %all-to-all-start = ((f32[16,16,128]{2,1,0:T(8,128)}), f32[16,16,128]{2,1,0:T(8,128)S(1)}, u32[]{:S(2)}, u32[]{:S(2)}) async-start(f32[16,16,128]{2,1,0:T(8,128)} %get-tuple-element.24), calls=%async_computation | async-start | bytes 262144 | tf_op jit(solution)/shard_map/all_to_all | solution.py:330
  37.2 0.0 collective-permute-done.3.up1
  37.2 0.0 collective-permute-done.5.down1
  37.2 3.2 %shard_map.78 = (bf16[8,128,384]{2,1,0:T(8,128)(2,1)S(1)}, bf16[1024,512]{1,0:T(8,128)(2,1)}, bf16[256,1024]{1,0:T(8,128)(2,1)S(1)}, bf16[2,128,512]{2,1,0:T(8,128)(2,1)S(1)}) custom-call(bf16[1024,512]{1,0:T(8,128)(2,1)} %anom.3, bf16[8,3,128,128]{3,2,1,0:T(8,128)(2,1)} %loc.3, bf16[128,640]{1,0:T(8,128)(2,1)S(1)} %collective-permute-done.2.up0, ...), custom_call_target="tpu_custom_call" | custom-call | flops 1000000000 | bytes 4000000 | tf_op jit(solution)/shard_map/pallas_call | solution.py:38
  40.4 5.7 %all-to-all-done.recv = f32[16,16,128]{2,1,0:T(8,128)S(1)} async-done(((f32[16,16,128]{2,1,0:T(8,128)}), f32[16,16,128]{2,1,0:T(8,128)S(1)}, u32[]{:S(2)}, u32[]{:S(2)}) %all-to-all-start) | async-done | bytes 131104 | tf_op jit(solution)/shard_map/all_to_all | solution.py:330
  46.1 0.0 collective-permute-done.1.far
  46.1 4.8 %shard_map.79 = bf16[256,2048]{1,0:T(8,128)(2,1)} custom-call(bf16[512,512]{1,0:T(8,128)(2,1)} %collective-permute-done.near, bf16[512,512]{1,0:T(8,128)(2,1)S(1)} %collective-permute-done.1.far, bf16[2,128,512]{2,1,0:T(8,128)(2,1)S(1)} %get-tuple-element.20.ends, bf16[8,128,384]{2,1,0:T(8,128)(2,1)S(1)} %get-tuple-element.21.lt, ...), custom_call_target="tpu_custom_call" | custom-call | flops 1000000000 | bytes 4000000 | tf_op jit(solution)/shard_map/pallas_call | solution.py:38
  50.9 5.6 %all-to-all-start.1 = ((bf16[8,32,2048]{2,1,0:T(8,128)(2,1)}), bf16[8,32,2048]{2,1,0:T(8,128)(2,1)S(1)}, u32[]{:S(2)}, u32[]{:S(2)}) async-start(bf16[8,32,2048]{2,1,0:T(8,128)(2,1)} %bitcast.1), calls=%async_computation.1 | async-start | bytes 2097152 | tf_op jit(solution)/shard_map/all_to_all | solution.py:399
  56.5 0.1 collective-permute-start.6
  56.6 1.4 %collective-permute-done.6.oth = bf16[8,128,128]{2,1,0:T(8,128)(2,1)S(1)} collective-permute-done((bf16[8,128,128]{2,1,0:T(8,128)(2,1)S(1)}, bf16[8,128,128]{2,1,0:T(8,128)(2,1)S(1)}, u32[]{:S(2)}, u32[]{:S(2)}) %collective-permute-start.6) | collective-permute-done | bytes 262176 | tf_op jit(solution)/shard_map/ppermute | solution.py:331
  58.0 1.7 %shard_map.80 = (s32[17,8]{1,0:T(8,128)S(1)}, bf16[2,128,128]{2,1,0:T(8,128)(2,1)S(1)}, bf16[2,128,128]{2,1,0:T(8,128)(2,1)S(1)}, bf16[2,128,128]{2,1,0:T(8,128)...) custom-call(bf16[8,128,128]{2,1,0:T(8,128)(2,1)S(1)} %get-tuple-element.25.own, ...), custom_call_target="tpu_custom_call" | custom-call | flops 1000000 | bytes 1000000 | tf_op jit(solution)/shard_map/pallas_call | solution.py:38
  59.8 0.2 collective-permute-start.7
  59.9 1.4 %collective-permute-start.8 = (bf16[2,128,128]{2,1,0:T(8,128)(2,1)S(1)}, bf16[2,128,128]{2,1,0:T(8,128)(2,1)S(1)}, u32[]{:S(2)}, u32[]{:S(2)}) collective-permute-start(bf16[2,128,128]{2,1,0:T(8,128)(2,1)S(1)} %get-tuple-element.28), channel_id=1, source_target_pairs={{0,64},{16,208},{32,96},{48,240},{64,128},{80,16},{96,160},{112,48... | collective-permute-start | bytes 196616 | tf_op jit(solution)/shard_map/ppermute | solution.py:348
  61.4 2.5 %collective-permute-start.9 = (bf16[2,128,128]{2,1,0:T(8,128)(2,1)S(1)}, bf16[2,128,128]{2,1,0:T(8,128)(2,1)S(1)}, u32[]{:S(2)}, u32[]{:S(2)}) collective-permute-start(bf16[2,128,128]{2,1,0:T(8,128)(2,1)S(1)} %get-tuple-element.29), channel_id=1, source_target_pairs={{0,96},{16,176},{32,128},{48,208},{64,160},{80,240},{96,192},{112,... | collective-permute-start | bytes 196616 | tf_op jit(solution)/shard_map/ppermute | solution.py:348
  63.8 2.5 %collective-permute-start.10 = (bf16[128,128]{1,0:T(8,128)(2,1)S(1)}, bf16[128,128]{1,0:T(8,128)(2,1)S(1)}, u32[]{:S(2)}, u32[]{:S(2)}) collective-permute-start(bf16[128,128]{1,0:T(8,128)(2,1)S(1)} %get-tuple-element.30), channel_id=1, source_target_pairs={{0,128},{32,160},{64,192},{96,224},{128,0},{160,32},{192,64},{224,... | collective-permute-start | bytes 98312 | tf_op jit(solution)/shard_map/ppermute | solution.py:349
  66.3 6.4 %collective-permute-done.10.refs_3_ = bf16[128,128]{1,0:T(8,128)(2,1)S(1)} collective-permute-done((bf16[128,128]{1,0:T(8,128)(2,1)S(1)}, bf16[128,128]{1,0:T(8,128)(2,1)S(1)}, u32[]{:S(2)}, u32[]{:S(2)}) %collective-permute-start.10) | collective-permute-done | bytes 32800 | tf_op jit(solution)/shard_map/ppermute | solution.py:349
  72.7 0.0 collective-permute-done.7.refs_0_
  72.7 0.0 collective-permute-done.8.refs_1_
  72.7 0.0 collective-permute-done.9.refs_2_
  72.8 0.7 collective-permute-start.11
  73.4 1.1 %collective-permute-done.11.theirs = bf16[7,128,128]{2,1,0:T(8,128)(2,1)S(1)} collective-permute-done((bf16[7,128,128]{2,1,0:T(8,128)(2,1)S(1)}, bf16[7,128,128]{2,1,0:T(8,128)(2,1)S(1)}, u32[]{:S(2)}, u32[]{:S(2)}) %collective-permute-start.11) | collective-permute-done | bytes 229408 | tf_op jit(solution)/shard_map/ppermute | solution.py:351
  74.5 0.0 all-to-all-done.1.parts
  74.5 2.0 %shard_map.82 = bf16[16,2,32,128]{3,2,1,0:T(8,128)(2,1)S(1)} custom-call(bf16[8,32,2048]{2,1,0:T(8,128)(2,1)S(1)} %all-to-all-done.1.parts, bf16[2,128,128]{2,1,0:T(8,128)(2,1)S(1)} %get-tuple-element.26.own, bf16[7,128,128]{2,1,0:T(8,128)(2,1)S(1)} %shard_map.81.mine, bf16[7,128,128]{2,1,0:T(8,128)(2,1)S(1)} %collective-permute-done.11.theirs), custom_call_target="tpu_custom_call" | custom-call | flops 1000000000 | bytes 2000000 | tf_op jit(solution)/shard_map/pallas_call | solution.py:38
  76.6 15.6 %all_to_all.19.recv = bf16[16,2,32,128]{3,2,1,0:T(8,128)(2,1)S(1)} all-to-all(bf16[16,2,32,128]{3,2,1,0:T(8,128)(2,1)S(1)} %shard_map.82), channel_id=1, replica_groups=mesh['z'=8,'co'=2,'lon'=8,'ens'=2] {'z','co'}, dimensions={0} | all-to-all | bytes 524288 | tf_op jit(solution)/shard_map/all_to_all | solution.py:408
  92.2 1.6 %shard_map.83 = (f32[1,64,1024]{2,1,0:T(8,128)}, f32[1,64,1024]{2,1,0:T(8,128)}) custom-call(bf16[16,2,32,128]{3,2,1,0:T(8,128)(2,1)S(1)} %all_to_all.19.recv, s32[17,8]{1,0:T(8,128)S(1)} %get-tuple-element.31.traj), custom_call_target="tpu_custom_call" | custom-call | flops 1000000 | bytes 1000000 | tf_op jit(solution)/shard_map/pallas_call | solution.py:38
  (1 shorter events, 0.0 us)
Async XLA Ops:
  2.8 14.3 %collective-permute-start = (bf16[512,512]{1,0:T(8,128)(2,1)S(1)}, bf16[512,512]{1,0:T(8,128)(2,1)}, u32[]{:S(2)}, u32[]{:S(2)}) collective-permute-start(bf16[512,512]{1,0:T(8,128)(2,1)S(1)} %get-tuple-element.17), channel_id=1, source_target_pairs={{0,1},{1,0},{2,3},{3,2},{4,5},{5,4},{6,7},{7,6},{8,9},{9,8},{10,11... | collective-permute-start | bytes 1572872 | tf_op jit(solution)/shard_map/ppermute | solution.py:329
  17.0 29.1 %collective-permute-start.1 = (bf16[512,512]{1,0:T(8,128)(2,1)}, bf16[512,512]{1,0:T(8,128)(2,1)S(1)}, u32[]{:S(2)}, u32[]{:S(2)}) collective-permute-start(bf16[512,512]{1,0:T(8,128)(2,1)} %collective-permute-done.near), channel_id=1, source_target_pairs={{0,16},{16,0},{1,17},{17,1},{2,18},{18,2},{3,19},{19,3},{4,20},{20... | collective-permute-start | bytes 1572872 | tf_op jit(solution)/shard_map/ppermute | solution.py:377
  19.4 8.5 %collective-permute-start.2 = (bf16[128,640]{1,0:T(8,128)(2,1)S(1)}, bf16[128,640]{1,0:T(8,128)(2,1)S(1)}, u32[]{:S(2)}, u32[]{:S(2)}) collective-permute-start(bf16[128,640]{1,0:T(8,128)(2,1)S(1)} %get-tuple-element.18), channel_id=1, source_target_pairs={{0,2},{1,3},{2,4},{3,5},{4,6},{5,7},{6,8},{7,9},{8,10},{9,11},{10,... | collective-permute-start | bytes 491528 | tf_op jit(solution)/shard_map/ppermute | solution.py:327
  22.1 5.8 %collective-permute-start.4 = (bf16[128,640]{1,0:T(8,128)(2,1)S(1)}, bf16[128,640]{1,0:T(8,128)(2,1)S(1)}, u32[]{:S(2)}, u32[]{:S(2)}) collective-permute-start(bf16[128,640]{1,0:T(8,128)(2,1)S(1)} %get-tuple-element.19), channel_id=1, source_target_pairs={{2,0},{3,1},{4,2},{5,3},{6,4},{7,5},{8,6},{9,7},{10,8},{11,9},{12,... | collective-permute-start | bytes 491528 | tf_op jit(solution)/shard_map/ppermute | solution.py:328
  27.9 9.3 %collective-permute-start.3 = (bf16[128,640]{1,0:T(8,128)(2,1)S(1)}, bf16[128,640]{1,0:T(8,128)(2,1)S(1)}, u32[]{:S(2)}, u32[]{:S(2)}) collective-permute-start(bf16[128,640]{1,0:T(8,128)(2,1)S(1)} %collective-permute-done.2.up0), channel_id=1, source_target_pairs={{0,16},{16,0},{1,17},{17,1},{2,18},{18,2},{3,19},{19,3},{4,20},{20... | collective-permute-start | bytes 491528 | tf_op jit(solution)/shard_map/ppermute | solution.py:353
  27.9 9.3 %collective-permute-start.5 = (bf16[128,640]{1,0:T(8,128)(2,1)S(1)}, bf16[128,640]{1,0:T(8,128)(2,1)S(1)}, u32[]{:S(2)}, u32[]{:S(2)}) collective-permute-start(bf16[128,640]{1,0:T(8,128)(2,1)S(1)} %collective-permute-done.4.down0), channel_id=1, source_target_pairs={{0,16},{16,0},{1,17},{17,1},{2,18},{18,2},{3,19},{19,3},{4,20},{20... | collective-permute-start | bytes 491528 | tf_op jit(solution)/shard_map/ppermute | solution.py:354
  28.4 17.7 %all-to-all-start = ((f32[16,16,128]{2,1,0:T(8,128)}), f32[16,16,128]{2,1,0:T(8,128)S(1)}, u32[]{:S(2)}, u32[]{:S(2)}) async-start(f32[16,16,128]{2,1,0:T(8,128)} %get-tuple-element.24), calls=%async_computation | async-start | bytes 262144 | tf_op jit(solution)/shard_map/all_to_all | solution.py:330
  50.9 23.6 %all-to-all-start.1 = ((bf16[8,32,2048]{2,1,0:T(8,128)(2,1)}), bf16[8,32,2048]{2,1,0:T(8,128)(2,1)S(1)}, u32[]{:S(2)}, u32[]{:S(2)}) async-start(bf16[8,32,2048]{2,1,0:T(8,128)(2,1)} %bitcast.1), calls=%async_computation.1 | async-start | bytes 2097152 | tf_op jit(solution)/shard_map/all_to_all | solution.py:399
  56.5 1.5 %collective-permute-start.6 = (bf16[8,128,128]{2,1,0:T(8,128)(2,1)S(1)}, bf16[8,128,128]{2,1,0:T(8,128)(2,1)S(1)}, u32[]{:S(2)}, u32[]{:S(2)}) collective-permute-start(bf16[8,128,128]{2,1,0:T(8,128)(2,1)S(1)} %get-tuple-element.25.own), channel_id=1, source_target_pairs={{0,16},{16,0},{1,17},{17,1},{2,18},{18,2},{3,19},{19,3},{4,20},{20... | collective-permute-start | bytes 786440 | tf_op jit(solution)/shard_map/ppermute | solution.py:331
  59.8 13.0 %collective-permute-start.7 = (bf16[2,128,128]{2,1,0:T(8,128)(2,1)S(1)}, bf16[2,128,128]{2,1,0:T(8,128)(2,1)S(1)}, u32[]{:S(2)}, u32[]{:S(2)}) collective-permute-start(bf16[2,128,128]{2,1,0:T(8,128)(2,1)S(1)} %get-tuple-element.27), channel_id=1, source_target_pairs={{0,32},{16,240},{32,64},{48,16},{64,96},{80,48},{96,128},{112,80},... | collective-permute-start | bytes 196616 | tf_op jit(solution)/shard_map/ppermute | solution.py:348
  59.9 12.8 %collective-permute-start.8 = (bf16[2,128,128]{2,1,0:T(8,128)(2,1)S(1)}, bf16[2,128,128]{2,1,0:T(8,128)(2,1)S(1)}, u32[]{:S(2)}, u32[]{:S(2)}) collective-permute-start(bf16[2,128,128]{2,1,0:T(8,128)(2,1)S(1)} %get-tuple-element.28), channel_id=1, source_target_pairs={{0,64},{16,208},{32,96},{48,240},{64,128},{80,16},{96,160},{112,48... | collective-permute-start | bytes 196616 | tf_op jit(solution)/shard_map/ppermute | solution.py:348
  61.4 11.4 %collective-permute-start.9 = (bf16[2,128,128]{2,1,0:T(8,128)(2,1)S(1)}, bf16[2,128,128]{2,1,0:T(8,128)(2,1)S(1)}, u32[]{:S(2)}, u32[]{:S(2)}) collective-permute-start(bf16[2,128,128]{2,1,0:T(8,128)(2,1)S(1)} %get-tuple-element.29), channel_id=1, source_target_pairs={{0,96},{16,176},{32,128},{48,208},{64,160},{80,240},{96,192},{112,... | collective-permute-start | bytes 196616 | tf_op jit(solution)/shard_map/ppermute | solution.py:348
  63.8 8.9 %collective-permute-start.10 = (bf16[128,128]{1,0:T(8,128)(2,1)S(1)}, bf16[128,128]{1,0:T(8,128)(2,1)S(1)}, u32[]{:S(2)}, u32[]{:S(2)}) collective-permute-start(bf16[128,128]{1,0:T(8,128)(2,1)S(1)} %get-tuple-element.30), channel_id=1, source_target_pairs={{0,128},{32,160},{64,192},{96,224},{128,0},{160,32},{192,64},{224,... | collective-permute-start | bytes 98312 | tf_op jit(solution)/shard_map/ppermute | solution.py:349
  72.8 1.8 %collective-permute-start.11 = (bf16[7,128,128]{2,1,0:T(8,128)(2,1)S(1)}, bf16[7,128,128]{2,1,0:T(8,128)(2,1)S(1)}, u32[]{:S(2)}, u32[]{:S(2)}) collective-permute-start(bf16[7,128,128]{2,1,0:T(8,128)(2,1)S(1)} %shard_map.81.mine), channel_id=1, source_target_pairs={{0,16},{16,0},{1,17},{17,1},{2,18},{18,2},{3,19},{19,3},{4,20},{20... | collective-permute-start | bytes 688136 | tf_op jit(solution)/shard_map/ppermute | solution.py:351

commit v6 on v5

--- a/solution.py
+++ b/solution.py
@@ -44,10 +44,6 @@
     return pl.ds(pl.multiple_of(i * BLK, BLK), BLK)
 
 
-def rows_at(i, n):
-    return pl.ds(pl.multiple_of(i * n, n), n)
-
-
 def copies_of(pairs, sem):
     out = [pltpu.make_async_copy(a, b, sem.at[i]) for i, (a, b) in enumerate(pairs)]
     for c in out:
@@ -56,12 +52,10 @@
 
 
 def entry_kernel(
-    innov, cell, order, anom, loc, tang, spread, up, down, piece, own, innov_v, cell_v, order_s, edge, ends, tang_v, sem
+    innov, cell, order, anom, loc, tang, spread, up, down, own, innov_v, cell_v, order_s, edge, ends, tang_v, sem
 ):
-    co = lax.axis_index("co")
     cells = anom.shape[0]
     n = loc.shape[0]
-    h = piece.shape[0]
     copies = copies_of(
         (
             (innov, innov_v),
@@ -71,7 +65,6 @@
             (anom.at[pl.ds(0, BLK)], edge.at[1]),
             (loc.at[n - 1, 2], ends.at[0]),
             (loc.at[0, 0], ends.at[1]),
-            (anom.at[rows_at(co, h)], piece),
             (tang, tang_v),
         ),
         sem,
@@ -131,24 +124,22 @@
             out[...] = mine
 
 
-def ready_kernel(anom, loc, up0, up1, down0, down1, lt, gown, asel, ends, anom_v, loc_v, pad, held, sem, out_sem):
+def ready_kernel(anom, loc, lt, gown, asel, anom_v, loc_v, held, sem, out_sem):
     co = lax.axis_index("co")
     copies = copies_of(((loc, loc_v), (anom, anom_v)), sem)
     n = loc.shape[0]
     half = anom.shape[1]
-    pad[:BLK] = jnp.where(co == 0, up0[:, :half], up1[:, :half])
-    pad[BLK + n * BLK :] = jnp.where(co == 0, down0[:, :half], down1[:, :half])
-    ends[0] = jnp.where(co == 0, up1[:, :half], up0[:, :half])
-    ends[1] = jnp.where(co == 0, down1[:, :half], down0[:, :half])
+    none = jnp.zeros((BLK, BLK), bf16)
     copies[0].wait()
     for b in range(n):
-        prev = up0[:, half:] if b == 0 else loc_v[b - 1, 2]
-        nxt = down0[:, half:] if b == n - 1 else loc_v[b + 1, 0]
-        lt[b] = jnp.concatenate([prev.T, loc_v[b, 1].T, nxt.T], axis=1)
+        prev = none if b == 0 else loc_v[b - 1, 2].T
+        nxt = none if b == n - 1 else loc_v[b + 1, 0].T
+        lt[b] = jnp.concatenate([prev, loc_v[b, 1].T, nxt], axis=1)
     copies[1].wait()
-    pad[BLK : BLK + n * BLK] = anom_v[...]
-    for b in range(n):
-        y = jnp.dot(lt[b], pad[b * BLK : (b + 3) * BLK], preferred_element_type=f32)
+    held[:BLK] = jnp.zeros((BLK, half), bf16)
+    held[(n - 1) * BLK :] = jnp.zeros((BLK, half), bf16)
+    for b in range(1, n - 1):
+        y = jnp.dot(lt[b], anom_v[(b - 1) * BLK : (b + 2) * BLK], preferred_element_type=f32)
         held[b * BLK : (b + 1) * BLK] = y.astype(bf16)
     sent = pltpu.make_async_copy(held, gown, out_sem)
     sent.start()
@@ -159,7 +150,29 @@
 
 
 def product_kernel(
-    scale, near, far, ends, lt, gown, asel, recv, out, pad, full, vals, wt, res, ints, order_s, sem, out_sem
+    scale,
+    fetched,
+    handed,
+    anom,
+    gown,
+    up0,
+    up1,
+    down0,
+    down1,
+    lt,
+    asel,
+    recv,
+    out,
+    pad,
+    full,
+    vals,
+    wt,
+    res,
+    ends,
+    ints,
+    order_s,
+    sem,
+    out_sem,
 ):
     co = lax.axis_index("co")
     e = lax.axis_index("ens")
@@ -167,30 +180,53 @@
     steps = recv.shape[0]
     for k in range(steps):
         ints[k : k + 1] = recv[k, 8:9, :].astype(i32)
-    h, half = near.shape
+    cells, half = anom.shape
     n = lt.shape[0]
+    here = pl.ds(pl.multiple_of(e * half, half), half)
     there = pl.ds(pl.multiple_of((1 - e) * half, half), half)
+
+    def other(src):
+        return pltpu.make_async_copy(src, pad.at[pl.ds(BLK, cells)], sem.at[0])
+
+    @pl.when(co == e)
+    def _():
+        other(handed).start()
+
+    @pl.when(co != e)
+    def _():
+        other(fetched).start()
+
     copies = copies_of(
         (
-            (near, pad.at[pl.ds(pl.multiple_of(BLK + co * h, BLK), h)]),
-            (far, pad.at[pl.ds(pl.multiple_of(BLK + (1 - co) * h, BLK), h)]),
+            (anom.at[pl.ds(0, 2 * BLK)], ends.at[0]),
             (ints, order_s),
-            (gown, full.at[:, pl.ds(pl.multiple_of(e * half, half), half)]),
+            (gown, full.at[:, here]),
+            (anom.at[pl.ds(cells - 2 * BLK, 2 * BLK)], ends.at[1]),
         ),
-        sem,
+        sem.at[pl.ds(1, 4)],
     )
     blank = jnp.zeros((BLK - steps, BLK), f32)
     for b in range(n):
         wt[b * BLK : (b + 1) * BLK] = jnp.concatenate([recv[:, b, :], blank], axis=0).T
-    pad[:BLK] = ends[0]
-    pad[BLK + n * BLK :] = ends[1]
+    first = jnp.concatenate([up0[:, half:].T, lt[0, :, BLK:]], axis=1)
+    final = jnp.concatenate([lt[n - 1, :, : 2 * BLK], down0[:, half:].T], axis=1)
+    pad[:BLK] = jnp.where(co == 0, up1[:, :half], up0[:, :half])
+    pad[BLK + cells :] = jnp.where(co == 0, down1[:, :half], down0[:, :half])
+    other(fetched).wait()
+    for b in range(n):
+        left = first if b == 0 else final if b == n - 1 else lt[b]
+        y = jnp.dot(left, pad[b * BLK : (b + 3) * BLK], preferred_element_type=f32)
+        full[b * BLK : (b + 1) * BLK, there] = y.astype(bf16)
     copies[0].wait()
+    copies[3].wait()
+    top = jnp.concatenate([jnp.where(co == 0, up0[:, :half], up1[:, :half]), ends[0]], axis=0)
+    low = jnp.concatenate([ends[1], jnp.where(co == 0, down0[:, :half], down1[:, :half])], axis=0)
+    top = jnp.dot(first, top, preferred_element_type=f32).astype(bf16)
+    low = jnp.dot(final, low, preferred_element_type=f32).astype(bf16)
     copies[1].wait()
-    for b in range(n):
-        y = jnp.dot(lt[b], pad[b * BLK : (b + 3) * BLK], preferred_element_type=f32)
-        full[b * BLK : (b + 1) * BLK, there] = y.astype(bf16)
     copies[2].wait()
-    copies[3].wait()
+    full[:BLK, here] = top
+    full[cells - BLK :, here] = low
     at = [None] * steps
     b = z
     for t in range(steps - 1, -1, -1):
@@ -293,13 +329,12 @@
     n = cells // BLK
     time = ("z", "co")
 
-    spread, tail, head, piece, own_blocks = call(
+    spread, tail, head, own_blocks = call(
         entry_kernel,
         [
             shape((steps, 16, BLK), f32),
             shape((BLK, half + BLK), bf16),
             shape((BLK, half + BLK), bf16),
-            shape((cells // 2, half), bf16),
             shape((NB, BLK, BLK), bf16),
         ],
         [HBM] * 6,
@@ -310,7 +345,7 @@
             pltpu.VMEM((2, BLK, half), bf16),
             pltpu.VMEM((2, BLK, BLK), bf16),
             pltpu.VMEM((NB, BLK, BLK), f32),
-            pltpu.SemaphoreType.DMA((9,)),
+            pltpu.SemaphoreType.DMA((8,)),
         ],
         flops=10**7,
         data=10**6,
@@ -326,7 +361,7 @@
                 downward.append(((c * n_lon + k2) * 2 + e, (c * n_lon + k) * 2 + f))
     up0 = lax.ppermute(tail, ("co", "lon", "ens"), upward)
     down0 = lax.ppermute(head, ("co", "lon", "ens"), downward)
-    near = lax.ppermute(piece, "ens", swap)
+    fetched = lax.ppermute(anomalies, ("co", "ens"), [(0, 1), (3, 2)])
     recv = lax.all_to_all(spread, time, 0, 0, tiled=True)
     oth_blocks = lax.ppermute(own_blocks, "co", swap)
     traj, *sends = call(
@@ -352,49 +387,48 @@
 
     up1 = lax.ppermute(up0, "co", swap)
     down1 = lax.ppermute(down0, "co", swap)
-    lt, gown, asel, ends = call(
+    lt, gown, asel = call(
         ready_kernel,
         [
             shape((n, BLK, 3 * BLK), bf16),
             pltpu.HBM((cells, half), bf16),
             shape((half // 2, cells), bf16),
-            shape((2, BLK, half), bf16),
         ],
-        [HBM, HBM, VM, VM, VM, VM],
+        [HBM, HBM],
         [
             pltpu.VMEM(anomalies.shape, bf16),
             pltpu.VMEM(localization.shape, bf16),
-            pltpu.VMEM((cells + 2 * BLK, half), bf16),
             pltpu.VMEM((cells, half), bf16),
             pltpu.SemaphoreType.DMA((2,)),
             pltpu.SemaphoreType.DMA,
         ],
         flops=10**9,
         data=4 * 10**6,
-        specs=[VM, HBM, VM, VM],
+        specs=[VM, HBM, VM],
         grant=10,
-    )(anomalies, localization, up0, up1, down0, down1)
-    far = lax.ppermute(near, "co", swap)
+    )(anomalies, localization)
+    handed = lax.ppermute(fetched, ("co", "ens"), [(1, 3), (2, 0)])
     (prod,) = call(
         functools.partial(product_kernel, scale),
         [shape((half // 2, steps * BLK), bf16)],
-        [HBM, VM, VM, VM, HBM, VM, VM],
+        [HBM] * 4 + [VM] * 7,
         [
             pltpu.VMEM((cells + 2 * BLK, half), bf16),
             pltpu.VMEM((cells, COLS), bf16),
             pltpu.VMEM((cells, steps * BLK), bf16),
             pltpu.VMEM((cells, BLK), f32),
             pltpu.VMEM((half // 2, steps * BLK), bf16),
+            pltpu.VMEM((2, 2 * BLK, half), bf16),
             pltpu.VMEM((steps, BLK), i32),
             pltpu.SMEM((steps, BLK), i32),
-            pltpu.SemaphoreType.DMA((4,)),
+            pltpu.SemaphoreType.DMA((5,)),
             pltpu.SemaphoreType.DMA((2,)),
         ],
         flops=10**9,
         data=4 * 10**6,
-        grant=14,
+        grant=16,
         specs=[HBM],
-    )(near, far, ends, lt, gown, asel, recv)
+    )(fetched, handed, anomalies, gown, up0, up1, down0, down1, lt, asel, recv)
     rows = half // 2 // n_lon
     parts = lax.all_to_all(prod, "lon", 0, 0, tiled=True).reshape(n_lon, rows, steps * BLK)
     (states,) = call(

time: 94.1 us -> 93.6 us (level)
  starting transfers between devices: 33.4 us -> 30.6 us
  waiting for transfers between devices: 28.6 us -> 30.7 us
    ppermute x2, waiting for transfers between devices: 10.6 us -> 16 us  [the longest x1 16 us: on_device(): fetched = lax.ppermute(anomalies, ('co', 'ens'), [(0, 1), (3, 2)])]
    ppermute x1, waiting for transfers between devices: 3.37 us -> 0.01 us  [on_device(): up0 = lax.ppermute(tail, ('co', 'lon', 'ens'), upward)]
    ppermute x1, starting transfers between devices: 2.7 us -> 0.08 us  [on_device(): up0 = lax.ppermute(tail, ('co', 'lon', 'ens'), upward)]
    ppermute x1, starting transfers between devices: 2.45 us -> 4.77 us  [on_device(): down0 = lax.ppermute(head, ('co', 'lon', 'ens'), downward)]
    all_to_all x1, starting transfers between devices: 5.56 us -> 3.57 us  [on_device(): lax.all_to_all(prod, 'lon', 0, 0, tiled=True)]
  transfers between devices with their start and end apart: 14 -> 14, of which waited for: 6 -> 5; matrix products, arithmetic and copies ran while one was open for 0% -> 0% of each run, Pallas kernels for 5% -> 7%
where the time goes in v6:
time: 93.6 us; the launch traced here: 93.2 us
  waiting for transfers between devices  30.7 us (33%)
  starting transfers between devices  30.6 us (33%)
  Pallas kernels  15.8 us (17%)
  blocking collectives  15.3 us (16%)
    ppermute x1, waiting for transfers between devices, on_device(): fetched = lax.ppermute(anomalies, ('co', 'ens'), [(0, 1), (3, 2)])  16 us
    pallas_call x7, Pallas kernels, run(): return made(*args)  15.8 us
    all_to_all x1, blocking collectives, on_device(): back = lax.all_to_all(states, time, 0, 0, tiled=True)  15.3 us
    all_to_all x1, starting transfers between devices, on_device(): recv = lax.all_to_all(spread, time, 0, 0, tiled=True)  8.59 us
    ppermute x1, waiting for transfers between devices, on_device(): lax.ppermute(sends[nz // 2], 'z', [(k, (k + nz // 2) % nz) for k in range...  6.89 us
    all_to_all x1, waiting for transfers between devices, on_device(): recv = lax.all_to_all(spread, time, 0, 0, tiled=True)  5.24 us
    ppermute x1, starting transfers between devices, on_device(): down0 = lax.ppermute(head, ('co', 'lon', 'ens'), downward)  4.77 us
    ppermute x1, starting transfers between devices, on_device(): handed = lax.ppermute(fetched, ('co', 'ens'), [(1, 3), (2, 0)])  4.67 us
  transfers between devices with their start and end apart: 14, of which 5 were waited for; matrix products, arithmetic and copies ran while one was open for 0% of the time, Pallas kernels for 7%

profile of v6, /device:TPU:1, one launch (start us, length us, event | category | flops | bytes accessed | tf_op | source)
XLA Modules:
  0.0 93.2 jit_solution(13012053486761231676)
XLA Ops:
  0.6 1.3 %collective-permute-start = (bf16[1024,512]{1,0:T(8,128)(2,1)}, bf16[1024,512]{1,0:T(8,128)(2,1)S(1)}, u32[]{:S(2)}, u32[]{:S(2)}) collective-permute-start(bf16[1024,512]{1,0:T(8,128)(2,1)} %anom.5), channel_id=1, source_target_pairs={{0,1},{17,16},{2,3},{19,18},{4,5},{21,20},{6,7},{23,22},{8,9},{25,... | collective-permute-start | bytes 3145736 | tf_op jit(solution)/shard_map/ppermute | solution.py:364
  1.9 16.0 %collective-permute-done.fetched = bf16[1024,512]{1,0:T(8,128)(2,1)S(1)} collective-permute-done((bf16[1024,512]{1,0:T(8,128)(2,1)}, bf16[1024,512]{1,0:T(8,128)(2,1)S(1)}, u32[]{:S(2)}, u32[]{:S(2)}) %collective-permute-start) | collective-permute-done | bytes 1048608 | tf_op jit(solution)/shard_map/ppermute | solution.py:364
  17.9 0.0 copy-start
  17.9 4.7 %collective-permute-start.1 = (bf16[1024,512]{1,0:T(8,128)(2,1)S(1)}, bf16[1024,512]{1,0:T(8,128)(2,1)}, u32[]{:S(2)}, u32[]{:S(2)}) collective-permute-start(bf16[1024,512]{1,0:T(8,128)(2,1)S(1)} %collective-permute-done.fetched), channel_id=1, source_target_pairs={{1,17},{16,0},{3,19},{18,2},{5,21},{20,4},{7,23},{22,6},{9,25},{24... | collective-permute-start | bytes 3145736 | tf_op jit(solution)/shard_map/ppermute | solution.py:410
  22.6 2.0 %shard_map.78 = (f32[16,16,128]{2,1,0:T(8,128)}, bf16[128,640]{1,0:T(8,128)(2,1)S(1)}, bf16[128,640]{1,0:T(8,128)(2,1)S(1)}, bf16[8,128,128]{2,1,0:T(8,128)(2,1)S(1)}) custom-call(f32[1,512]{1,0:T(1,128)} %innov.1, s32[1,512]{1,0:T(1,128)} %cell.1, s32[1,8]{1,0:T(1,128)} %order.1, bf16[1024,512]{1,0:T(8,128)(2,1)} %anom.5, bf16[8,3,128,128]{3,2,1,0:T(8,128)(2,1)} %loc.3, ...), custom_call_target="tpu_custom_call" | custom-call | flops 10000000 | bytes 1000000 | tf_op jit(solution)/shard_map/pallas_call | solution.py:38
  24.6 0.0 copy-done
  24.6 0.1 collective-permute-start.2
  24.7 4.8 %collective-permute-start.4 = (bf16[128,640]{1,0:T(8,128)(2,1)S(1)}, bf16[128,640]{1,0:T(8,128)(2,1)S(1)}, u32[]{:S(2)}, u32[]{:S(2)}) collective-permute-start(bf16[128,640]{1,0:T(8,128)(2,1)S(1)} %get-tuple-element.17), channel_id=1, source_target_pairs={{2,0},{3,1},{4,2},{5,3},{6,4},{7,5},{8,6},{9,7},{10,8},{11,9},{12,... | collective-permute-start | bytes 491528 | tf_op jit(solution)/shard_map/ppermute | solution.py:363
  29.4 8.6 %all-to-all-start = ((f32[16,16,128]{2,1,0:T(8,128)}), f32[16,16,128]{2,1,0:T(8,128)S(1)}, u32[]{:S(2)}, u32[]{:S(2)}) async-start(f32[16,16,128]{2,1,0:T(8,128)} %get-tuple-element.20), calls=%async_computation | async-start | bytes 262144 | tf_op jit(solution)/shard_map/all_to_all | solution.py:365
  38.0 0.0 collective-permute-done.2.up0
  38.0 0.2 collective-permute-start.3
  38.2 0.0 collective-permute-done.4.down0
  38.2 0.4 collective-permute-start.5
  38.6 3.0 %shard_map.77 = (bf16[8,128,384]{2,1,0:T(8,128)(2,1)S(1)}, bf16[1024,512]{1,0:T(8,128)(2,1)}, bf16[256,1024]{1,0:T(8,128)(2,1)S(1)}) custom-call(bf16[1024,512]{1,0:T(8,128)(2,1)} %anom.5, bf16[8,3,128,128]{3,2,1,0:T(8,128)(2,1)} %loc.3), custom_call_target="tpu_custom_call" | custom-call | flops 1000000000 | bytes 4000000 | tf_op jit(solution)/shard_map/pallas_call | solution.py:38
  41.7 5.2 %all-to-all-done.recv = f32[16,16,128]{2,1,0:T(8,128)S(1)} async-done(((f32[16,16,128]{2,1,0:T(8,128)}), f32[16,16,128]{2,1,0:T(8,128)S(1)}, u32[]{:S(2)}, u32[]{:S(2)}) %all-to-all-start) | async-done | bytes 131104 | tf_op jit(solution)/shard_map/all_to_all | solution.py:365
  46.9 0.0 collective-permute-done.3.up1
  46.9 0.0 collective-permute-done.5.down1
  46.9 0.0 collective-permute-done.1.handed
  46.9 5.4 %shard_map.79 = bf16[256,2048]{1,0:T(8,128)(2,1)} custom-call(bf16[1024,512]{1,0:T(8,128)(2,1)} %copy-done, bf16[1024,512]{1,0:T(8,128)(2,1)} %collective-permute-done.1.handed, bf16[1024,512]{1,0:T(8,128)(2,1)} %anom.5, bf16[1024,512]{1,0:T(8,128)(2,1)} %get-tuple-element.15.gown, bf16[128,640]{1,0:T(8,128)(2,1)S(1)} %collective-permute-done.2.up0, ...), custom_call_target="tpu_custom_call" | custom-call | flops 1000000000 | bytes 4000000 | tf_op jit(solution)/shard_map/pallas_call | solution.py:38
  52.3 3.6 %all-to-all-start.1 = ((bf16[8,32,2048]{2,1,0:T(8,128)(2,1)}), bf16[8,32,2048]{2,1,0:T(8,128)(2,1)S(1)}, u32[]{:S(2)}, u32[]{:S(2)}) async-start(bf16[8,32,2048]{2,1,0:T(8,128)(2,1)} %bitcast.1), calls=%async_computation.1 | async-start | bytes 2097152 | tf_op jit(solution)/shard_map/all_to_all | solution.py:433
  55.9 0.1 collective-permute-start.6
  56.0 1.5 %collective-permute-done.6.oth = bf16[8,128,128]{2,1,0:T(8,128)(2,1)S(1)} collective-permute-done((bf16[8,128,128]{2,1,0:T(8,128)(2,1)S(1)}, bf16[8,128,128]{2,1,0:T(8,128)(2,1)S(1)}, u32[]{:S(2)}, u32[]{:S(2)}) %collective-permute-start.6) | collective-permute-done | bytes 262176 | tf_op jit(solution)/shard_map/ppermute | solution.py:366
  57.5 1.7 %shard_map.80 = (s32[17,8]{1,0:T(8,128)S(1)}, bf16[2,128,128]{2,1,0:T(8,128)(2,1)S(1)}, bf16[2,128,128]{2,1,0:T(8,128)(2,1)S(1)}, bf16[2,128,128]{2,1,0:T(8,128)...) custom-call(bf16[8,128,128]{2,1,0:T(8,128)(2,1)S(1)} %get-tuple-element.21.own, ...), custom_call_target="tpu_custom_call" | custom-call | flops 1000000 | bytes 1000000 | tf_op jit(solution)/shard_map/pallas_call | solution.py:38
  59.3 0.2 collective-permute-start.7
  59.4 1.1 %collective-permute-start.8 = (bf16[2,128,128]{2,1,0:T(8,128)(2,1)S(1)}, bf16[2,128,128]{2,1,0:T(8,128)(2,1)S(1)}, u32[]{:S(2)}, u32[]{:S(2)}) collective-permute-start(bf16[2,128,128]{2,1,0:T(8,128)(2,1)S(1)} %get-tuple-element.24), channel_id=1, source_target_pairs={{0,64},{16,208},{32,96},{48,240},{64,128},{80,16},{96,160},{112,48... | collective-permute-start | bytes 196616 | tf_op jit(solution)/shard_map/ppermute | solution.py:383
  60.6 2.8 %collective-permute-start.9 = (bf16[2,128,128]{2,1,0:T(8,128)(2,1)S(1)}, bf16[2,128,128]{2,1,0:T(8,128)(2,1)S(1)}, u32[]{:S(2)}, u32[]{:S(2)}) collective-permute-start(bf16[2,128,128]{2,1,0:T(8,128)(2,1)S(1)} %get-tuple-element.25), channel_id=1, source_target_pairs={{0,96},{16,176},{32,128},{48,208},{64,160},{80,240},{96,192},{112,... | collective-permute-start | bytes 196616 | tf_op jit(solution)/shard_map/ppermute | solution.py:383
  63.3 2.2 %collective-permute-start.10 = (bf16[128,128]{1,0:T(8,128)(2,1)S(1)}, bf16[128,128]{1,0:T(8,128)(2,1)S(1)}, u32[]{:S(2)}, u32[]{:S(2)}) collective-permute-start(bf16[128,128]{1,0:T(8,128)(2,1)S(1)} %get-tuple-element.26), channel_id=1, source_target_pairs={{0,128},{32,160},{64,192},{96,224},{128,0},{160,32},{192,64},{224,... | collective-permute-start | bytes 98312 | tf_op jit(solution)/shard_map/ppermute | solution.py:384
  65.6 6.9 %collective-permute-done.10.refs_3_ = bf16[128,128]{1,0:T(8,128)(2,1)S(1)} collective-permute-done((bf16[128,128]{1,0:T(8,128)(2,1)S(1)}, bf16[128,128]{1,0:T(8,128)(2,1)S(1)}, u32[]{:S(2)}, u32[]{:S(2)}) %collective-permute-start.10) | collective-permute-done | bytes 32800 | tf_op jit(solution)/shard_map/ppermute | solution.py:384
  72.5 0.0 collective-permute-done.7.refs_0_
  72.5 0.0 collective-permute-done.8.refs_1_
  72.5 0.0 collective-permute-done.9.refs_2_
  72.5 0.6 collective-permute-start.11
  73.1 1.1 %collective-permute-done.11.theirs = bf16[7,128,128]{2,1,0:T(8,128)(2,1)S(1)} collective-permute-done((bf16[7,128,128]{2,1,0:T(8,128)(2,1)S(1)}, bf16[7,128,128]{2,1,0:T(8,128)(2,1)S(1)}, u32[]{:S(2)}, u32[]{:S(2)}) %collective-permute-start.11) | collective-permute-done | bytes 229408 | tf_op jit(solution)/shard_map/ppermute | solution.py:386
  74.2 0.0 all-to-all-done.1.parts
  74.2 2.0 %shard_map.82 = bf16[16,2,32,128]{3,2,1,0:T(8,128)(2,1)S(1)} custom-call(bf16[8,32,2048]{2,1,0:T(8,128)(2,1)S(1)} %all-to-all-done.1.parts, bf16[2,128,128]{2,1,0:T(8,128)(2,1)S(1)} %get-tuple-element.22.own, bf16[7,128,128]{2,1,0:T(8,128)(2,1)S(1)} %shard_map.81.mine, bf16[7,128,128]{2,1,0:T(8,128)(2,1)S(1)} %collective-permute-done.11.theirs), custom_call_target="tpu_custom_call" | custom-call | flops 1000000000 | bytes 2000000 | tf_op jit(solution)/shard_map/pallas_call | solution.py:38
  76.3 15.3 %all_to_all.19.recv = bf16[16,2,32,128]{3,2,1,0:T(8,128)(2,1)S(1)} all-to-all(bf16[16,2,32,128]{3,2,1,0:T(8,128)(2,1)S(1)} %shard_map.82), channel_id=1, replica_groups=mesh['z'=8,'co'=2,'lon'=8,'ens'=2] {'z','co'}, dimensions={0} | all-to-all | bytes 524288 | tf_op jit(solution)/shard_map/all_to_all | solution.py:442
  91.6 1.6 %shard_map.83 = (f32[1,64,1024]{2,1,0:T(8,128)}, f32[1,64,1024]{2,1,0:T(8,128)}) custom-call(bf16[16,2,32,128]{3,2,1,0:T(8,128)(2,1)S(1)} %all_to_all.19.recv, s32[17,8]{1,0:T(8,128)S(1)} %get-tuple-element.27.traj), custom_call_target="tpu_custom_call" | custom-call | flops 1000000 | bytes 1000000 | tf_op jit(solution)/shard_map/pallas_call | solution.py:38
  (1 shorter events, 0.0 us)
Async XLA Ops:
  0.6 17.3 %collective-permute-start = (bf16[1024,512]{1,0:T(8,128)(2,1)}, bf16[1024,512]{1,0:T(8,128)(2,1)S(1)}, u32[]{:S(2)}, u32[]{:S(2)}) collective-permute-start(bf16[1024,512]{1,0:T(8,128)(2,1)} %anom.5), channel_id=1, source_target_pairs={{0,1},{17,16},{2,3},{19,18},{4,5},{21,20},{6,7},{23,22},{8,9},{25,... | collective-permute-start | bytes 3145736 | tf_op jit(solution)/shard_map/ppermute | solution.py:364
  17.9 6.7 %copy-start = (bf16[1024,512]{1,0:T(8,128)(2,1)}, bf16[1024,512]{1,0:T(8,128)(2,1)S(1)}, u32[]{:S(2)}) copy-start(bf16[1024,512]{1,0:T(8,128)(2,1)S(1)} %collective-permute-done.fetched) | copy-start | bytes 3145732
  17.9 29.0 %collective-permute-start.1 = (bf16[1024,512]{1,0:T(8,128)(2,1)S(1)}, bf16[1024,512]{1,0:T(8,128)(2,1)}, u32[]{:S(2)}, u32[]{:S(2)}) collective-permute-start(bf16[1024,512]{1,0:T(8,128)(2,1)S(1)} %collective-permute-done.fetched), channel_id=1, source_target_pairs={{1,17},{16,0},{3,19},{18,2},{5,21},{20,4},{7,23},{22,6},{9,25},{24... | collective-permute-start | bytes 3145736 | tf_op jit(solution)/shard_map/ppermute | solution.py:410
  24.6 13.5 %collective-permute-start.2 = (bf16[128,640]{1,0:T(8,128)(2,1)S(1)}, bf16[128,640]{1,0:T(8,128)(2,1)S(1)}, u32[]{:S(2)}, u32[]{:S(2)}) collective-permute-start(bf16[128,640]{1,0:T(8,128)(2,1)S(1)} %get-tuple-element.16), channel_id=1, source_target_pairs={{0,2},{1,3},{2,4},{3,5},{4,6},{5,7},{6,8},{7,9},{8,10},{9,11},{10,... | collective-permute-start | bytes 491528 | tf_op jit(solution)/shard_map/ppermute | solution.py:362
  24.7 13.6 %collective-permute-start.4 = (bf16[128,640]{1,0:T(8,128)(2,1)S(1)}, bf16[128,640]{1,0:T(8,128)(2,1)S(1)}, u32[]{:S(2)}, u32[]{:S(2)}) collective-permute-start(bf16[128,640]{1,0:T(8,128)(2,1)S(1)} %get-tuple-element.17), channel_id=1, source_target_pairs={{2,0},{3,1},{4,2},{5,3},{6,4},{7,5},{8,6},{9,7},{10,8},{11,9},{12,... | collective-permute-start | bytes 491528 | tf_op jit(solution)/shard_map/ppermute | solution.py:363
  29.4 17.5 %all-to-all-start = ((f32[16,16,128]{2,1,0:T(8,128)}), f32[16,16,128]{2,1,0:T(8,128)S(1)}, u32[]{:S(2)}, u32[]{:S(2)}) async-start(f32[16,16,128]{2,1,0:T(8,128)} %get-tuple-element.20), calls=%async_computation | async-start | bytes 262144 | tf_op jit(solution)/shard_map/all_to_all | solution.py:365
  38.0 8.9 %collective-permute-start.3 = (bf16[128,640]{1,0:T(8,128)(2,1)S(1)}, bf16[128,640]{1,0:T(8,128)(2,1)S(1)}, u32[]{:S(2)}, u32[]{:S(2)}) collective-permute-start(bf16[128,640]{1,0:T(8,128)(2,1)S(1)} %collective-permute-done.2.up0), channel_id=1, source_target_pairs={{0,16},{16,0},{1,17},{17,1},{2,18},{18,2},{3,19},{19,3},{4,20},{20... | collective-permute-start | bytes 491528 | tf_op jit(solution)/shard_map/ppermute | solution.py:388
  38.2 8.7 %collective-permute-start.5 = (bf16[128,640]{1,0:T(8,128)(2,1)S(1)}, bf16[128,640]{1,0:T(8,128)(2,1)S(1)}, u32[]{:S(2)}, u32[]{:S(2)}) collective-permute-start(bf16[128,640]{1,0:T(8,128)(2,1)S(1)} %collective-permute-done.4.down0), channel_id=1, source_target_pairs={{0,16},{16,0},{1,17},{17,1},{2,18},{18,2},{3,19},{19,3},{4,20},{20... | collective-permute-start | bytes 491528 | tf_op jit(solution)/shard_map/ppermute | solution.py:389
  52.3 21.9 %all-to-all-start.1 = ((bf16[8,32,2048]{2,1,0:T(8,128)(2,1)}), bf16[8,32,2048]{2,1,0:T(8,128)(2,1)S(1)}, u32[]{:S(2)}, u32[]{:S(2)}) async-start(bf16[8,32,2048]{2,1,0:T(8,128)(2,1)} %bitcast.1), calls=%async_computation.1 | async-start | bytes 2097152 | tf_op jit(solution)/shard_map/all_to_all | solution.py:433
  55.9 1.6 %collective-permute-start.6 = (bf16[8,128,128]{2,1,0:T(8,128)(2,1)S(1)}, bf16[8,128,128]{2,1,0:T(8,128)(2,1)S(1)}, u32[]{:S(2)}, u32[]{:S(2)}) collective-permute-start(bf16[8,128,128]{2,1,0:T(8,128)(2,1)S(1)} %get-tuple-element.21.own), channel_id=1, source_target_pairs={{0,16},{16,0},{1,17},{17,1},{2,18},{18,2},{3,19},{19,3},{4,20},{20... | collective-permute-start | bytes 786440 | tf_op jit(solution)/shard_map/ppermute | solution.py:366
  59.3 13.2 %collective-permute-start.7 = (bf16[2,128,128]{2,1,0:T(8,128)(2,1)S(1)}, bf16[2,128,128]{2,1,0:T(8,128)(2,1)S(1)}, u32[]{:S(2)}, u32[]{:S(2)}) collective-permute-start(bf16[2,128,128]{2,1,0:T(8,128)(2,1)S(1)} %get-tuple-element.23), channel_id=1, source_target_pairs={{0,32},{16,240},{32,64},{48,16},{64,96},{80,48},{96,128},{112,80},... | collective-permute-start | bytes 196616 | tf_op jit(solution)/shard_map/ppermute | solution.py:383
  59.4 13.0 %collective-permute-start.8 = (bf16[2,128,128]{2,1,0:T(8,128)(2,1)S(1)}, bf16[2,128,128]{2,1,0:T(8,128)(2,1)S(1)}, u32[]{:S(2)}, u32[]{:S(2)}) collective-permute-start(bf16[2,128,128]{2,1,0:T(8,128)(2,1)S(1)} %get-tuple-element.24), channel_id=1, source_target_pairs={{0,64},{16,208},{32,96},{48,240},{64,128},{80,16},{96,160},{112,48... | collective-permute-start | bytes 196616 | tf_op jit(solution)/shard_map/ppermute | solution.py:383
  60.6 11.9 %collective-permute-start.9 = (bf16[2,128,128]{2,1,0:T(8,128)(2,1)S(1)}, bf16[2,128,128]{2,1,0:T(8,128)(2,1)S(1)}, u32[]{:S(2)}, u32[]{:S(2)}) collective-permute-start(bf16[2,128,128]{2,1,0:T(8,128)(2,1)S(1)} %get-tuple-element.25), channel_id=1, source_target_pairs={{0,96},{16,176},{32,128},{48,208},{64,160},{80,240},{96,192},{112,... | collective-permute-start | bytes 196616 | tf_op jit(solution)/shard_map/ppermute | solution.py:383
  63.3 9.1 %collective-permute-start.10 = (bf16[128,128]{1,0:T(8,128)(2,1)S(1)}, bf16[128,128]{1,0:T(8,128)(2,1)S(1)}, u32[]{:S(2)}, u32[]{:S(2)}) collective-permute-start(bf16[128,128]{1,0:T(8,128)(2,1)S(1)} %get-tuple-element.26), channel_id=1, source_target_pairs={{0,128},{32,160},{64,192},{96,224},{128,0},{160,32},{192,64},{224,... | collective-permute-start | bytes 98312 | tf_op jit(solution)/shard_map/ppermute | solution.py:384
  72.5 1.7 %collective-permute-start.11 = (bf16[7,128,128]{2,1,0:T(8,128)(2,1)S(1)}, bf16[7,128,128]{2,1,0:T(8,128)(2,1)S(1)}, u32[]{:S(2)}, u32[]{:S(2)}) collective-permute-start(bf16[7,128,128]{2,1,0:T(8,128)(2,1)S(1)} %shard_map.81.mine), channel_id=1, source_target_pairs={{0,16},{16,0},{1,17},{17,1},{2,18},{18,2},{3,19},{19,3},{4,20},{20... | collective-permute-start | bytes 688136 | tf_op jit(solution)/shard_map/ppermute | solution.py:386

commit v7 on v6

--- a/solution.py
+++ b/solution.py
@@ -44,6 +44,10 @@
     return pl.ds(pl.multiple_of(i * BLK, BLK), BLK)
 
 
+def rows_at(i, n):
+    return pl.ds(pl.multiple_of(i * n, n), n)
+
+
 def copies_of(pairs, sem):
     out = [pltpu.make_async_copy(a, b, sem.at[i]) for i, (a, b) in enumerate(pairs)]
     for c in out:
@@ -52,10 +56,12 @@
 
 
 def entry_kernel(
-    innov, cell, order, anom, loc, tang, spread, up, down, own, innov_v, cell_v, order_s, edge, ends, tang_v, sem
+    innov, cell, order, anom, loc, tang, spread, up, down, piece, own, innov_v, cell_v, order_s, edge, ends, tang_v, sem
 ):
+    co = lax.axis_index("co")
     cells = anom.shape[0]
     n = loc.shape[0]
+    h = piece.shape[0]
     copies = copies_of(
         (
             (innov, innov_v),
@@ -65,6 +71,7 @@
             (anom.at[pl.ds(0, BLK)], edge.at[1]),
             (loc.at[n - 1, 2], ends.at[0]),
             (loc.at[0, 0], ends.at[1]),
+            (anom.at[rows_at(co, h)], piece),
             (tang, tang_v),
         ),
         sem,
@@ -151,8 +158,8 @@
 
 def product_kernel(
     scale,
-    fetched,
-    handed,
+    near,
+    far,
     anom,
     gown,
     up0,
@@ -185,25 +192,17 @@
     here = pl.ds(pl.multiple_of(e * half, half), half)
     there = pl.ds(pl.multiple_of((1 - e) * half, half), half)
 
-    def other(src):
-        return pltpu.make_async_copy(src, pad.at[pl.ds(BLK, cells)], sem.at[0])
-
-    @pl.when(co == e)
-    def _():
-        other(handed).start()
-
-    @pl.when(co != e)
-    def _():
-        other(fetched).start()
-
+    h = near.shape[0]
     copies = copies_of(
         (
+            (near, pad.at[pl.ds(pl.multiple_of(BLK + co * h, BLK), h)]),
+            (far, pad.at[pl.ds(pl.multiple_of(BLK + (1 - co) * h, BLK), h)]),
             (anom.at[pl.ds(0, 2 * BLK)], ends.at[0]),
+            (anom.at[pl.ds(cells - 2 * BLK, 2 * BLK)], ends.at[1]),
             (ints, order_s),
             (gown, full.at[:, here]),
-            (anom.at[pl.ds(cells - 2 * BLK, 2 * BLK)], ends.at[1]),
         ),
-        sem.at[pl.ds(1, 4)],
+        sem,
     )
     blank = jnp.zeros((BLK - steps, BLK), f32)
     for b in range(n):
@@ -212,19 +211,20 @@
     final = jnp.concatenate([lt[n - 1, :, : 2 * BLK], down0[:, half:].T], axis=1)
     pad[:BLK] = jnp.where(co == 0, up1[:, :half], up0[:, :half])
     pad[BLK + cells :] = jnp.where(co == 0, down1[:, :half], down0[:, :half])
-    other(fetched).wait()
+    copies[0].wait()
+    copies[1].wait()
     for b in range(n):
         left = first if b == 0 else final if b == n - 1 else lt[b]
         y = jnp.dot(left, pad[b * BLK : (b + 3) * BLK], preferred_element_type=f32)
         full[b * BLK : (b + 1) * BLK, there] = y.astype(bf16)
-    copies[0].wait()
+    copies[2].wait()
     copies[3].wait()
     top = jnp.concatenate([jnp.where(co == 0, up0[:, :half], up1[:, :half]), ends[0]], axis=0)
     low = jnp.concatenate([ends[1], jnp.where(co == 0, down0[:, :half], down1[:, :half])], axis=0)
     top = jnp.dot(first, top, preferred_element_type=f32).astype(bf16)
     low = jnp.dot(final, low, preferred_element_type=f32).astype(bf16)
-    copies[1].wait()
-    copies[2].wait()
+    copies[4].wait()
+    copies[5].wait()
     full[:BLK, here] = top
     full[cells - BLK :, here] = low
     at = [None] * steps
@@ -329,12 +329,13 @@
     n = cells // BLK
     time = ("z", "co")
 
-    spread, tail, head, own_blocks = call(
+    spread, tail, head, piece, own_blocks = call(
         entry_kernel,
         [
             shape((steps, 16, BLK), f32),
             shape((BLK, half + BLK), bf16),
             shape((BLK, half + BLK), bf16),
+            shape((cells // 2, half), bf16),
             shape((NB, BLK, BLK), bf16),
         ],
         [HBM] * 6,
@@ -345,7 +346,7 @@
             pltpu.VMEM((2, BLK, half), bf16),
             pltpu.VMEM((2, BLK, BLK), bf16),
             pltpu.VMEM((NB, BLK, BLK), f32),
-            pltpu.SemaphoreType.DMA((8,)),
+            pltpu.SemaphoreType.DMA((9,)),
         ],
         flops=10**7,
         data=10**6,
@@ -361,7 +362,7 @@
                 downward.append(((c * n_lon + k2) * 2 + e, (c * n_lon + k) * 2 + f))
     up0 = lax.ppermute(tail, ("co", "lon", "ens"), upward)
     down0 = lax.ppermute(head, ("co", "lon", "ens"), downward)
-    fetched = lax.ppermute(anomalies, ("co", "ens"), [(0, 1), (3, 2)])
+    near = lax.ppermute(piece, "ens", swap)
     recv = lax.all_to_all(spread, time, 0, 0, tiled=True)
     oth_blocks = lax.ppermute(own_blocks, "co", swap)
     traj, *sends = call(
@@ -407,11 +408,11 @@
         specs=[VM, HBM, VM],
         grant=10,
     )(anomalies, localization)
-    handed = lax.ppermute(fetched, ("co", "ens"), [(1, 3), (2, 0)])
+    far = lax.ppermute(near, "co", swap)
     (prod,) = call(
         functools.partial(product_kernel, scale),
         [shape((half // 2, steps * BLK), bf16)],
-        [HBM] * 4 + [VM] * 7,
+        [HBM, VM, HBM, HBM] + [VM] * 7,
         [
             pltpu.VMEM((cells + 2 * BLK, half), bf16),
             pltpu.VMEM((cells, COLS), bf16),
@@ -421,14 +422,14 @@
             pltpu.VMEM((2, 2 * BLK, half), bf16),
             pltpu.VMEM((steps, BLK), i32),
             pltpu.SMEM((steps, BLK), i32),
-            pltpu.SemaphoreType.DMA((5,)),
+            pltpu.SemaphoreType.DMA((6,)),
             pltpu.SemaphoreType.DMA((2,)),
         ],
         flops=10**9,
         data=4 * 10**6,
         grant=16,
         specs=[HBM],
-    )(fetched, handed, anomalies, gown, up0, up1, down0, down1, lt, asel, recv)
+    )(near, far, anomalies, gown, up0, up1, down0, down1, lt, asel, recv)
     rows = half // 2 // n_lon
     parts = lax.all_to_all(prod, "lon", 0, 0, tiled=True).reshape(n_lon, rows, steps * BLK)
     (states,) = call(

time: 93.6 us -> 88.3 us (0.943)
  waiting for transfers between devices: 30.7 us -> 25.4 us
    ppermute x2, waiting for transfers between devices: 16 us -> 10.6 us  [the longest x1 10.6 us: on_device(): near = lax.ppermute(piece, 'ens', swap)]
    ppermute x1, starting transfers between devices: 0.08 us -> 2.7 us  [on_device(): up0 = lax.ppermute(tail, ('co', 'lon', 'ens'), upward)]
    ppermute x1, starting transfers between devices: 4.77 us -> 2.45 us  [on_device(): down0 = lax.ppermute(head, ('co', 'lon', 'ens'), downward)]
  transfers between devices with their start and end apart: 14 -> 14, of which waited for: 5 -> 5; matrix products, arithmetic and copies ran while one was open for 0% -> 0% of each run, Pallas kernels for 7% -> 5%
where the time goes in v7:
time: 88.3 us; the launch traced here: 88 us
  starting transfers between devices  30.8 us (35%)
  waiting for transfers between devices  25.4 us (29%)
  Pallas kernels  15.7 us (18%)
  blocking collectives  15.3 us (17%)
    pallas_call x7, Pallas kernels, run(): return made(*args)  15.7 us
    all_to_all x1, blocking collectives, on_device(): back = lax.all_to_all(states, time, 0, 0, tiled=True)  15.3 us
    ppermute x1, waiting for transfers between devices, on_device(): near = lax.ppermute(piece, 'ens', swap)  10.6 us
    all_to_all x1, starting transfers between devices, on_device(): recv = lax.all_to_all(spread, time, 0, 0, tiled=True)  8.59 us
    ppermute x1, waiting for transfers between devices, on_device(): lax.ppermute(sends[nz // 2], 'z', [(k, (k + nz // 2) % nz) for k in range...  6.92 us
    all_to_all x1, waiting for transfers between devices, on_device(): recv = lax.all_to_all(spread, time, 0, 0, tiled=True)  5.22 us
    ppermute x3, starting transfers between devices, on_device(): got.append(lax.ppermute(sends[d], time, pairs))  4.1 us
    ppermute x1, starting transfers between devices, on_device(): near = lax.ppermute(piece, 'ens', swap)  3.65 us
  transfers between devices with their start and end apart: 14, of which 5 were waited for; matrix products, arithmetic and copies ran while one was open for 0% of the time, Pallas kernels for 5%

profile of v7, /device:TPU:1, one launch (start us, length us, event | category | flops | bytes accessed | tf_op | source)
XLA Modules:
  0.0 88.0 jit_solution(14119771900421879632)
XLA Ops:
  0.6 2.1 %shard_map.77 = (f32[16,16,128]{2,1,0:T(8,128)}, bf16[128,640]{1,0:T(8,128)(2,1)S(1)}, bf16[128,640]{1,0:T(8,128)(2,1)S(1)}, bf16[512,512]{1,0:T(8,128)(2,1)S(1)}, bf16[8,128,128]{2,1,0:T(8,128)(2,1)S(1)}) custom-call(f32[1,512]{1,0:T(1,128)} %innov.1, s32[1,512]{1,0:T(1,128)} %cell.1, s32[1,8]{1,0:T(1,128)} %order.1, bf16[1024,512]{1,0:T(8,128)(2,1)} %anom.5, ...), custom_call_target="tpu_custom_call" | custom-call | flops 10000000 | bytes 1000000 | tf_op jit(solution)/shard_map/pallas_call | solution.py:38
  2.8 3.6 %collective-permute-start = (bf16[512,512]{1,0:T(8,128)(2,1)S(1)}, bf16[512,512]{1,0:T(8,128)(2,1)S(1)}, u32[]{:S(2)}, u32[]{:S(2)}) collective-permute-start(bf16[512,512]{1,0:T(8,128)(2,1)S(1)} %get-tuple-element.16), channel_id=1, source_target_pairs={{0,1},{1,0},{2,3},{3,2},{4,5},{5,4},{6,7},{7,6},{8,9},{9,8},{10,11... | collective-permute-start | bytes 1572872 | tf_op jit(solution)/shard_map/ppermute | solution.py:365
  6.4 10.6 %collective-permute-done.near = bf16[512,512]{1,0:T(8,128)(2,1)S(1)} collective-permute-done((bf16[512,512]{1,0:T(8,128)(2,1)S(1)}, bf16[512,512]{1,0:T(8,128)(2,1)S(1)}, u32[]{:S(2)}, u32[]{:S(2)}) %collective-permute-start) | collective-permute-done | bytes 524320 | tf_op jit(solution)/shard_map/ppermute | solution.py:365
  17.0 0.0 copy-start
  17.0 2.3 %collective-permute-start.1 = (bf16[512,512]{1,0:T(8,128)(2,1)S(1)}, bf16[512,512]{1,0:T(8,128)(2,1)S(1)}, u32[]{:S(2)}, u32[]{:S(2)}) collective-permute-start(bf16[512,512]{1,0:T(8,128)(2,1)S(1)} %collective-permute-done.near), channel_id=1, source_target_pairs={{0,16},{16,0},{1,17},{17,1},{2,18},{18,2},{3,19},{19,3},{4,20},{20... | collective-permute-start | bytes 1572872 | tf_op jit(solution)/shard_map/ppermute | solution.py:411
  19.3 2.7 %collective-permute-start.2 = (bf16[128,640]{1,0:T(8,128)(2,1)S(1)}, bf16[128,640]{1,0:T(8,128)(2,1)S(1)}, u32[]{:S(2)}, u32[]{:S(2)}) collective-permute-start(bf16[128,640]{1,0:T(8,128)(2,1)S(1)} %get-tuple-element.18), channel_id=1, source_target_pairs={{0,2},{1,3},{2,4},{3,5},{4,6},{5,7},{6,8},{7,9},{8,10},{9,11},{10,... | collective-permute-start | bytes 491528 | tf_op jit(solution)/shard_map/ppermute | solution.py:363
  22.0 2.5 %collective-permute-start.4 = (bf16[128,640]{1,0:T(8,128)(2,1)S(1)}, bf16[128,640]{1,0:T(8,128)(2,1)S(1)}, u32[]{:S(2)}, u32[]{:S(2)}) collective-permute-start(bf16[128,640]{1,0:T(8,128)(2,1)S(1)} %get-tuple-element.19), channel_id=1, source_target_pairs={{2,0},{3,1},{4,2},{5,3},{6,4},{7,5},{8,6},{9,7},{10,8},{11,9},{12,... | collective-permute-start | bytes 491528 | tf_op jit(solution)/shard_map/ppermute | solution.py:364
  24.5 8.6 %all-to-all-start = ((f32[16,16,128]{2,1,0:T(8,128)}), f32[16,16,128]{2,1,0:T(8,128)S(1)}, u32[]{:S(2)}, u32[]{:S(2)}) async-start(f32[16,16,128]{2,1,0:T(8,128)} %get-tuple-element.22), calls=%async_computation | async-start | bytes 262144 | tf_op jit(solution)/shard_map/all_to_all | solution.py:366
  33.0 0.0 collective-permute-done.2.up0
  33.1 0.2 collective-permute-start.3
  33.2 0.0 collective-permute-done.4.down0
  33.2 0.4 collective-permute-start.5
  33.7 3.0 %shard_map.78 = (bf16[8,128,384]{2,1,0:T(8,128)(2,1)S(1)}, bf16[1024,512]{1,0:T(8,128)(2,1)}, bf16[256,1024]{1,0:T(8,128)(2,1)S(1)}) custom-call(bf16[1024,512]{1,0:T(8,128)(2,1)} %anom.5, bf16[8,3,128,128]{3,2,1,0:T(8,128)(2,1)} %loc.3), custom_call_target="tpu_custom_call" | custom-call | flops 1000000000 | bytes 4000000 | tf_op jit(solution)/shard_map/pallas_call | solution.py:38
  36.7 0.0 copy-done
  36.7 5.2 %all-to-all-done.recv = f32[16,16,128]{2,1,0:T(8,128)S(1)} async-done(((f32[16,16,128]{2,1,0:T(8,128)}), f32[16,16,128]{2,1,0:T(8,128)S(1)}, u32[]{:S(2)}, u32[]{:S(2)}) %all-to-all-start) | async-done | bytes 131104 | tf_op jit(solution)/shard_map/all_to_all | solution.py:366
  41.9 0.0 collective-permute-done.3.up1
  41.9 0.0 collective-permute-done.5.down1
  41.9 0.0 collective-permute-done.1.far
  41.9 5.1 %shard_map.79 = bf16[256,2048]{1,0:T(8,128)(2,1)} custom-call(bf16[512,512]{1,0:T(8,128)(2,1)} %copy-done, bf16[512,512]{1,0:T(8,128)(2,1)S(1)} %collective-permute-done.1.far, bf16[1024,512]{1,0:T(8,128)(2,1)} %anom.5, bf16[1024,512]{1,0:T(8,128)(2,1)} %get-tuple-element.17.gown, bf16[128,640]{1,0:T(8,128)(2,1)S(1)} %collective-permute-done.2.up0, ...), custom_call_target="tpu_custom_call" | custom-call | flops 1000000000 | bytes 4000000 | tf_op jit(solution)/shard_map/pallas_call | solution.py:38
  47.1 3.6 %all-to-all-start.1 = ((bf16[8,32,2048]{2,1,0:T(8,128)(2,1)}), bf16[8,32,2048]{2,1,0:T(8,128)(2,1)S(1)}, u32[]{:S(2)}, u32[]{:S(2)}) async-start(bf16[8,32,2048]{2,1,0:T(8,128)(2,1)} %bitcast.1), calls=%async_computation.1 | async-start | bytes 2097152 | tf_op jit(solution)/shard_map/all_to_all | solution.py:434
  50.7 0.1 collective-permute-start.6
  50.8 1.5 %collective-permute-done.6.oth = bf16[8,128,128]{2,1,0:T(8,128)(2,1)S(1)} collective-permute-done((bf16[8,128,128]{2,1,0:T(8,128)(2,1)S(1)}, bf16[8,128,128]{2,1,0:T(8,128)(2,1)S(1)}, u32[]{:S(2)}, u32[]{:S(2)}) %collective-permute-start.6) | collective-permute-done | bytes 262176 | tf_op jit(solution)/shard_map/ppermute | solution.py:367
  52.3 1.7 %shard_map.80 = (s32[17,8]{1,0:T(8,128)S(1)}, bf16[2,128,128]{2,1,0:T(8,128)(2,1)S(1)}, bf16[2,128,128]{2,1,0:T(8,128)(2,1)S(1)}, bf16[2,128,128]{2,1,0:T(8,128)...) custom-call(bf16[8,128,128]{2,1,0:T(8,128)(2,1)S(1)} %get-tuple-element.23.own, ...), custom_call_target="tpu_custom_call" | custom-call | flops 1000000 | bytes 1000000 | tf_op jit(solution)/shard_map/pallas_call | solution.py:38
  54.0 0.2 collective-permute-start.7
  54.2 1.2 %collective-permute-start.8 = (bf16[2,128,128]{2,1,0:T(8,128)(2,1)S(1)}, bf16[2,128,128]{2,1,0:T(8,128)(2,1)S(1)}, u32[]{:S(2)}, u32[]{:S(2)}) collective-permute-start(bf16[2,128,128]{2,1,0:T(8,128)(2,1)S(1)} %get-tuple-element.26), channel_id=1, source_target_pairs={{0,64},{16,208},{32,96},{48,240},{64,128},{80,16},{96,160},{112,48... | collective-permute-start | bytes 196616 | tf_op jit(solution)/shard_map/ppermute | solution.py:384
  55.3 2.8 %collective-permute-start.9 = (bf16[2,128,128]{2,1,0:T(8,128)(2,1)S(1)}, bf16[2,128,128]{2,1,0:T(8,128)(2,1)S(1)}, u32[]{:S(2)}, u32[]{:S(2)}) collective-permute-start(bf16[2,128,128]{2,1,0:T(8,128)(2,1)S(1)} %get-tuple-element.27), channel_id=1, source_target_pairs={{0,96},{16,176},{32,128},{48,208},{64,160},{80,240},{96,192},{112,... | collective-permute-start | bytes 196616 | tf_op jit(solution)/shard_map/ppermute | solution.py:384
  58.1 2.2 %collective-permute-start.10 = (bf16[128,128]{1,0:T(8,128)(2,1)S(1)}, bf16[128,128]{1,0:T(8,128)(2,1)S(1)}, u32[]{:S(2)}, u32[]{:S(2)}) collective-permute-start(bf16[128,128]{1,0:T(8,128)(2,1)S(1)} %get-tuple-element.28), channel_id=1, source_target_pairs={{0,128},{32,160},{64,192},{96,224},{128,0},{160,32},{192,64},{224,... | collective-permute-start | bytes 98312 | tf_op jit(solution)/shard_map/ppermute | solution.py:385
  60.3 6.9 %collective-permute-done.10.refs_3_ = bf16[128,128]{1,0:T(8,128)(2,1)S(1)} collective-permute-done((bf16[128,128]{1,0:T(8,128)(2,1)S(1)}, bf16[128,128]{1,0:T(8,128)(2,1)S(1)}, u32[]{:S(2)}, u32[]{:S(2)}) %collective-permute-start.10) | collective-permute-done | bytes 32800 | tf_op jit(solution)/shard_map/ppermute | solution.py:385
  67.3 0.0 collective-permute-done.7.refs_0_
  67.3 0.0 collective-permute-done.8.refs_1_
  67.3 0.0 collective-permute-done.9.refs_2_
  67.3 0.6 collective-permute-start.11
  67.9 1.1 %collective-permute-done.11.theirs = bf16[7,128,128]{2,1,0:T(8,128)(2,1)S(1)} collective-permute-done((bf16[7,128,128]{2,1,0:T(8,128)(2,1)S(1)}, bf16[7,128,128]{2,1,0:T(8,128)(2,1)S(1)}, u32[]{:S(2)}, u32[]{:S(2)}) %collective-permute-start.11) | collective-permute-done | bytes 229408 | tf_op jit(solution)/shard_map/ppermute | solution.py:387
  69.0 0.0 all-to-all-done.1.parts
  69.0 2.0 %shard_map.82 = bf16[16,2,32,128]{3,2,1,0:T(8,128)(2,1)S(1)} custom-call(bf16[8,32,2048]{2,1,0:T(8,128)(2,1)S(1)} %all-to-all-done.1.parts, bf16[2,128,128]{2,1,0:T(8,128)(2,1)S(1)} %get-tuple-element.24.own, bf16[7,128,128]{2,1,0:T(8,128)(2,1)S(1)} %shard_map.81.mine, bf16[7,128,128]{2,1,0:T(8,128)(2,1)S(1)} %collective-permute-done.11.theirs), custom_call_target="tpu_custom_call" | custom-call | flops 1000000000 | bytes 2000000 | tf_op jit(solution)/shard_map/pallas_call | solution.py:38
  71.1 15.3 %all_to_all.19.recv = bf16[16,2,32,128]{3,2,1,0:T(8,128)(2,1)S(1)} all-to-all(bf16[16,2,32,128]{3,2,1,0:T(8,128)(2,1)S(1)} %shard_map.82), channel_id=1, replica_groups=mesh['z'=8,'co'=2,'lon'=8,'ens'=2] {'z','co'}, dimensions={0} | all-to-all | bytes 524288 | tf_op jit(solution)/shard_map/all_to_all | solution.py:443
  86.4 1.6 %shard_map.83 = (f32[1,64,1024]{2,1,0:T(8,128)}, f32[1,64,1024]{2,1,0:T(8,128)}) custom-call(bf16[16,2,32,128]{3,2,1,0:T(8,128)(2,1)S(1)} %all_to_all.19.recv, s32[17,8]{1,0:T(8,128)S(1)} %get-tuple-element.29.traj), custom_call_target="tpu_custom_call" | custom-call | flops 1000000 | bytes 1000000 | tf_op jit(solution)/shard_map/pallas_call | solution.py:38
  (1 shorter events, 0.0 us)
Async XLA Ops:
  2.8 14.3 %collective-permute-start = (bf16[512,512]{1,0:T(8,128)(2,1)S(1)}, bf16[512,512]{1,0:T(8,128)(2,1)S(1)}, u32[]{:S(2)}, u32[]{:S(2)}) collective-permute-start(bf16[512,512]{1,0:T(8,128)(2,1)S(1)} %get-tuple-element.16), channel_id=1, source_target_pairs={{0,1},{1,0},{2,3},{3,2},{4,5},{5,4},{6,7},{7,6},{8,9},{9,8},{10,11... | collective-permute-start | bytes 1572872 | tf_op jit(solution)/shard_map/ppermute | solution.py:365
  17.0 19.7 %copy-start = (bf16[512,512]{1,0:T(8,128)(2,1)}, bf16[512,512]{1,0:T(8,128)(2,1)S(1)}, u32[]{:S(2)}) copy-start(bf16[512,512]{1,0:T(8,128)(2,1)S(1)} %collective-permute-done.near) | copy-start | bytes 1572868
  17.0 24.9 %collective-permute-start.1 = (bf16[512,512]{1,0:T(8,128)(2,1)S(1)}, bf16[512,512]{1,0:T(8,128)(2,1)S(1)}, u32[]{:S(2)}, u32[]{:S(2)}) collective-permute-start(bf16[512,512]{1,0:T(8,128)(2,1)S(1)} %collective-permute-done.near), channel_id=1, source_target_pairs={{0,16},{16,0},{1,17},{17,1},{2,18},{18,2},{3,19},{19,3},{4,20},{20... | collective-permute-start | bytes 1572872 | tf_op jit(solution)/shard_map/ppermute | solution.py:411
  19.3 13.7 %collective-permute-start.2 = (bf16[128,640]{1,0:T(8,128)(2,1)S(1)}, bf16[128,640]{1,0:T(8,128)(2,1)S(1)}, u32[]{:S(2)}, u32[]{:S(2)}) collective-permute-start(bf16[128,640]{1,0:T(8,128)(2,1)S(1)} %get-tuple-element.18), channel_id=1, source_target_pairs={{0,2},{1,3},{2,4},{3,5},{4,6},{5,7},{6,8},{7,9},{8,10},{9,11},{10,... | collective-permute-start | bytes 491528 | tf_op jit(solution)/shard_map/ppermute | solution.py:363
  22.0 11.2 %collective-permute-start.4 = (bf16[128,640]{1,0:T(8,128)(2,1)S(1)}, bf16[128,640]{1,0:T(8,128)(2,1)S(1)}, u32[]{:S(2)}, u32[]{:S(2)}) collective-permute-start(bf16[128,640]{1,0:T(8,128)(2,1)S(1)} %get-tuple-element.19), channel_id=1, source_target_pairs={{2,0},{3,1},{4,2},{5,3},{6,4},{7,5},{8,6},{9,7},{10,8},{11,9},{12,... | collective-permute-start | bytes 491528 | tf_op jit(solution)/shard_map/ppermute | solution.py:364
  24.5 17.5 %all-to-all-start = ((f32[16,16,128]{2,1,0:T(8,128)}), f32[16,16,128]{2,1,0:T(8,128)S(1)}, u32[]{:S(2)}, u32[]{:S(2)}) async-start(f32[16,16,128]{2,1,0:T(8,128)} %get-tuple-element.22), calls=%async_computation | async-start | bytes 262144 | tf_op jit(solution)/shard_map/all_to_all | solution.py:366
  33.1 8.9 %collective-permute-start.3 = (bf16[128,640]{1,0:T(8,128)(2,1)S(1)}, bf16[128,640]{1,0:T(8,128)(2,1)S(1)}, u32[]{:S(2)}, u32[]{:S(2)}) collective-permute-start(bf16[128,640]{1,0:T(8,128)(2,1)S(1)} %collective-permute-done.2.up0), channel_id=1, source_target_pairs={{0,16},{16,0},{1,17},{17,1},{2,18},{18,2},{3,19},{19,3},{4,20},{20... | collective-permute-start | bytes 491528 | tf_op jit(solution)/shard_map/ppermute | solution.py:389
  33.2 8.7 %collective-permute-start.5 = (bf16[128,640]{1,0:T(8,128)(2,1)S(1)}, bf16[128,640]{1,0:T(8,128)(2,1)S(1)}, u32[]{:S(2)}, u32[]{:S(2)}) collective-permute-start(bf16[128,640]{1,0:T(8,128)(2,1)S(1)} %collective-permute-done.4.down0), channel_id=1, source_target_pairs={{0,16},{16,0},{1,17},{17,1},{2,18},{18,2},{3,19},{19,3},{4,20},{20... | collective-permute-start | bytes 491528 | tf_op jit(solution)/shard_map/ppermute | solution.py:390
  47.1 21.9 %all-to-all-start.1 = ((bf16[8,32,2048]{2,1,0:T(8,128)(2,1)}), bf16[8,32,2048]{2,1,0:T(8,128)(2,1)S(1)}, u32[]{:S(2)}, u32[]{:S(2)}) async-start(bf16[8,32,2048]{2,1,0:T(8,128)(2,1)} %bitcast.1), calls=%async_computation.1 | async-start | bytes 2097152 | tf_op jit(solution)/shard_map/all_to_all | solution.py:434
  50.7 1.6 %collective-permute-start.6 = (bf16[8,128,128]{2,1,0:T(8,128)(2,1)S(1)}, bf16[8,128,128]{2,1,0:T(8,128)(2,1)S(1)}, u32[]{:S(2)}, u32[]{:S(2)}) collective-permute-start(bf16[8,128,128]{2,1,0:T(8,128)(2,1)S(1)} %get-tuple-element.23.own), channel_id=1, source_target_pairs={{0,16},{16,0},{1,17},{17,1},{2,18},{18,2},{3,19},{19,3},{4,20},{20... | collective-permute-start | bytes 786440 | tf_op jit(solution)/shard_map/ppermute | solution.py:367
  54.0 13.2 %collective-permute-start.7 = (bf16[2,128,128]{2,1,0:T(8,128)(2,1)S(1)}, bf16[2,128,128]{2,1,0:T(8,128)(2,1)S(1)}, u32[]{:S(2)}, u32[]{:S(2)}) collective-permute-start(bf16[2,128,128]{2,1,0:T(8,128)(2,1)S(1)} %get-tuple-element.25), channel_id=1, source_target_pairs={{0,32},{16,240},{32,64},{48,16},{64,96},{80,48},{96,128},{112,80},... | collective-permute-start | bytes 196616 | tf_op jit(solution)/shard_map/ppermute | solution.py:384
  54.2 13.1 %collective-permute-start.8 = (bf16[2,128,128]{2,1,0:T(8,128)(2,1)S(1)}, bf16[2,128,128]{2,1,0:T(8,128)(2,1)S(1)}, u32[]{:S(2)}, u32[]{:S(2)}) collective-permute-start(bf16[2,128,128]{2,1,0:T(8,128)(2,1)S(1)} %get-tuple-element.26), channel_id=1, source_target_pairs={{0,64},{16,208},{32,96},{48,240},{64,128},{80,16},{96,160},{112,48... | collective-permute-start | bytes 196616 | tf_op jit(solution)/shard_map/ppermute | solution.py:384
  55.3 11.9 %collective-permute-start.9 = (bf16[2,128,128]{2,1,0:T(8,128)(2,1)S(1)}, bf16[2,128,128]{2,1,0:T(8,128)(2,1)S(1)}, u32[]{:S(2)}, u32[]{:S(2)}) collective-permute-start(bf16[2,128,128]{2,1,0:T(8,128)(2,1)S(1)} %get-tuple-element.27), channel_id=1, source_target_pairs={{0,96},{16,176},{32,128},{48,208},{64,160},{80,240},{96,192},{112,... | collective-permute-start | bytes 196616 | tf_op jit(solution)/shard_map/ppermute | solution.py:384
  58.1 9.1 %collective-permute-start.10 = (bf16[128,128]{1,0:T(8,128)(2,1)S(1)}, bf16[128,128]{1,0:T(8,128)(2,1)S(1)}, u32[]{:S(2)}, u32[]{:S(2)}) collective-permute-start(bf16[128,128]{1,0:T(8,128)(2,1)S(1)} %get-tuple-element.28), channel_id=1, source_target_pairs={{0,128},{32,160},{64,192},{96,224},{128,0},{160,32},{192,64},{224,... | collective-permute-start | bytes 98312 | tf_op jit(solution)/shard_map/ppermute | solution.py:385
  67.3 1.7 %collective-permute-start.11 = (bf16[7,128,128]{2,1,0:T(8,128)(2,1)S(1)}, bf16[7,128,128]{2,1,0:T(8,128)(2,1)S(1)}, u32[]{:S(2)}, u32[]{:S(2)}) collective-permute-start(bf16[7,128,128]{2,1,0:T(8,128)(2,1)S(1)} %shard_map.81.mine), channel_id=1, source_target_pairs={{0,16},{16,0},{1,17},{17,1},{2,18},{18,2},{3,19},{19,3},{4,20},{20... | collective-permute-start | bytes 688136 | tf_op jit(solution)/shard_map/ppermute | solution.py:387
